TPU v7x, 256 devices: a whole 4x4x8 slice. The times are simulated.
256 devices in a mesh: dp: 16 (over z, y_hi), seq: 16 (over x, y_lo, core).
Axes of the slice: x: 4, y: 4 (y_hi: 2, y_lo: 2; y = y_hi * 2 + y_lo), z: 8, core: 2. Of those that a mesh axis runs over, the one named last changes fastest.
Arguments:
- queries: bfloat16 [16, 3072, 512], P('dp', 'seq'), may hold values from -7 to 7
- key_rows: bfloat16 [16, 3072, 512], P('dp', 'seq'), may hold values from -7 to 7
- values: bfloat16 [16, 3072, 1536], P('dp', 'seq'), may hold values from -6 to 6
- out_proj: bfloat16 [1536, 768], replicated, may hold values from -0.15625 to 0.15625
- stream: bfloat16 [16, 3072, 768], P('dp', 'seq'), may hold values from -6 to 6
- cotangent: bfloat16 [16, 3072, 768], P('dp', 'seq'), may hold values from -6 to 6
- conv_weight: bfloat16 [3, 768, 768], replicated, may hold values from -0.125 to 0.125
Outputs:
- query_grad: bfloat16 [16, 3072, 512], P('dp', 'seq')
- key_grad: bfloat16 [16, 3072, 512], P('dp', 'seq')
- value_grad: bfloat16 [16, 3072, 1536], P('dp', 'seq')
- stream_grad: bfloat16 [16, 3072, 768], P('dp', 'seq')
- weight_grad: float32 [3, 768, 768], P(None, 'seq', 'dp')
All inputs are finite; a program needn't handle non-finite values.
Results may differ from a plain program's by a relative error of at most 0.033.
Values may be sent and summed in bfloat16 or wider, within the bound.
No kernel may reach another device: no remote copies, remote signals or barrier semaphores. Data moves between devices by JAX's collectives and lax.ppermute only.
A program may use at most 256 MiB of HBM per device.

v0:
```python
import math

import jax
import jax.numpy as jnp
from jax import lax
from jax.sharding import PartitionSpec as P

HEADS = 8
KEY = 64
VAL = 192


def passed_along(value, axis, by):
    count = lax.axis_size(axis)
    pairs = [(i, i + by) for i in range(count) if 0 <= i + by < count]
    return lax.ppermute(value, axis, pairs)


def gelu_pieces(inputs):
    wide = inputs.astype(jnp.float32)
    normal_cdf = 0.5 * (1.0 + jax.scipy.special.erf(wide * (1.0 / math.sqrt(2.0))))
    density = jnp.exp(-0.5 * wide * wide) * (1.0 / math.sqrt(2.0 * math.pi))
    return (wide * normal_cdf, normal_cdf + wide * density)


def contract_rows(left, right):
    return lax.dot_general(
        left, right, (((1,), (1,)), ((), ())), preferred_element_type=jnp.float32
    )


def contract_bins(left, right):
    return lax.dot_general(
        left, right, (((0,), (0,)), ((), ())), preferred_element_type=jnp.float32
    )


def shift_taps(grads, offset):
    return passed_along(grads, "seq", offset)


def column_pair(source, pair, width, rows):
    return lax.dynamic_slice_in_dim(source, pair * 2 * width, 2 * width, 1).reshape(rows, 2, width)


def shards(queries, key_rows, values, out_proj, stream, cotangent, conv_weight):
    local_queries = queries[0]
    local_grads = cotangent[0]
    rows = local_queries.shape[0]
    score_scale = 1.0 / math.sqrt(KEY)
    all_keys, all_values = (
        lax.all_gather(key_rows[0], "seq", axis=0, tiled=True),
        lax.all_gather(values[0], "seq", axis=0, tiled=True),
    )
    seq_len = all_keys.shape[0]
    pairs = HEADS // 2
    pair_index = jnp.arange(pairs, dtype=jnp.int32)

    def forward_pair(pair):
        query_pair = column_pair(local_queries, pair, KEY, rows)
        key_pair = column_pair(all_keys, pair, KEY, seq_len)
        value_pair = column_pair(all_values, pair, VAL, seq_len)
        scores = (
            jnp.einsum("bhd,lhd->hbl", query_pair, key_pair, preferred_element_type=jnp.float32)
            * score_scale
        )
        exponent = jnp.exp(scores - jnp.max(scores, axis=2, keepdims=True))
        prob_pair = exponent / jnp.sum(exponent, axis=2, keepdims=True)
        half_pair = prob_pair.astype(jnp.bfloat16)
        attended_pair = jnp.einsum(
            "hbl,lhe->bhe", half_pair, value_pair, preferred_element_type=jnp.float32
        ).astype(jnp.bfloat16)
        return (prob_pair, half_pair, attended_pair)

    prob_full, prob_pairs, attended_pairs = lax.map(forward_pair, pair_index)
    attended = jnp.transpose(attended_pairs, (1, 0, 2, 3)).reshape(rows, HEADS * VAL)
    projected = jnp.dot(attended, out_proj, preferred_element_type=jnp.float32)
    stream_in = (stream[0].astype(jnp.float32) + projected).astype(jnp.bfloat16)
    activated, gelu_slope = gelu_pieces(stream_in)
    activated = activated.astype(jnp.bfloat16)
    distance = max(1, lax.axis_size("seq") // 4)
    gradient_forward_shift = shift_taps(local_grads, -distance)
    gradient_backward_shift = shift_taps(local_grads, distance)
    branch = (
        contract_rows(gradient_forward_shift, conv_weight[0])
        + contract_rows(local_grads, conv_weight[1])
        + contract_rows(gradient_backward_shift, conv_weight[2])
    )
    stream_grad = (local_grads.astype(jnp.float32) + gelu_slope * branch).astype(jnp.bfloat16)
    out_grad = contract_rows(stream_grad, out_proj).astype(jnp.bfloat16)

    def backward_pair(pieces):
        pair, prob_pair, half_pair = pieces
        out_pair = column_pair(out_grad, pair, VAL, rows)
        attended_pair = column_pair(attended, pair, VAL, rows)
        key_pair = column_pair(all_keys, pair, KEY, seq_len)
        value_pair = column_pair(all_values, pair, VAL, seq_len)
        row_delta = jnp.sum(
            out_pair.astype(jnp.float32) * attended_pair.astype(jnp.float32), axis=2
        )
        prob_grad = jnp.einsum(
            "bhe,lhe->hbl", out_pair, value_pair, preferred_element_type=jnp.float32
        )
        score_pair = (prob_pair * (prob_grad - row_delta.T[:, :, None])).astype(jnp.bfloat16)
        query_pair = (
            jnp.einsum("hbl,lhd->bhd", score_pair, key_pair, preferred_element_type=jnp.float32)
            * score_scale
        ).astype(jnp.bfloat16)
        return (score_pair, query_pair)

    score_pairs, query_pairs = lax.map(backward_pair, (pair_index, prob_full, prob_pairs))
    score_half = score_pairs.reshape(HEADS, rows, seq_len)
    prob_half = prob_pairs.reshape(HEADS, rows, seq_len)
    query_grad = jnp.transpose(query_pairs, (1, 0, 2, 3)).reshape(rows, HEADS * KEY)
    query_heads = local_queries.reshape(rows, HEADS, KEY)
    out_heads = out_grad.reshape(rows, HEADS, VAL)
    key_part = (
        jnp.einsum("hbl,bhd->lhd", score_half, query_heads, preferred_element_type=jnp.float32)
        * score_scale
    )
    value_part = jnp.einsum(
        "hbl,bhe->lhe", prob_half, out_heads, preferred_element_type=jnp.float32
    )
    summed = lax.psum_scatter(
        jnp.concatenate(
            [
                key_part.reshape(rows * lax.axis_size("seq"), HEADS * KEY),
                value_part.reshape(rows * lax.axis_size("seq"), HEADS * VAL),
            ],
            axis=1,
        ).astype(jnp.bfloat16),
        "seq",
        scatter_dimension=0,
        tiled=True,
    ).astype(jnp.float32)
    key_grad = summed[:, : HEADS * KEY].astype(jnp.bfloat16)
    value_grad = summed[:, HEADS * KEY :].astype(jnp.bfloat16)
    weight_term = jnp.stack(
        [
            contract_bins(activated, gradient_forward_shift),
            contract_bins(activated, local_grads),
            contract_bins(activated, gradient_backward_shift),
        ]
    )
    partial_sum = lax.psum_scatter(
        weight_term.astype(jnp.bfloat16), "dp", scatter_dimension=2, tiled=True
    )
    weight_grad = lax.psum_scatter(partial_sum, "seq", scatter_dimension=1, tiled=True).astype(
        jnp.float32
    )
    weight_grad = weight_grad * (1.0 / lax.axis_size("dp"))
    return (query_grad[None], key_grad[None], value_grad[None], stream_grad[None], weight_grad)


def solution(mesh):
    return jax.shard_map(
        shards,
        mesh=mesh,
        in_specs=(
            P("dp", "seq", None),
            P("dp", "seq", None),
            P("dp", "seq", None),
            P(),
            P("dp", "seq", None),
            P("dp", "seq", None),
            P(),
        ),
        out_specs=(
            P("dp", "seq", None),
            P("dp", "seq", None),
            P("dp", "seq", None),
            P("dp", "seq", None),
            P(None, "seq", "dp"),
        ),
        check_vma=False,
    )
```

profile of v0, /device:TPU:1, one launch (start us, length us, event | category | flops | bytes accessed | tf_op | source)
XLA Modules:
  0.0 690.9 jit_solution(16924919098687064529)
XLA Ops:
  8.7 4.0 collective-permute-start.1
  17.0 2.8 fusion.24
  19.8 2.7 fusion.22
  22.5 29.8 %all-gather.5.cloned.1.call-done = bf16[1,3072,512]{2,1,0:T(8,128)(2,1)} async-done(((bf16[1,192,512]{2,1,0:T(8,128)(2,1)}), bf16[1,3072,512]{2,1,0:T(8,128)(2,1)}) %all-gather.5.cloned.1.call-update) | async-done | bytes 3145744 | tf_op jit(solution)/shard_map/all_gather | solution.py:52
  52.3 4.7 copy.49
  57.0 57.1 %all-gather.7.cloned.1.call-done = bf16[1,3072,1536]{2,1,0:T(8,128)(2,1)} async-done(((bf16[1,192,1536]{2,1,0:T(8,128)(2,1)}), bf16[1,3072,1536]{2,1,0:T(8,128)(2,1)}) %all-gather.7.cloned.1.call-update) | async-done | bytes 9437200 | tf_op jit(solution)/shard_map/all_gather | solution.py:53
  114.1 12.7 %copy.50 = bf16[3072,1536]{0,1:T(8,128)(2,1)} copy(bf16[3072,1536]{1,0:T(8,128)(2,1)} %bitcast.162) | data formatting | bytes 18874368 | tf_op jit(solution)/shard_map/while | solution.py:75
  126.8 4.9 broadcast.22.clone
  131.7 74.7 %while.30 = (s32[]{:T(128)}, f32[4,2,192,3072]{3,2,1,0:T(8,128)}, bf16[4,2,192,3072]{3,2,1,0:T(8,128)(2,1)}, bf16[4,192,2,192]{1,3,2,0:T(8,128)(2,1)}, s32[4]{0:...) while((s32[]{:T(128)}, f32[4,2,192,3072]{3,2,1,0:T(8,128)}, ...), condition=%wide.region_3.4_spmd, body=%wide.region_0.3_spmd.sunk | while | flops 611134464 | bytes 59332932 | solution.py:75
  134.2 3.6 fusion.74
  137.8 5.5 bitcast_dynamic-update-slice_fusion.7
  144.0 2.0 constant_dynamic-slice_fusion.14
  147.8 2.6 bitcast_dynamic-update-slice_fusion.6
  152.8 3.6 fusion.74
  156.5 5.4 bitcast_dynamic-update-slice_fusion.7
  162.5 2.0 constant_dynamic-slice_fusion.14
  166.3 2.6 bitcast_dynamic-update-slice_fusion.6
  171.4 3.6 fusion.74
  175.1 5.4 bitcast_dynamic-update-slice_fusion.7
  181.2 2.0 constant_dynamic-slice_fusion.14
  185.0 2.7 bitcast_dynamic-update-slice_fusion.6
  190.1 3.6 fusion.74
  193.8 5.5 bitcast_dynamic-update-slice_fusion.7
  199.9 2.0 constant_dynamic-slice_fusion.14
  203.8 2.6 bitcast_dynamic-update-slice_fusion.6
  206.4 2.3 copy.61
  208.6 1.9 multiply_convert_fusion.1
  210.6 2.4 fusion.19
  216.5 2.0 pad_maximum_fusion.1
  218.5 8.2 %copy.58 = bf16[3,768,768]{1,0,2:T(4,128)(2,1)} copy(bf16[3,768,768]{2,1,0:T(8,128)(2,1)} %pad_maximum_fusion.1) | data formatting | bytes 7077888 | tf_op jit(solution)/shard_map/stack | solution.py:138
  226.9 4.8 broadcast.22
  231.7 51.3 %while.31 = (s32[]{:T(128)}, bf16[4,2,192,3072]{3,2,1,0:T(8,128)(2,1)}, bf16[4,192,2,64]{1,3,2,0:T(8,128)(2,1)}, f32[4,2,192,3072]{3,2,1,0:T(8,128)}, s32[4]{0:T...) while((s32[]{:T(128)}, ...), condition=%wide.region_6.7_spmd, body=%wide.region_4.6_spmd.sunk | while | flops 607862400 | bytes 23518464 | solution.py:111
  236.6 4.6 bitcast_dynamic-update-slice_fusion.8
  247.5 1.9 constant_dynamic-slice_fusion.15
  249.4 4.6 bitcast_dynamic-update-slice_fusion.8
  262.2 4.6 bitcast_dynamic-update-slice_fusion.8
  275.0 4.6 bitcast_dynamic-update-slice_fusion.8
  283.3 7.3 %multiply_convert_fusion = bf16[8,3072,64]{1,2,0:T(8,128)(2,1)} fusion(bf16[192,8,64]{0,2,1:T(8,128)(2,1)S(1)} %bitcast.165, bf16[8,192,3072]{2,1,0:T(8,128)(2,1)} %bitcast.157), kind=kOutput, calls=%fused_computation.31 | convolution fusion | flops 607125504 | bytes 12779520 | tf_op jit(solution)/shard_map/hbl,bhd->lhd/dot_general | solution.py:118
  290.6 4.7 copy.56
  295.4 10.0 %convolution_convert_fusion.1 = bf16[8,192,3072]{2,1,0:T(8,128)(2,1)} fusion(bf16[192,8,192]{0,2,1:T(8,128)(2,1)S(1)} %bitcast.163, bf16[8,192,3072]{2,1,0:T(8,128)(2,1)} %bitcast.154), kind=kOutput, calls=%fused_computation.30 | convolution fusion | flops 1816657920 | bytes 19464192 | tf_op jit(solution)/shard_map/hbl,bhe->lhe/dot_general | solution.py:121
  305.4 12.6 %copy.57 = bf16[3072,1536]{1,0:T(8,128)(2,1)} copy(bf16[3072,1536]{0,1:T(8,128)(2,1)} %bitcast.155) | data formatting | bytes 18874368 | tf_op jit(solution)/shard_map/reshape | solution.py:128
  318.0 133.8 %all-reduce.3.cloned.1.call-done = bf16[3,768,768]{1,0,2:T(4,128)(2,1)} async-done(((bf16[3,768,768]{1,0,2:T(4,128)(2,1)}), bf16[3,768,768]{1,0,2:T(4,128)(2,1)}) %all-reduce.3.cloned.1.call-update) | async-done | bytes 3538960
  452.8 10.1 %copy.63 = bf16[3,768,48]{0,2,1:T(8,128)(2,1)} copy(bf16[3,768,48]{1,0,2:T(4,128)(2,1)S(1)} %constant_dynamic-slice_fusion.6) | data formatting | bytes 442368
  462.9 11.1 %reshape.95 = bf16[768,144]{1,0:T(8,128)(2,1)} reshape(bf16[768,48,3]{2,1,0:T(8,128)(2,1)} %bitcast.158) | data formatting | bytes 442368
  474.1 10.5 %pad_maximum_fusion = bf16[3072,2048]{1,0:T(8,128)(2,1)} fusion(bf16[3072,1536]{1,0:T(8,128)(2,1)} %copy.57, bf16[3072,512]{1,0:T(8,128)(2,1)} %copy.56), kind=kLoop, calls=%fused_computation.29 | loop fusion | flops 25165824 | bytes 25165824 | tf_op jit(solution)/shard_map/concatenate | solution.py:125
  486.4 49.0 %reduce-scatter.7.cloned.1.call-done = bf16[48,144]{1,0:T(8,128)(2,1)} async-done(((bf16[768,144]{1,0:T(8,128)(2,1)}), bf16[48,144]{1,0:T(8,128)(2,1)}) %reduce-scatter.7.cloned.1.call-update) | async-done | bytes 13840
  538.1 142.8 %reduce-scatter.5.cloned.1.call-done = bf16[192,2048]{1,0:T(8,128)(2,1)} async-done(((bf16[3072,2048]{1,0:T(8,128)(2,1)}), bf16[192,2048]{1,0:T(8,128)(2,1)}) %reduce-scatter.5.cloned.1.call-update) | async-done | bytes 786448 | tf_op jit(solution)/shard_map/reduce_scatter | solution.py:124
  680.8 1.9 slice_bitcast_fusion
  (127 shorter events, 56.5 us)
Async XLA Ops:
  7.2 201.5 %copy-start = (bf16[1536,768]{1,0:T(8,128)(2,1)S(1)}, bf16[1536,768]{1,0:T(8,128)(2,1)}, u32[]{:S(2)}) copy-start(bf16[1536,768]{1,0:T(8,128)(2,1)} %param.14) | copy-start | bytes 7077892
  7.2 45.1 %all-gather.5.cloned.1.call-start = ((), (), s32[]{:S(2)}) async-start(), calls=%async_computation.3 | async-start | bytes 3342336 | tf_op jit(solution)/shard_map/all_gather | solution.py:52
  7.9 106.2 %all-gather.7.cloned.1.call-start = ((), (), s32[]{:S(2)}) async-start(), calls=%async_computation.4 | async-start | bytes 10027008 | tf_op jit(solution)/shard_map/all_gather | solution.py:53
  8.7 443.1 %all-reduce.3.cloned.1.call-start = ((), (), s32[]{:S(2)}) async-start(), calls=%async_computation.6 | async-start | bytes 9437184
  8.7 11.1 %collective-permute-start.1 = (bf16[192,768]{1,0:T(8,128)(2,1)}, bf16[192,768]{1,0:T(8,128)(2,1)S(1)}, u32[]{:S(2)}, u32[]{:S(2)}) collective-permute-start(bf16[192,768]{1,0:T(8,128)(2,1)} %bitcast.169), channel_id=1, source_target_pairs={{0,4},{1,5},{2,6},{3,7},{4,8},{5,9},{6,10},{7,11},{8,12},{9,13},{1... | collective-permute-start | bytes 884744 | tf_op jit(solution)/shard_map/ppermute | solution.py:16
  12.7 197.9 %collective-permute-start = (bf16[192,768]{1,0:T(8,128)(2,1)}, bf16[192,768]{1,0:T(8,128)(2,1)}, u32[]{:S(2)}, u32[]{:S(2)}) collective-permute-start(bf16[192,768]{1,0:T(8,128)(2,1)} %bitcast.170), channel_id=1, source_target_pairs={{4,0},{5,1},{6,2},{7,3},{8,4},{9,5},{10,6},{11,7},{12,8},{13,9},{1... | collective-permute-start | bytes 884744 | tf_op jit(solution)/shard_map/ppermute | solution.py:16
  19.8 107.1 %copy-start.5 = (bf16[192,768]{1,0:T(8,128)(2,1)}, bf16[192,768]{1,0:T(8,128)(2,1)S(1)}, u32[]{:S(2)}) copy-start(bf16[192,768]{1,0:T(8,128)(2,1)S(1)} %collective-permute-done.1) | copy-start | bytes 884740
  137.8 10.0 %slice-start = ((s8[4718592]{0:T(1024)(128)(4,1)}), s8[524288]{0:T(1024)(128)(4,1)S(1)}, s32[]{:S(2)}) async-start(s8[4718592]{0:T(1024)(128)(4,1)} %bitcast.150), calls=%async_computation.7 | async-start | bytes 1048576 | tf_op jit(solution)/shard_map/while
  144.0 2.4 copy-start.2
  144.0 3.8 slice-start.1
  156.4 9.9 %slice-start = ((s8[4718592]{0:T(1024)(128)(4,1)}), s8[524288]{0:T(1024)(128)(4,1)S(1)}, s32[]{:S(2)}) async-start(s8[4718592]{0:T(1024)(128)(4,1)} %bitcast.150), calls=%async_computation.7 | async-start | bytes 1048576 | tf_op jit(solution)/shard_map/while
  162.5 2.4 copy-start.2
  162.5 3.8 slice-start.1
  175.1 9.9 %slice-start = ((s8[4718592]{0:T(1024)(128)(4,1)}), s8[524288]{0:T(1024)(128)(4,1)S(1)}, s32[]{:S(2)}) async-start(s8[4718592]{0:T(1024)(128)(4,1)} %bitcast.150), calls=%async_computation.7 | async-start | bytes 1048576 | tf_op jit(solution)/shard_map/while
  181.1 2.4 copy-start.2
  181.1 3.8 slice-start.1
  193.8 10.0 %slice-start = ((s8[4718592]{0:T(1024)(128)(4,1)}), s8[524288]{0:T(1024)(128)(4,1)S(1)}, s32[]{:S(2)}) async-start(s8[4718592]{0:T(1024)(128)(4,1)} %bitcast.150), calls=%async_computation.7 | async-start | bytes 1048576 | tf_op jit(solution)/shard_map/while
  199.9 2.4 copy-start.2
  199.9 3.8 slice-start.1
  206.4 4.2 copy-start.3
  210.6 3.4 copy-start.4
  210.6 5.4 copy-start.6
  213.0 1.5 copy-start.7
  226.6 308.7 %reduce-scatter.7.cloned.1.call-start = ((), (), s32[]{:S(2)}) async-start(), calls=%async_computation.5 | async-start | bytes 417792
  474.0 206.8 %reduce-scatter.5.cloned.1.call-start = ((), (), s32[]{:S(2)}) async-start(), calls=%async_computation.2 | async-start | bytes 13369344 | tf_op jit(solution)/shard_map/reduce_scatter | solution.py:124
  484.6 0.9 copy-start.8
  484.6 199.7 %copy-start.1 = (bf16[1536,768]{1,0:T(8,128)(2,1)S(1)}, bf16[1536,768]{1,0:T(8,128)(2,1)}, u32[]{:S(2)}) copy-start(bf16[1536,768]{1,0:T(8,128)(2,1)} %param.14) | copy-start | bytes 7077892
Sparse Core Ops, SparseCore 0:
  9.9 42.4 all-gather.4
  54.2 59.9 all-gather.6
  226.8 224.9 all-reduce.2
  474.1 61.1 reduce-scatter.6
  537.9 142.8 reduce-scatter.4
where the time goes:
time: 694 us; the launch traced here: 691 us
  waiting for transfers between devices  414 us (60%)
  local copies, waits for them, and re-layouts  121 us (17%)
  matrix products  75.3 us (11%)
  other arithmetic  49.9 us (7%)
  between operations  14.7 us (2%)
  loops' own time  10.8 us (2%)
    unnamed x7, waiting for transfers between devices  184 us
    reduce_scatter x1, waiting for transfers between devices, shards(): lax.psum_scatter(jnp.concatenate([key_part.reshape(rows * lax.axis_size('...  143 us
    all_gather x1, waiting for transfers between devices, shards(): lax.all_gather(values[0], 'seq', axis=0, tiled=True)  57.1 us
    dynamic_update_slice x8, other arithmetic, shards(): prob_full, prob_pairs, attended_pairs = lax.map(forward_pair, pair_index)  32.3 us
    all_gather x1, waiting for transfers between devices, shards(): lax.all_gather(key_rows[0], 'seq', axis=0, tiled=True)  29.8 us
    unnamed x25, local copies, waits for them, and re-layouts  29 us
    dynamic_slice x20, local copies, waits for them, and re-layouts, column_pair(): lax.dynamic_slice_in_dim(source, pair * 2 * width, 2 * width, 1)  24.9 us
    dot_general x4, matrix products, backward_pair(): jnp.einsum('bhe,lhe->hbl', out_pair, value_pair, preferred_element_type=j...  18.4 us
  transfers between devices with their start and end apart: 7, of which 5 were waited for; matrix products, arithmetic and copies ran while one was open for 29% of the time, Pallas kernels for 0%

commit v1 on v0

v1 whole, which is shorter than its diff:
```python
import math

import jax
import jax.numpy as jnp
from jax import lax
from jax.experimental import pallas as pl
from jax.experimental.pallas import tpu as pltpu
from jax.sharding import PartitionSpec as P

HEADS = 8
KEY = 64
VAL = 192
WIDE = VAL + KEY
LOG2E = math.log2(math.e)
BF = jnp.bfloat16
F32 = jnp.float32
MIB = 1024 * 1024


def rows_by_rows(left, right):
    return lax.dot_general(left, right, (((1,), (1,)), ((), ())), preferred_element_type=F32)


def plain(left, right):
    return lax.dot_general(left, right, (((1,), (0,)), ((), ())), preferred_element_type=F32)


def call(body, outs, scratch, vmem_mib, flops, nbytes, exps, name, far_in=(), far_out=()):
    vmem = pl.BlockSpec(memory_space=pltpu.VMEM)
    far = pl.BlockSpec(memory_space=pl.ANY)
    outs = tuple(outs)

    def run(*arrays):
        got = pl.pallas_call(
            body,
            out_shape=outs,
            in_specs=[far if i in far_in else vmem for i in range(len(arrays))],
            out_specs=tuple(far if i in far_out else vmem for i in range(len(outs))),
            scratch_shapes=list(scratch),
            compiler_params=pltpu.CompilerParams(vmem_limit_bytes=vmem_mib * MIB),
            cost_estimate=pl.CostEstimate(flops=flops, bytes_accessed=nbytes, transcendentals=exps),
            name=name,
        )(*arrays)
        return got if len(outs) > 1 else got[0]

    return run


def side_by_side(block, parts):
    rows = block.shape[0] // parts
    return jnp.concatenate([block[i * rows : (i + 1) * rows] for i in range(parts)], axis=1)


def on_top(block, parts):
    width = block.shape[1] // parts
    return jnp.concatenate([block[:, i * width : (i + 1) * width] for i in range(parts)], axis=0)


def pack_body(q_ref, k_ref, v_ref, out_ref):
    rows = q_ref.shape[0]
    for h in range(HEADS):
        out_ref[h, :rows, :VAL] = v_ref[:, h * VAL : (h + 1) * VAL]
        out_ref[h, :rows, VAL:] = k_ref[:, h * KEY : (h + 1) * KEY]
        part = q_ref[:, h * KEY : (h + 1) * KEY].astype(F32) * (1.0 / math.sqrt(KEY))
        out_ref[h, rows:, :] = side_by_side(part, 4).astype(BF)


def key_tiles(own_ref, oth_ref, count=2):
    chips = own_ref.shape[0]
    rows, step = own_ref.shape[1] * 4 // 5, chips // count
    return [
        (
            side,
            t * step,
            step,
            lambda r=ref, t=t: r[t * step : (t + 1) * step, :rows, :].reshape(step * rows, WIDE),
        )
        for side, ref in enumerate((own_ref, oth_ref))
        for t in range(count)
    ]


def forward_body(own_ref, oth_ref, q_ref, att_ref, lse_ref, send_ref, score_ref):
    block = score_ref.shape[0]
    chips = own_ref.shape[0]
    rows = own_ref.shape[1] * 4 // 5
    mine = chips * rows
    for c in range(chips):
        query = on_top(own_ref[c, rows:, :].astype(F32), 4)
        padded = jnp.concatenate([jnp.zeros((rows, VAL), F32), query], axis=1)
        q_ref[c * rows : (c + 1) * rows, :] = padded.astype(BF)
    tiles = key_tiles(own_ref, oth_ref)
    tile = 2 * mine // len(tiles)

    def step(b, _):
        at = pl.ds(pl.multiple_of(b * block, block), block)
        query = q_ref[at, :]
        top = None
        for j, (_, _, _, part) in enumerate(tiles):
            scores = rows_by_rows(query, part())
            score_ref[:, j * tile : (j + 1) * tile] = scores
            high = jnp.max(scores, axis=1, keepdims=True)
            top = high if top is None else jnp.maximum(top, high)
        top = top * LOG2E
        total = jnp.zeros((block, 1), F32)
        summed = jnp.zeros((block, WIDE), F32)
        for j, (_, _, _, part) in enumerate(tiles):
            expo = jnp.exp2(score_ref[:, j * tile : (j + 1) * tile] * LOG2E - top)
            total = total + jnp.sum(expo, axis=1, keepdims=True)
            summed = summed + plain(expo.astype(BF), part())
        att_ref[at, :] = (summed * (1.0 / total)).astype(BF)
        turned = jnp.transpose(jnp.broadcast_to(top + jnp.log2(total), (block, 128)))
        lse_ref[b] = turned[:8, :]
        return 0

    lax.fori_loop(0, mine // block, step, 0)
    for c in range(chips):
        part = att_ref[c * rows : (c + 1) * rows, :].astype(F32)
        for j in range(3):
            piece = side_by_side(part[:, j * 64 : (j + 1) * 64], 4).astype(BF)
            send_ref[c, j * (rows // 4) : (j + 1) * (rows // 4), :] = piece


def probs_body(own_ref, oth_ref, q_ref, lse_ref, far_prob_ref, kt_ref, prob_ref, sems):
    blocks, _, block = lse_ref.shape
    tiles = key_tiles(own_ref, oth_ref)
    tile = prob_ref.shape[0] // len(tiles)
    for j, (_, _, _, part) in enumerate(tiles):
        here = slice(j * tile, (j + 1) * tile)
        keys = part()
        kt_ref[:, here] = jnp.transpose(keys[:, 128:].astype(F32)).astype(BF)
        for b in range(blocks):
            at = slice(b * block, (b + 1) * block)
            scores = rows_by_rows(keys, q_ref[at, :])
            prob_ref[here, at] = jnp.exp2(scores * LOG2E - lse_ref[b][:1, :]).astype(BF)
        pltpu.make_async_copy(prob_ref.at[here], far_prob_ref.at[here], sems.at[j]).start()
    for j in range(len(tiles)):
        here = slice(j * tile, (j + 1) * tile)
        pltpu.make_async_copy(prob_ref.at[here], far_prob_ref.at[here], sems.at[j]).wait()


def branch_body(cot_ref, ahead_ref, behind_ref, conv_ref, out_ref):
    ring = 4
    place = lax.axis_index("seq") // (lax.axis_size("seq") // ring)
    out_ref[...] = (
        jnp.where(place < ring - 1, rows_by_rows(ahead_ref[...], conv_ref[0]), 0.0)
        + rows_by_rows(cot_ref[...], conv_ref[1])
        + jnp.where(place > 0, rows_by_rows(behind_ref[...], conv_ref[2]), 0.0)
    )


def gelu_pieces(wide):
    normal_cdf = 0.5 * (1.0 + lax.erf(wide * (1.0 / math.sqrt(2.0))))
    density = jnp.exp(-0.5 * wide * wide) * (1.0 / math.sqrt(2.0 * math.pi))
    return (wide * normal_cdf, normal_cdf + wide * density)


def middle_body(recv_ref, proj_ref, stream_ref, cot_ref, branch_ref, grad_ref, send_ref, *rest):
    *acts, att_ref = rest
    ring = len(acts)
    place = lax.axis_index("seq") // (lax.axis_size("seq") // ring)
    quarter = recv_ref.shape[1] // 3
    for h in range(HEADS):
        for j in range(3):
            piece = recv_ref[h, j * quarter : (j + 1) * quarter, :].astype(F32)
            at = h * VAL + j * 64
            att_ref[:, at : at + 64] = on_top(piece, 4).astype(BF)
    inside = stream_ref[...].astype(F32) + plain(att_ref[...], proj_ref[...])
    activated, slope = gelu_pieces(inside.astype(BF).astype(F32))
    grad = (cot_ref[...].astype(F32) + slope * branch_ref[...]).astype(BF)
    grad_ref[...] = grad
    out_grad = rows_by_rows(grad, proj_ref[...])
    for h in range(HEADS):
        for j in range(3):
            at = h * VAL + j * 64
            piece = side_by_side(out_grad[:, at : at + 64], 4).astype(BF)
            send_ref[h, j * quarter : (j + 1) * quarter, :] = piece
    share = activated.shape[1] // ring
    blocks = [activated[:, k * share : (k + 1) * share].astype(BF) for k in range(ring)]
    for r, act_ref in enumerate(acts):
        block = blocks[0]
        for k in range(1, ring):
            block = jnp.where(lax.rem(place + r, ring) == k, blocks[k], block)
        act_ref[...] = block


def backward_body(
    own_ref,
    oth_ref,
    q_ref,
    kt_ref,
    far_prob_ref,
    att_ref,
    recv_ref,
    own_out_ref,
    oth_out_ref,
    dq_ref,
    out_ref,
    grad_ref,
    turned_ref,
    prob_ref,
    sems,
):
    def arriving(j):
        here = slice(j * tile, (j + 1) * tile)
        return pltpu.make_async_copy(far_prob_ref.at[here], prob_ref.at[here], sems.at[j])

    tiles = key_tiles(own_ref, oth_ref)
    tile = prob_ref.shape[0] // len(tiles)
    for j in range(len(tiles)):
        arriving(j).start()
    chips, rows, _ = own_out_ref.shape
    mine = chips * rows
    quarter = rows // 4
    block = 512
    for c in range(chips):
        pieces = [
            on_top(recv_ref[c, j * quarter : (j + 1) * quarter, :].astype(F32), 4) for j in range(3)
        ]
        padded = jnp.concatenate([*pieces, jnp.zeros((rows, KEY), F32)], axis=1)
        out_ref[c * rows : (c + 1) * rows, :] = padded.astype(BF)
    deltas = []
    for b in range(mine // block):
        at = slice(b * block, (b + 1) * block)
        each = out_ref[at, :].astype(F32) * att_ref[at, :].astype(F32)
        delta = jnp.sum(each, axis=1, keepdims=True)
        deltas.append(jnp.transpose(jnp.broadcast_to(delta, (block, 128)))[:1, :])
    for j, (side, first, step, part) in enumerate(tiles):
        here = slice(j * tile, (j + 1) * tile)
        keys = part()
        slot = grad_ref.at[j % 2]
        arriving(j).wait()
        for b, delta in enumerate(deltas):
            at = slice(b * block, (b + 1) * block)
            grads = rows_by_rows(keys, out_ref[at, :]) - delta
            slot[:, at] = (prob_ref[here, at].astype(F32) * grads).astype(BF)
        summed = plain(prob_ref[here, :], out_ref[...]) + plain(slot[...], q_ref[...])
        to = (own_out_ref, oth_out_ref)[side]
        to[first : first + step] = summed.astype(BF).reshape(step, rows, WIDE)
        turned = plain(kt_ref[:, here], slot[...])
        turned_ref[...] = turned if j == 0 else turned_ref[...] + turned
    scale = 1.0 / math.sqrt(KEY)
    for b in range(mine // 384):
        turned = jnp.transpose(turned_ref[:, b * 384 : (b + 1) * 384]) * scale
        for i in range(384 // rows):
            part = turned[i * rows : (i + 1) * rows, 64:]
            dq_ref[b * (384 // rows) + i] = side_by_side(part, 4).astype(BF)


def weight_body(*refs):
    ring = 4
    acts, cots, outs = refs[:ring], refs[ring : 2 * ring], refs[2 * ring : 3 * ring]
    act_ref, cot_ref = refs[3 * ring :]
    index = lax.axis_index("seq")
    stride = lax.axis_size("seq") // ring
    place, here = index // stride, index % stride
    rows, share = acts[0].shape
    for r in range(ring):
        at = pl.ds(pl.multiple_of(lax.rem(place + r, ring) * rows, rows), rows)
        act_ref[at, :] = acts[r][...]
        cot_ref[at, :] = cots[r][...]
    bins = ring * rows
    act = jnp.transpose(act_ref[...].astype(F32)).astype(BF)
    terms = (
        plain(act[:, : bins - rows], cot_ref[rows:, :]),
        plain(act, cot_ref[...]),
        plain(act[:, rows:], cot_ref[: bins - rows, :]),
    )
    piece = share // 4
    parts = [
        jnp.concatenate([t[g * piece : (g + 1) * piece] for t in terms], axis=0).astype(BF)
        for g in range(4)
    ]
    for r in range(4):
        part = parts[r]
        for g in range(1, 4):
            part = jnp.where(here == g, parts[g ^ r], part)
        outs[r][...] = part


def quarters(whole_ref, bit, outs):
    size = whole_ref.shape[0] // 4
    mine = lax.axis_index("dp") // bit % 4
    for r, out_ref in enumerate(outs):
        at = pl.ds(pl.multiple_of(jnp.bitwise_xor(mine, r) * size, size), size)
        out_ref[...] = whole_ref[at, :].astype(out_ref.dtype)


def sum_of(refs):
    both = refs[0][...].astype(F32)
    for ref in refs[1:]:
        both = both + ref[...].astype(F32)
    return both


def first_sum_body(*refs):
    refs[8][...] = jnp.transpose(sum_of(refs[:4]))
    quarters(refs[8], 4, refs[4:8])


def second_sum_body(*refs):
    refs[8][...] = sum_of(refs[:4])
    quarters(refs[8], 1, refs[4:8])


def last_sum_body(*refs):
    both = jnp.transpose(sum_of(refs[:4])) * (1.0 / lax.axis_size("dp"))
    rows = both.shape[0] // 3
    for t in range(3):
        refs[4][t] = both[t * rows : (t + 1) * rows]


def add_body(own_ref, recv_ref, dq_ref, out_ref):
    rows = own_ref.shape[1]
    for c in range(own_ref.shape[0]):
        out_ref[c, :rows, :] = (own_ref[c].astype(F32) + recv_ref[c].astype(F32)).astype(BF)
        out_ref[c, rows:, :] = dq_ref[c]


def finish_body(recv_ref, q_ref, k_ref, v_ref):
    rows = q_ref.shape[0]
    for h in range(HEADS):
        v_ref[:, h * VAL : (h + 1) * VAL] = recv_ref[h, :rows, :VAL]
        k_ref[:, h * KEY : (h + 1) * KEY] = recv_ref[h, :rows, VAL:]
        q_ref[:, h * KEY : (h + 1) * KEY] = on_top(recv_ref[h, rows:, :].astype(F32), 4).astype(BF)


def shards(queries, key_rows, values, out_proj, stream, cotangent, conv_weight):
    count = lax.axis_size("seq")
    chips = count // 2
    rows = queries.shape[1]
    channels = cotangent.shape[2]
    mine = chips * rows
    same_core = [[2 * c + p for c in range(chips)] for p in range(2)]
    partner = [(i, i ^ 1) for i in range(count)]

    def shape(*dims, dtype=BF):
        return jax.ShapeDtypeStruct(dims, dtype)

    def exchange(value):
        return lax.all_to_all(value, "seq", 0, 0, axis_index_groups=same_core, tiled=True)

    def swap(value, bit=1):
        return lax.ppermute(value, "seq", [(i, i ^ bit) for i in range(count)])

    def round_ring(value, by):
        return lax.ppermute(value, "seq", [(i, (i - by) % count) for i in range(count)])

    ring = 4
    stride = count // ring
    copies = lax.axis_size("dp")
    block = 512
    pairs_done = mine * 2 * mine
    part, quarter = 3 * channels // count, rows // 4

    packed = call(pack_body, [shape(chips, rows + quarter, WIDE)], [], 60, 0, 2 * MIB, 0, "pack")(
        queries[0], key_rows[0], values[0]
    )
    own, cot = lax.optimization_barrier((exchange(packed), cotangent[0]))
    oth = swap(own)
    cots = [round_ring(cot, by * stride) for by in (1, 2, 3)]
    query, attended, lse, send = call(
        forward_body,
        [
            shape(mine, WIDE),
            shape(mine, WIDE),
            shape(mine // block, 8, block, dtype=F32),
            shape(chips, 3 * quarter, WIDE),
        ],
        [pltpu.VMEM((block, 2 * mine), F32)],
        56,
        4 * pairs_done * WIDE,
        6 * MIB,
        pairs_done,
        "forward",
    )(own, oth)
    send, *cots = lax.optimization_barrier((send, *cots))
    recv = exchange(send)
    probs, keys_turned = call(
        probs_body,
        [shape(2 * mine, mine), shape(128, 2 * mine)],
        [pltpu.VMEM((2 * mine, mine), BF), pltpu.SemaphoreType.DMA((4,))],
        56,
        2 * pairs_done * WIDE,
        12 * MIB,
        pairs_done,
        "probs",
        far_out=(0,),
    )(own, oth, query, lse)
    branch = call(
        branch_body,
        [shape(rows, channels, dtype=F32)],
        [],
        56,
        6 * rows * channels * channels,
        5 * MIB,
        0,
        "branch",
    )(cot, cots[0], cots[2], conv_weight)
    recv, probs, branch = lax.optimization_barrier((recv, probs, branch))
    stream_grad, send, *acts = call(
        middle_body,
        [
            shape(rows, channels),
            shape(chips, 3 * quarter, WIDE),
            *[shape(rows, channels // ring)] * ring,
        ],
        [pltpu.VMEM((rows, HEADS * VAL), BF)],
        56,
        4 * rows * channels * HEADS * VAL,
        5 * MIB,
        2 * rows * channels,
        "middle",
    )(recv, out_proj, stream[0], cot, branch)
    moved = [round_ring(acts[ring - by], by * stride) for by in (1, 2, 3)]
    send, *moved = lax.optimization_barrier((send, *moved))
    recv = exchange(send)
    parts = call(
        weight_body,
        [shape(part, channels)] * 4,
        [
            pltpu.VMEM((ring * rows, channels // ring), BF),
            pltpu.VMEM((ring * rows, channels), BF),
        ],
        56,
        6 * ring * rows * channels * channels // ring,
        5 * MIB,
        0,
        "weight",
    )(acts[0], *moved, cot, *cots)
    def shared(parts, size, body, name):
        return call(
            body,
            [shape(size, part, dtype=F32)] + [shape(size, part)] * 3,
            [pltpu.VMEM((4 * size, part), F32)],
            12,
            0,
            MIB,
            0,
            name,
        )(*parts)

    def dp_swap(value, bit):
        return lax.ppermute(value, "dp", [(i, i ^ bit) for i in range(copies)])

    given = [swap(parts[r], r) for r in (1, 2, 3)]
    parts = shared([parts[0], *given], channels // 4, first_sum_body, "first_sum")
    recv, *parts = lax.optimization_barrier((recv, *parts))
    parts = [parts[0]] + [dp_swap(parts[r], 4 * r) for r in (1, 2, 3)]
    own_grad, oth_grad, dq = call(
        backward_body,
        [shape(chips, rows, WIDE), shape(chips, rows, WIDE), shape(chips, quarter, WIDE)],
        [
            pltpu.VMEM((mine, WIDE), BF),
            pltpu.VMEM((2, mine // 2, mine), BF),
            pltpu.VMEM((128, mine), F32),
            pltpu.VMEM((2 * mine, mine), BF),
            pltpu.SemaphoreType.DMA((4,)),
        ],
        56,
        8 * pairs_done * WIDE,
        16 * MIB,
        0,
        "backward",
        far_in=(4,),
    )(own, oth, query, keys_turned, probs, attended, recv)
    *parts, oth_grad = lax.optimization_barrier((*parts, oth_grad))
    swapped = swap(oth_grad)
    parts = shared(parts, channels // copies, second_sum_body, "second_sum")
    packed = call(add_body, [shape(chips, rows + quarter, WIDE)], [], 12, 0, 3 * MIB, 0, "add")(
        own_grad, swapped, dq
    )
    packed, *parts = lax.optimization_barrier((packed, *parts))
    recv = exchange(packed)
    parts = [parts[0]] + [dp_swap(parts[r], r) for r in (1, 2, 3)]
    weight_grad = call(
        last_sum_body,
        [shape(3, channels // count, channels // copies, dtype=F32)],
        [],
        12,
        0,
        MIB,
        0,
        "last_sum",
    )(*parts)
    query_grad, key_grad, value_grad = call(
        finish_body,
        [shape(rows, HEADS * KEY), shape(rows, HEADS * KEY), shape(rows, HEADS * VAL)],
        [],
        12,
        0,
        2 * MIB,
        0,
        "finish",
    )(recv)
    return (query_grad[None], key_grad[None], value_grad[None], stream_grad[None], weight_grad)


def solution(mesh):
    return jax.shard_map(
        shards,
        mesh=mesh,
        in_specs=(
            P("dp", "seq", None),
            P("dp", "seq", None),
            P("dp", "seq", None),
            P(),
            P("dp", "seq", None),
            P("dp", "seq", None),
            P(),
        ),
        out_specs=(
            P("dp", "seq", None),
            P("dp", "seq", None),
            P("dp", "seq", None),
            P("dp", "seq", None),
            P(None, "seq", "dp"),
        ),
        check_vma=False,
    )
```

time: 694 us -> 156 us (0.22)
  waiting for transfers between devices: 414 us -> 29.9 us
  local copies, waits for them, and re-layouts: 121 us -> 4.78 us
  matrix products: 75.3 us -> 0 us
  Pallas kernels: 0 us -> 61.6 us
  other arithmetic: 49.9 us -> 0 us
  starting transfers between devices: 5.63 us -> 38.1 us
  blocking collectives: 0 us -> 19.4 us
  between operations: 14.7 us -> 0.85 us
  loops' own time: 10.8 us -> 0 us
    unnamed x7 -> x0, waiting for transfers between devices: 184 us -> none
    reduce_scatter x1 -> x0, waiting for transfers between devices: 143 us -> none  [shards(): lax.psum_scatter(jnp.concatenate([key_part.reshape(rows * lax.axis_size('...]
    all_gather x2 -> x0, waiting for transfers between devices: 86.9 us -> none  [the longest x1 57.1 us: shards(): lax.all_gather(values[0], 'seq', axis=0, tiled=True)]
    pallas_call x0 -> x12, Pallas kernels: none -> 61.6 us  [run(): pl.pallas_call(body, out_shape=outs, in_specs=[far if i in far_in else vm...]
    dot_general x22 -> x0, matrix products: 60.9 us -> none  [the longest x4 18.4 us: backward_pair(): jnp.einsum('bhe,lhe->hbl', out_pair, value_pair, preferred_element_type=j...]
    dynamic_update_slice x8 -> x0, other arithmetic: 32.3 us -> none  [shards(): prob_full, prob_pairs, attended_pairs = lax.map(forward_pair, pair_index)]
    dynamic_slice x28 -> x0, local copies, waits for them, and re-layouts: 29.5 us -> none  [the longest x20 24.9 us: column_pair(): lax.dynamic_slice_in_dim(source, pair * 2 * width, 2 * width, 1)]
    ppermute x2 -> x17, waiting for transfers between devices: 0.01 us -> 28 us  [the longest x5 14.5 us: swap(): return lax.ppermute(value, 'seq', [(i, i ^ bit) for i in range(count)])]
  transfers between devices with their start and end apart: 7 -> 20, of which waited for: 5 -> 8; matrix products, arithmetic and copies ran while one was open for 29% -> 0% of each run, Pallas kernels for 0% -> 33%
where the time goes in v1:
time: 156 us; the launch traced here: 155 us
  Pallas kernels  61.6 us (39%)
  starting transfers between devices  38.1 us (24%)
  waiting for transfers between devices  29.9 us (19%)
  blocking collectives  19.4 us (12%)
  local copies, waits for them, and re-layouts  4.78 us (3%)
    pallas_call x12, Pallas kernels, run(): pl.pallas_call(body, out_shape=outs, in_specs=[far if i in far_in else vm...  61.6 us
    all_to_all x1, blocking collectives, exchange(): lax.all_to_all(value, 'seq', 0, 0, axis_index_groups=same_core, tiled=True)  19.4 us
    ppermute x5, waiting for transfers between devices, swap(): return lax.ppermute(value, 'seq', [(i, i ^ bit) for i in range(count)])  14.5 us
    ppermute x6, starting transfers between devices, dp_swap(): return lax.ppermute(value, 'dp', [(i, i ^ bit) for i in range(copies)])  12.4 us
    all_to_all x3, starting transfers between devices, exchange(): lax.all_to_all(value, 'seq', 0, 0, axis_index_groups=same_core, tiled=True)  10.8 us
    ppermute x6, waiting for transfers between devices, dp_swap(): return lax.ppermute(value, 'dp', [(i, i ^ bit) for i in range(copies)])  8.41 us
    ppermute x5, starting transfers between devices, swap(): return lax.ppermute(value, 'seq', [(i, i ^ bit) for i in range(count)])  7.74 us
    ppermute x6, starting transfers between devices, round_ring(): lax.ppermute(value, 'seq', [(i, (i - by) % count) for i in range(count)])  7.06 us
  transfers between devices with their start and end apart: 20, of which 8 were waited for; matrix products, arithmetic and copies ran while one was open for 0% of the time, Pallas kernels for 33%

profile of v1, /device:TPU:1, one launch (start us, length us, event | category | flops | bytes accessed | tf_op | source)
XLA Modules:
  0.0 154.7 jit_solution(1922404314004069695)
XLA Ops:
  0.6 0.0 copy-start.4
  0.6 2.6 %pack.1 = bf16[8,240,256]{2,1,0:T(8,128)(2,1)} custom-call(bf16[192,512]{1,0:T(8,128)(2,1)} %bitcast.17, bf16[192,512]{1,0:T(8,128)(2,1)} %bitcast.18, bf16[192,1536]{1,0:T(8,128)(2,1)} %bitcast.15), custom_call_target="tpu_custom_call" | custom-call | bytes 2097152 | tf_op jit(solution)/shard_map/pack/pallas_call | solution.py:34
  3.2 19.4 %all_to_all.20.own_ref = bf16[8,240,256]{2,1,0:T(8,128)(2,1)S(1)} all-to-all(bf16[8,240,256]{2,1,0:T(8,128)(2,1)} %pack.1), channel_id=1, replica_groups={{0,2,4,6,8,10,12,14},{1,3,5,7,9,11,13,15},{16,18,20,22,24,26,28,30},{17..., dimensions={0} | all-to-all | bytes 1966080 | tf_op jit(solution)/shard_map/all_to_all | solution.py:341
  22.7 2.1 %collective-permute-start = (bf16[8,240,256]{2,1,0:T(8,128)(2,1)S(1)}, bf16[8,240,256]{2,1,0:T(8,128)(2,1)S(1)}, u32[]{:S(2)}, u32[]{:S(2)}) collective-permute-start(bf16[8,240,256]{2,1,0:T(8,128)(2,1)S(1)} %all_to_all.20.own_ref), channel_id=1, source_target_pairs={{0,1},{1,0},{2,3},{3,2},{4,5},{5,4},{6,7},{7,6},{8,9},{9,8},{10,11... | collective-permute-start | bytes 2949128 | tf_op jit(solution)/shard_map/ppermute | solution.py:344
  24.8 0.2 collective-permute-start.3
  25.0 1.9 %collective-permute-start.2 = (bf16[192,768]{1,0:T(8,128)(2,1)S(1)}, bf16[192,768]{1,0:T(8,128)(2,1)S(1)}, u32[]{:S(2)}, u32[]{:S(2)}) collective-permute-start(bf16[192,768]{1,0:T(8,128)(2,1)S(1)} %bitcast.13), channel_id=1, source_target_pairs={{0,8},{1,9},{2,10},{3,11},{4,12},{5,13},{6,14},{7,15},{8,0},{9,1},... | collective-permute-start | bytes 884744 | tf_op jit(solution)/shard_map/ppermute | solution.py:347
  26.9 1.3 collective-permute-start.1
  28.2 0.9 copy-done.9
  29.1 14.9 %forward.1 = (bf16[1536,256]{1,0:T(8,128)(2,1)}, bf16[1536,256]{1,0:T(8,128)(2,1)}, f32[3,8,512]{2,1,0:T(8,128)}, bf16[8,144,256]{2,1,0:T(8,128)(2,1)}) custom-call(bf16[8,240,256]{2,1,0:T(8,128)(2,1)} %copy-done.5, bf16[8,240,256]{2,1,0:T(8,128)(2,1)} %copy-done.9), custom_call_target="tpu_custom_call" | custom-call | flops 4831838208 | bytes 6291456 | tf_op jit(solution)/shard_map/forward/pallas_call | solution.py:34
  44.0 3.7 %all-to-all-start.1 = ((bf16[8,144,256]{2,1,0:T(8,128)(2,1)}), bf16[8,144,256]{2,1,0:T(8,128)(2,1)S(1)}, u32[]{:S(2)}, u32[]{:S(2)}) async-start(bf16[8,144,256]{2,1,0:T(8,128)(2,1)} %get-tuple-element.69), calls=%async_computation.1 | async-start | bytes 1179648 | tf_op jit(solution)/shard_map/all_to_all | solution.py:341
  47.8 4.5 %branch.1.branch_ref = f32[192,768]{1,0:T(8,128)} custom-call(bf16[192,768]{1,0:T(8,128)(2,1)} %bitcast.9, bf16[192,768]{1,0:T(8,128)(2,1)} %copy-done.8, bf16[192,768]{1,0:T(8,128)(2,1)} %copy-done.7, bf16[3,768,768]{2,1,0:T(8,128)(2,1)} %conv_ref.1), custom_call_target="tpu_custom_call" | custom-call | flops 679477248 | bytes 5242880 | tf_op jit(solution)/shard_map/branch/pallas_call | solution.py:34
  52.3 7.1 %probs.1 = (bf16[3072,1536]{1,0:T(8,128)(2,1)}, bf16[128,3072]{1,0:T(8,128)(2,1)}) custom-call(bf16[8,240,256]{2,1,0:T(8,128)(2,1)} %copy-done.5, bf16[8,240,256]{2,1,0:T(8,128)(2,1)} %copy-done.9, bf16[1536,256]{1,0:T(8,128)(2,1)} %get-tuple-element.64.q_ref, f32[3,8,512]{2,1,0:T(8,128)} %get-tuple-element.65.lse_ref), custom_call_target="tpu_custom_call" | custom-call | flops 2415919104 | bytes 12582912 | tf_op jit(solution)/shard_map/probs/pallas_call | solution.py:34
  59.4 0.0 copy-start.3
  59.4 0.8 copy-done.3
  60.2 5.2 %middle.1 = (bf16[192,768]{1,0:T(8,128)(2,1)}, bf16[8,144,256]{2,1,0:T(8,128)(2,1)}, bf16[192,192]{1,0:T(8,128)(2,1)}, bf16[192,192]{1,0:T(8,128)(2,1)}, bf16[19...) custom-call(bf16[8,144,256]{2,1,0:T(8,128)(2,1)} %copy-done.3, bf16[1536,768]{1,0:T(8,128)(2,1)} %proj_ref.1, ...), custom_call_target="tpu_custom_call" | custom-call | flops 905969664 | bytes 5242880 | tf_op jit(solution)/shard_map/middle/pallas_call | solution.py:34
  65.4 2.5 %collective-permute-start.4 = (bf16[192,192]{1,0:T(8,128)(2,1)}, bf16[192,192]{1,0:T(8,128)(2,1)S(1)}, u32[]{:S(2)}, u32[]{:S(2)}) collective-permute-start(bf16[192,192]{1,0:T(8,128)(2,1)} %get-tuple-element.78), channel_id=1, source_target_pairs={{0,12},{1,13},{2,14},{3,15},{4,0},{5,1},{6,2},{7,3},{8,4},{9,5},{1... | collective-permute-start | bytes 221192 | tf_op jit(solution)/shard_map/ppermute | solution.py:347
  67.9 0.6 collective-permute-start.5
  68.5 0.6 collective-permute-start.6
  69.1 0.8 collective-permute-done.4.refs_1_
  69.9 3.3 %collective-permute-done.5.refs_2_ = bf16[192,192]{1,0:T(8,128)(2,1)S(1)} collective-permute-done((bf16[192,192]{1,0:T(8,128)(2,1)}, bf16[192,192]{1,0:T(8,128)(2,1)S(1)}, u32[]{:S(2)}, u32[]{:S(2)}) %collective-permute-start.5) | collective-permute-done | bytes 73760 | tf_op jit(solution)/shard_map/ppermute | solution.py:347
  73.2 1.0 collective-permute-done.6.refs_3_
  74.2 3.5 %all-to-all-start.2 = ((bf16[8,144,256]{2,1,0:T(8,128)(2,1)}), bf16[8,144,256]{2,1,0:T(8,128)(2,1)S(1)}, u32[]{:S(2)}, u32[]{:S(2)}) async-start(bf16[8,144,256]{2,1,0:T(8,128)(2,1)} %get-tuple-element.81), calls=%async_computation.2 | async-start | bytes 1179648 | tf_op jit(solution)/shard_map/all_to_all | solution.py:341
  77.8 3.4 %weight.1 = (bf16[144,768]{1,0:T(8,128)(2,1)}, bf16[144,768]{1,0:T(8,128)(2,1)}, bf16[144,768]{1,0:T(8,128)(2,1)}, bf16[144,768]{1,0:T(8,128)(2,1)}) custom-call(bf16[192,192]{1,0:T(8,128)(2,1)} %get-tuple-element.82.refs_0_, bf16[192,192]{1,0:T(8,128)(2,1)} %copy-done.11, bf16[192,192]{1,0:T(8,128)(2,1)} %copy-done.12, bf16[192,192]{1,0:T(8,128)(2,1)} %copy-done.13, ...), custom_call_target="tpu_custom_call" | custom-call | flops 679477248 | bytes 5242880 | tf_op jit(solution)/shard_map/weight/pallas_call | solution.py:34
  81.1 2.9 %collective-permute-start.7 = (bf16[144,768]{1,0:T(8,128)(2,1)}, bf16[144,768]{1,0:T(8,128)(2,1)S(1)}, u32[]{:S(2)}, u32[]{:S(2)}) collective-permute-start(bf16[144,768]{1,0:T(8,128)(2,1)} %get-tuple-element.88), channel_id=1, source_target_pairs={{0,1},{1,0},{2,3},{3,2},{4,5},{5,4},{6,7},{7,6},{8,9},{9,8},{10,11... | collective-permute-start | bytes 663560 | tf_op jit(solution)/shard_map/ppermute | solution.py:344
  84.0 1.6 %collective-permute-start.8 = (bf16[144,768]{1,0:T(8,128)(2,1)}, bf16[144,768]{1,0:T(8,128)(2,1)S(1)}, u32[]{:S(2)}, u32[]{:S(2)}) collective-permute-start(bf16[144,768]{1,0:T(8,128)(2,1)} %get-tuple-element.89), channel_id=1, source_target_pairs={{0,2},{1,3},{2,0},{3,1},{4,6},{5,7},{6,4},{7,5},{8,10},{9,11},{10,... | collective-permute-start | bytes 663560 | tf_op jit(solution)/shard_map/ppermute | solution.py:344
  85.7 0.1 collective-permute-start.9
  85.7 7.7 %collective-permute-done.8.refs_2_ = bf16[144,768]{1,0:T(8,128)(2,1)S(1)} collective-permute-done((bf16[144,768]{1,0:T(8,128)(2,1)}, bf16[144,768]{1,0:T(8,128)(2,1)S(1)}, u32[]{:S(2)}, u32[]{:S(2)}) %collective-permute-start.8) | collective-permute-done | bytes 221216 | tf_op jit(solution)/shard_map/ppermute | solution.py:344
  93.4 4.7 %collective-permute-done.9.refs_3_ = bf16[144,768]{1,0:T(8,128)(2,1)S(1)} collective-permute-done((bf16[144,768]{1,0:T(8,128)(2,1)}, bf16[144,768]{1,0:T(8,128)(2,1)S(1)}, u32[]{:S(2)}, u32[]{:S(2)}) %collective-permute-start.9) | collective-permute-done | bytes 221216 | tf_op jit(solution)/shard_map/ppermute | solution.py:344
  98.1 0.9 copy-done.1
  99.1 0.3 first_sum.1
  99.4 0.0 copy-start.6
  99.4 3.1 %collective-permute-start.10 = (bf16[192,144]{1,0:T(8,128)(2,1)S(1)}, bf16[192,144]{1,0:T(8,128)(2,1)S(1)}, u32[]{:S(2)}, u32[]{:S(2)}) collective-permute-start(bf16[192,144]{1,0:T(8,128)(2,1)S(1)} %get-tuple-element.98), channel_id=1, source_target_pairs={{0,64},{16,80},{32,96},{48,112},{64,0},{80,16},{96,32},{112,48},{1... | collective-permute-start | bytes 165896 | tf_op jit(solution)/shard_map/ppermute | solution.py:444
  102.5 5.1 %collective-permute-start.11 = (bf16[192,144]{1,0:T(8,128)(2,1)S(1)}, bf16[192,144]{1,0:T(8,128)(2,1)S(1)}, u32[]{:S(2)}, u32[]{:S(2)}) collective-permute-start(bf16[192,144]{1,0:T(8,128)(2,1)S(1)} %get-tuple-element.99), channel_id=1, source_target_pairs={{0,128},{16,144},{32,160},{48,176},{64,192},{80,208},{96,224},{112... | collective-permute-start | bytes 165896 | tf_op jit(solution)/shard_map/ppermute | solution.py:444
  107.6 20.3 %backward.1 = (bf16[8,192,256]{2,1,0:T(8,128)(2,1)}, bf16[8,192,256]{2,1,0:T(8,128)(2,1)}, bf16[8,48,256]{2,1,0:T(8,128)(2,1)}) custom-call(bf16[8,240,256]{2,1,0:T(8,128)(2,1)} %copy-done.5, bf16[8,240,256]{2,1,0:T(8,128)(2,1)} %copy-done.9, bf16[1536,256]{1,0:T(8,128)(2,1)} %get-tuple-element.64.q_ref, bf16[128,3072]{1,0:T(8,128)(2,1)} %get-tuple-element.66.kt_ref, ...), custom_call_target="tpu_custom_call" | custom-call | flops 9663676416 | bytes 16777216 | tf_op jit(solution)/shard_map/backward/pallas_call | solution.py:34
  127.9 1.0 collective-permute-start.13
  129.0 0.1 second_sum.1
  129.0 2.1 %collective-permute-done.13.recv_ref = bf16[8,192,256]{2,1,0:T(8,128)(2,1)S(1)} collective-permute-done((bf16[8,192,256]{2,1,0:T(8,128)(2,1)}, bf16[8,192,256]{2,1,0:T(8,128)(2,1)S(1)}, u32[]{:S(2)}, u32[]{:S(2)}) %collective-permute-start.13) | collective-permute-done | bytes 786464 | tf_op jit(solution)/shard_map/ppermute | solution.py:344
  131.1 1.1 copy-done
  132.2 0.9 copy-done.2
  133.2 1.1 add.1
  134.3 3.6 %all-to-all-start.3 = ((bf16[8,240,256]{2,1,0:T(8,128)(2,1)}), bf16[8,240,256]{2,1,0:T(8,128)(2,1)S(1)}, u32[]{:S(2)}, u32[]{:S(2)}) async-start(bf16[8,240,256]{2,1,0:T(8,128)(2,1)} %add.1), calls=%async_computation.3 | async-start | bytes 1966080 | tf_op jit(solution)/shard_map/all_to_all | solution.py:341
  137.9 2.7 %collective-permute-start.14 = (bf16[48,144]{1,0:T(8,128)(2,1)S(1)}, bf16[48,144]{1,0:T(8,128)(2,1)S(1)}, u32[]{:S(2)}, u32[]{:S(2)}) collective-permute-start(bf16[48,144]{1,0:T(8,128)(2,1)S(1)} %get-tuple-element.118), channel_id=1, source_target_pairs={{0,16},{16,0},{32,48},{48,32},{64,80},{80,64},{96,112},{112,96},{1... | collective-permute-start | bytes 41480 | tf_op jit(solution)/shard_map/ppermute | solution.py:444
  140.6 0.7 collective-permute-start.15
  141.3 0.8 collective-permute-start.16
  142.1 8.4 %collective-permute-done.14.refs_1_ = bf16[48,144]{1,0:T(8,128)(2,1)S(1)} collective-permute-done((bf16[48,144]{1,0:T(8,128)(2,1)S(1)}, bf16[48,144]{1,0:T(8,128)(2,1)S(1)}, u32[]{:S(2)}, u32[]{:S(2)}) %collective-permute-start.14) | collective-permute-done | bytes 13856 | tf_op jit(solution)/shard_map/ppermute | solution.py:444
  150.5 0.7 last_sum.1
  151.2 1.9 %all-to-all-done.3.recv_ref = bf16[8,240,256]{2,1,0:T(8,128)(2,1)S(1)} async-done(((bf16[8,240,256]{2,1,0:T(8,128)(2,1)}), bf16[8,240,256]{2,1,0:T(8,128)(2,1)S(1)}, u32[]{:S(2)}, u32[]{:S(2)}) %all-to-all-start.3) | async-done | bytes 983072 | tf_op jit(solution)/shard_map/all_to_all | solution.py:341
  153.2 1.5 finish.1
  (33 shorter events, 0.1 us)
Async XLA Ops:
  0.6 24.1 %copy-start.4 = (bf16[1,192,768]{2,1,0:T(8,128)(2,1)S(1)}, bf16[1,192,768]{2,1,0:T(8,128)(2,1)}, u32[]{:S(2)}) copy-start(bf16[1,192,768]{2,1,0:T(8,128)(2,1)} %param.12) | copy-start | bytes 884740
  22.6 5.5 %copy-start.5 = (bf16[8,240,256]{2,1,0:T(8,128)(2,1)}, bf16[8,240,256]{2,1,0:T(8,128)(2,1)S(1)}, u32[]{:S(2)}) copy-start(bf16[8,240,256]{2,1,0:T(8,128)(2,1)S(1)} %all_to_all.20.own_ref) | copy-start | bytes 2949124
  22.7 5.5 %collective-permute-start = (bf16[8,240,256]{2,1,0:T(8,128)(2,1)S(1)}, bf16[8,240,256]{2,1,0:T(8,128)(2,1)S(1)}, u32[]{:S(2)}, u32[]{:S(2)}) collective-permute-start(bf16[8,240,256]{2,1,0:T(8,128)(2,1)S(1)} %all_to_all.20.own_ref), channel_id=1, source_target_pairs={{0,1},{1,0},{2,3},{3,2},{4,5},{5,4},{6,7},{7,6},{8,9},{9,8},{10,11... | collective-permute-start | bytes 2949128 | tf_op jit(solution)/shard_map/ppermute | solution.py:344
  24.8 19.2 %collective-permute-start.3 = (bf16[192,768]{1,0:T(8,128)(2,1)S(1)}, bf16[192,768]{1,0:T(8,128)(2,1)S(1)}, u32[]{:S(2)}, u32[]{:S(2)}) collective-permute-start(bf16[192,768]{1,0:T(8,128)(2,1)S(1)} %bitcast.12), channel_id=1, source_target_pairs={{0,4},{1,5},{2,6},{3,7},{4,8},{5,9},{6,10},{7,11},{8,12},{9,13},{1... | collective-permute-start | bytes 884744 | tf_op jit(solution)/shard_map/ppermute | solution.py:347
  25.0 19.0 %collective-permute-start.2 = (bf16[192,768]{1,0:T(8,128)(2,1)S(1)}, bf16[192,768]{1,0:T(8,128)(2,1)S(1)}, u32[]{:S(2)}, u32[]{:S(2)}) collective-permute-start(bf16[192,768]{1,0:T(8,128)(2,1)S(1)} %bitcast.13), channel_id=1, source_target_pairs={{0,8},{1,9},{2,10},{3,11},{4,12},{5,13},{6,14},{7,15},{8,0},{9,1},... | collective-permute-start | bytes 884744 | tf_op jit(solution)/shard_map/ppermute | solution.py:347
  26.9 17.1 %collective-permute-start.1 = (bf16[192,768]{1,0:T(8,128)(2,1)S(1)}, bf16[192,768]{1,0:T(8,128)(2,1)S(1)}, u32[]{:S(2)}, u32[]{:S(2)}) collective-permute-start(bf16[192,768]{1,0:T(8,128)(2,1)S(1)} %bitcast.14), channel_id=1, source_target_pairs={{0,12},{1,13},{2,14},{3,15},{4,0},{5,1},{6,2},{7,3},{8,4},{9,5},{1... | collective-permute-start | bytes 884744 | tf_op jit(solution)/shard_map/ppermute | solution.py:347
  28.2 0.9 copy-start.9
  44.0 3.8 %copy-start.7 = (bf16[192,768]{1,0:T(8,128)(2,1)}, bf16[192,768]{1,0:T(8,128)(2,1)S(1)}, u32[]{:S(2)}) copy-start(bf16[192,768]{1,0:T(8,128)(2,1)S(1)} %collective-permute-done.3.behind_ref.refs_7_) | copy-start | bytes 884740
  44.0 15.4 %copy-start.10 = (bf16[192,768]{1,0:T(8,128)(2,1)}, bf16[192,768]{1,0:T(8,128)(2,1)S(1)}, u32[]{:S(2)}) copy-start(bf16[192,768]{1,0:T(8,128)(2,1)S(1)} %collective-permute-done.2.refs_6_) | copy-start | bytes 884740
  44.0 3.8 %copy-start.8 = (bf16[192,768]{1,0:T(8,128)(2,1)}, bf16[192,768]{1,0:T(8,128)(2,1)S(1)}, u32[]{:S(2)}) copy-start(bf16[192,768]{1,0:T(8,128)(2,1)S(1)} %collective-permute-done.1.ahead_ref.refs_5_) | copy-start | bytes 884740
  44.0 15.3 %all-to-all-start.1 = ((bf16[8,144,256]{2,1,0:T(8,128)(2,1)}), bf16[8,144,256]{2,1,0:T(8,128)(2,1)S(1)}, u32[]{:S(2)}, u32[]{:S(2)}) async-start(bf16[8,144,256]{2,1,0:T(8,128)(2,1)} %get-tuple-element.69), calls=%async_computation.1 | async-start | bytes 1179648 | tf_op jit(solution)/shard_map/all_to_all | solution.py:341
  59.4 0.8 copy-start.3
  65.4 4.5 %collective-permute-start.4 = (bf16[192,192]{1,0:T(8,128)(2,1)}, bf16[192,192]{1,0:T(8,128)(2,1)S(1)}, u32[]{:S(2)}, u32[]{:S(2)}) collective-permute-start(bf16[192,192]{1,0:T(8,128)(2,1)} %get-tuple-element.78), channel_id=1, source_target_pairs={{0,12},{1,13},{2,14},{3,15},{4,0},{5,1},{6,2},{7,3},{8,4},{9,5},{1... | collective-permute-start | bytes 221192 | tf_op jit(solution)/shard_map/ppermute | solution.py:347
  67.9 5.3 %collective-permute-start.5 = (bf16[192,192]{1,0:T(8,128)(2,1)}, bf16[192,192]{1,0:T(8,128)(2,1)S(1)}, u32[]{:S(2)}, u32[]{:S(2)}) collective-permute-start(bf16[192,192]{1,0:T(8,128)(2,1)} %get-tuple-element.79), channel_id=1, source_target_pairs={{0,8},{1,9},{2,10},{3,11},{4,12},{5,13},{6,14},{7,15},{8,0},{9,1},... | collective-permute-start | bytes 221192 | tf_op jit(solution)/shard_map/ppermute | solution.py:347
  68.5 5.7 %collective-permute-start.6 = (bf16[192,192]{1,0:T(8,128)(2,1)}, bf16[192,192]{1,0:T(8,128)(2,1)S(1)}, u32[]{:S(2)}, u32[]{:S(2)}) collective-permute-start(bf16[192,192]{1,0:T(8,128)(2,1)} %get-tuple-element.80), channel_id=1, source_target_pairs={{0,4},{1,5},{2,6},{3,7},{4,8},{5,9},{6,10},{7,11},{8,12},{9,13},{1... | collective-permute-start | bytes 221192 | tf_op jit(solution)/shard_map/ppermute | solution.py:347
  69.9 7.8 %copy-start.11 = (bf16[192,192]{1,0:T(8,128)(2,1)}, bf16[192,192]{1,0:T(8,128)(2,1)S(1)}, u32[]{:S(2)}) copy-start(bf16[192,192]{1,0:T(8,128)(2,1)S(1)} %collective-permute-done.4.refs_1_) | copy-start | bytes 221188
  73.2 4.5 %copy-start.12 = (bf16[192,192]{1,0:T(8,128)(2,1)}, bf16[192,192]{1,0:T(8,128)(2,1)S(1)}, u32[]{:S(2)}) copy-start(bf16[192,192]{1,0:T(8,128)(2,1)S(1)} %collective-permute-done.5.refs_2_) | copy-start | bytes 221188
  74.2 3.6 %copy-start.13 = (bf16[192,192]{1,0:T(8,128)(2,1)}, bf16[192,192]{1,0:T(8,128)(2,1)S(1)}, u32[]{:S(2)}) copy-start(bf16[192,192]{1,0:T(8,128)(2,1)S(1)} %collective-permute-done.6.refs_3_) | copy-start | bytes 221188
  74.2 25.2 %all-to-all-start.2 = ((bf16[8,144,256]{2,1,0:T(8,128)(2,1)}), bf16[8,144,256]{2,1,0:T(8,128)(2,1)S(1)}, u32[]{:S(2)}, u32[]{:S(2)}) async-start(bf16[8,144,256]{2,1,0:T(8,128)(2,1)} %get-tuple-element.81), calls=%async_computation.2 | async-start | bytes 1179648 | tf_op jit(solution)/shard_map/all_to_all | solution.py:341
  81.1 4.6 %collective-permute-start.7 = (bf16[144,768]{1,0:T(8,128)(2,1)}, bf16[144,768]{1,0:T(8,128)(2,1)S(1)}, u32[]{:S(2)}, u32[]{:S(2)}) collective-permute-start(bf16[144,768]{1,0:T(8,128)(2,1)} %get-tuple-element.88), channel_id=1, source_target_pairs={{0,1},{1,0},{2,3},{3,2},{4,5},{5,4},{6,7},{7,6},{8,9},{9,8},{10,11... | collective-permute-start | bytes 663560 | tf_op jit(solution)/shard_map/ppermute | solution.py:344
  84.0 9.4 %collective-permute-start.8 = (bf16[144,768]{1,0:T(8,128)(2,1)}, bf16[144,768]{1,0:T(8,128)(2,1)S(1)}, u32[]{:S(2)}, u32[]{:S(2)}) collective-permute-start(bf16[144,768]{1,0:T(8,128)(2,1)} %get-tuple-element.89), channel_id=1, source_target_pairs={{0,2},{1,3},{2,0},{3,1},{4,6},{5,7},{6,4},{7,5},{8,10},{9,11},{10,... | collective-permute-start | bytes 663560 | tf_op jit(solution)/shard_map/ppermute | solution.py:344
  85.7 12.5 %collective-permute-start.9 = (bf16[144,768]{1,0:T(8,128)(2,1)}, bf16[144,768]{1,0:T(8,128)(2,1)S(1)}, u32[]{:S(2)}, u32[]{:S(2)}) collective-permute-start(bf16[144,768]{1,0:T(8,128)(2,1)} %get-tuple-element.90), channel_id=1, source_target_pairs={{0,3},{1,2},{2,1},{3,0},{4,7},{5,6},{6,5},{7,4},{8,11},{9,10},{10,... | collective-permute-start | bytes 663560 | tf_op jit(solution)/shard_map/ppermute | solution.py:344
  98.1 0.9 copy-start.1
  99.4 8.2 %copy-start.6 = (bf16[8,144,256]{2,1,0:T(8,128)(2,1)}, bf16[8,144,256]{2,1,0:T(8,128)(2,1)S(1)}, u32[]{:S(2)}) copy-start(bf16[8,144,256]{2,1,0:T(8,128)(2,1)S(1)} %all-to-all-done.2.recv_ref) | copy-start | bytes 1769476
  99.4 28.5 %collective-permute-start.10 = (bf16[192,144]{1,0:T(8,128)(2,1)S(1)}, bf16[192,144]{1,0:T(8,128)(2,1)S(1)}, u32[]{:S(2)}, u32[]{:S(2)}) collective-permute-start(bf16[192,144]{1,0:T(8,128)(2,1)S(1)} %get-tuple-element.98), channel_id=1, source_target_pairs={{0,64},{16,80},{32,96},{48,112},{64,0},{80,16},{96,32},{112,48},{1... | collective-permute-start | bytes 165896 | tf_op jit(solution)/shard_map/ppermute | solution.py:444
  102.5 25.4 %collective-permute-start.11 = (bf16[192,144]{1,0:T(8,128)(2,1)S(1)}, bf16[192,144]{1,0:T(8,128)(2,1)S(1)}, u32[]{:S(2)}, u32[]{:S(2)}) collective-permute-start(bf16[192,144]{1,0:T(8,128)(2,1)S(1)} %get-tuple-element.99), channel_id=1, source_target_pairs={{0,128},{16,144},{32,160},{48,176},{64,192},{80,208},{96,224},{112... | collective-permute-start | bytes 165896 | tf_op jit(solution)/shard_map/ppermute | solution.py:444
  107.6 20.3 %collective-permute-start.12 = (bf16[192,144]{1,0:T(8,128)(2,1)S(1)}, bf16[192,144]{1,0:T(8,128)(2,1)S(1)}, u32[]{:S(2)}, u32[]{:S(2)}) collective-permute-start(bf16[192,144]{1,0:T(8,128)(2,1)S(1)} %get-tuple-element.100), channel_id=1, source_target_pairs={{0,192},{16,208},{32,224},{48,240},{64,128},{80,144},{96,160},{112... | collective-permute-start | bytes 165896 | tf_op jit(solution)/shard_map/ppermute | solution.py:444
  127.9 3.2 %collective-permute-start.13 = (bf16[8,192,256]{2,1,0:T(8,128)(2,1)}, bf16[8,192,256]{2,1,0:T(8,128)(2,1)S(1)}, u32[]{:S(2)}, u32[]{:S(2)}) collective-permute-start(bf16[8,192,256]{2,1,0:T(8,128)(2,1)} %get-tuple-element.102), channel_id=1, source_target_pairs={{0,1},{1,0},{2,3},{3,2},{4,5},{5,4},{6,7},{7,6},{8,9},{9,8},{10,11... | collective-permute-start | bytes 2359304 | tf_op jit(solution)/shard_map/ppermute | solution.py:344
  131.1 1.1 copy-start
  132.2 0.9 copy-start.2
  134.3 18.9 %all-to-all-start.3 = ((bf16[8,240,256]{2,1,0:T(8,128)(2,1)}), bf16[8,240,256]{2,1,0:T(8,128)(2,1)S(1)}, u32[]{:S(2)}, u32[]{:S(2)}) async-start(bf16[8,240,256]{2,1,0:T(8,128)(2,1)} %add.1), calls=%async_computation.3 | async-start | bytes 1966080 | tf_op jit(solution)/shard_map/all_to_all | solution.py:341
  137.9 12.6 %collective-permute-start.14 = (bf16[48,144]{1,0:T(8,128)(2,1)S(1)}, bf16[48,144]{1,0:T(8,128)(2,1)S(1)}, u32[]{:S(2)}, u32[]{:S(2)}) collective-permute-start(bf16[48,144]{1,0:T(8,128)(2,1)S(1)} %get-tuple-element.118), channel_id=1, source_target_pairs={{0,16},{16,0},{32,48},{48,32},{64,80},{80,64},{96,112},{112,96},{1... | collective-permute-start | bytes 41480 | tf_op jit(solution)/shard_map/ppermute | solution.py:444
  140.6 9.9 %collective-permute-start.15 = (bf16[48,144]{1,0:T(8,128)(2,1)S(1)}, bf16[48,144]{1,0:T(8,128)(2,1)S(1)}, u32[]{:S(2)}, u32[]{:S(2)}) collective-permute-start(bf16[48,144]{1,0:T(8,128)(2,1)S(1)} %get-tuple-element.119), channel_id=1, source_target_pairs={{0,32},{16,48},{32,0},{48,16},{64,96},{80,112},{96,64},{112,80},{1... | collective-permute-start | bytes 41480 | tf_op jit(solution)/shard_map/ppermute | solution.py:444
  141.3 9.2 %collective-permute-start.16 = (bf16[48,144]{1,0:T(8,128)(2,1)S(1)}, bf16[48,144]{1,0:T(8,128)(2,1)S(1)}, u32[]{:S(2)}, u32[]{:S(2)}) collective-permute-start(bf16[48,144]{1,0:T(8,128)(2,1)S(1)} %get-tuple-element.120), channel_id=1, source_target_pairs={{0,48},{16,32},{32,16},{48,0},{64,112},{80,96},{96,80},{112,64},{1... | collective-permute-start | bytes 41480 | tf_op jit(solution)/shard_map/ppermute | solution.py:444

commit v2 on v1

--- a/solution.py
+++ b/solution.py
@@ -80,11 +80,12 @@
     ]
 
 
-def forward_body(own_ref, oth_ref, q_ref, att_ref, lse_ref, send_ref, score_ref):
-    block = score_ref.shape[0]
+def forward_body(own_ref, oth_ref, q_ref, att_ref, lse_ref, send_ref, *score_refs):
+    block = score_refs[0].shape[0]
     chips = own_ref.shape[0]
     rows = own_ref.shape[1] * 4 // 5
     mine = chips * rows
+    blocks = mine // block
     for c in range(chips):
         query = on_top(own_ref[c, rows:, :].astype(F32), 4)
         padded = jnp.concatenate([jnp.zeros((rows, VAL), F32), query], axis=1)
@@ -92,28 +93,30 @@
     tiles = key_tiles(own_ref, oth_ref)
     tile = 2 * mine // len(tiles)
 
-    def step(b, _):
-        at = pl.ds(pl.multiple_of(b * block, block), block)
-        query = q_ref[at, :]
-        top = None
-        for j, (_, _, _, part) in enumerate(tiles):
-            scores = rows_by_rows(query, part())
-            score_ref[:, j * tile : (j + 1) * tile] = scores
-            high = jnp.max(scores, axis=1, keepdims=True)
-            top = high if top is None else jnp.maximum(top, high)
+    def score(b, j, top):
+        scores = rows_by_rows(q_ref[b * block : (b + 1) * block, :], tiles[j][3]())
+        score_refs[b % 2][:, j * tile : (j + 1) * tile] = scores
+        high = jnp.max(scores, axis=1, keepdims=True)
+        return high if top is None else jnp.maximum(top, high)
+
+    top = None
+    for j in range(len(tiles)):
+        top = score(0, j, top)
+    for b in range(blocks):
+        following = None
         top = top * LOG2E
         total = jnp.zeros((block, 1), F32)
         summed = jnp.zeros((block, WIDE), F32)
         for j, (_, _, _, part) in enumerate(tiles):
-            expo = jnp.exp2(score_ref[:, j * tile : (j + 1) * tile] * LOG2E - top)
+            if b + 1 < blocks:
+                following = score(b + 1, j, following)
+            expo = jnp.exp2(score_refs[b % 2][:, j * tile : (j + 1) * tile] * LOG2E - top)
             total = total + jnp.sum(expo, axis=1, keepdims=True)
             summed = summed + plain(expo.astype(BF), part())
-        att_ref[at, :] = (summed * (1.0 / total)).astype(BF)
+        att_ref[b * block : (b + 1) * block, :] = (summed * (1.0 / total)).astype(BF)
         turned = jnp.transpose(jnp.broadcast_to(top + jnp.log2(total), (block, 128)))
         lse_ref[b] = turned[:8, :]
-        return 0
-
-    lax.fori_loop(0, mine // block, step, 0)
+        top = following
     for c in range(chips):
         part = att_ref[c * rows : (c + 1) * rows, :].astype(F32)
         for j in range(3):
@@ -184,60 +187,80 @@
         act_ref[...] = block
 
 
-def backward_body(
-    own_ref,
-    oth_ref,
-    q_ref,
-    kt_ref,
-    far_prob_ref,
-    att_ref,
-    recv_ref,
-    own_out_ref,
-    oth_out_ref,
-    dq_ref,
-    out_ref,
-    grad_ref,
-    turned_ref,
-    prob_ref,
-    sems,
-):
-    def arriving(j):
-        here = slice(j * tile, (j + 1) * tile)
-        return pltpu.make_async_copy(far_prob_ref.at[here], prob_ref.at[here], sems.at[j])
-
-    tiles = key_tiles(own_ref, oth_ref)
-    tile = prob_ref.shape[0] // len(tiles)
-    for j in range(len(tiles)):
-        arriving(j).start()
+def backward_body(*refs):
+    far_recv, far_att, far_own, far_prob, far_kt, far_q, far_oth = refs[:7]
+    far_own_out, far_oth_out, dq_ref = refs[7:10]
+    recv_ref, att_ref, own_ref, prob_ref, kt_ref, q_ref, oth_ref = refs[10:17]
+    own_out_ref, oth_out_ref, out_ref, grad_ref, turned_ref, sems = refs[17:]
     chips, rows, _ = own_out_ref.shape
     mine = chips * rows
     quarter = rows // 4
     block = 512
+    tiles = key_tiles(own_ref, oth_ref)
+    tile = 2 * mine // len(tiles)
+    heres = [slice(j * tile, (j + 1) * tile) for j in range(len(tiles))]
+    recv, att, own, kt, query, oth = [
+        pltpu.make_async_copy(far, near, sems.at[i])
+        for i, (far, near) in enumerate(
+            (
+                (far_recv, recv_ref),
+                (far_att, att_ref),
+                (far_own, own_ref),
+                (far_kt, kt_ref),
+                (far_q, q_ref),
+                (far_oth, oth_ref),
+            )
+        )
+    ]
+    probs = [
+        pltpu.make_async_copy(far_prob.at[here], prob_ref.at[here], sems.at[6 + j])
+        for j, here in enumerate(heres)
+    ]
+    leaving = []
+    for j, (side, first, step, _) in enumerate(tiles):
+        far, near = ((far_own_out, own_out_ref), (far_oth_out, oth_out_ref))[side]
+        at = slice(first, first + step)
+        leaving.append(pltpu.make_async_copy(near.at[at], far.at[at], sems.at[10 + j]))
+    for one in (recv, att, own, probs[0], query, kt, probs[1], oth, probs[2], probs[3]):
+        one.start()
+    recv.wait()
     for c in range(chips):
         pieces = [
             on_top(recv_ref[c, j * quarter : (j + 1) * quarter, :].astype(F32), 4) for j in range(3)
         ]
         padded = jnp.concatenate([*pieces, jnp.zeros((rows, KEY), F32)], axis=1)
         out_ref[c * rows : (c + 1) * rows, :] = padded.astype(BF)
+    att.wait()
     deltas = []
     for b in range(mine // block):
         at = slice(b * block, (b + 1) * block)
         each = out_ref[at, :].astype(F32) * att_ref[at, :].astype(F32)
         delta = jnp.sum(each, axis=1, keepdims=True)
         deltas.append(jnp.transpose(jnp.broadcast_to(delta, (block, 128)))[:1, :])
-    for j, (side, first, step, part) in enumerate(tiles):
-        here = slice(j * tile, (j + 1) * tile)
-        keys = part()
-        slot = grad_ref.at[j % 2]
-        arriving(j).wait()
+
+    def score_grads(j):
+        probs[j].wait()
+        keys = tiles[j][3]()
         for b, delta in enumerate(deltas):
             at = slice(b * block, (b + 1) * block)
             grads = rows_by_rows(keys, out_ref[at, :]) - delta
-            slot[:, at] = (prob_ref[here, at].astype(F32) * grads).astype(BF)
-        summed = plain(prob_ref[here, :], out_ref[...]) + plain(slot[...], q_ref[...])
-        to = (own_out_ref, oth_out_ref)[side]
-        to[first : first + step] = summed.astype(BF).reshape(step, rows, WIDE)
-        turned = plain(kt_ref[:, here], slot[...])
+            grad_ref[j % 2, :, at] = (prob_ref[heres[j], at].astype(F32) * grads).astype(BF)
+
+    own.wait()
+    score_grads(0)
+    query.wait()
+    kt.wait()
+    for j, (side, first, step, _) in enumerate(tiles):
+        if j + 1 < len(tiles):
+            if j + 1 == len(tiles) // 2:
+                oth.wait()
+            score_grads(j + 1)
+        slot = grad_ref[j % 2]
+        summed = plain(prob_ref[heres[j], :], out_ref[...]) + plain(slot, q_ref[...])
+        near = (own_out_ref, oth_out_ref)[side]
+        near[first : first + step] = summed.astype(BF).reshape(step, rows, WIDE)
+        leaving[j].start()
+        turned = plain(kt_ref[:, heres[j]], slot)
         turned_ref[...] = turned if j == 0 else turned_ref[...] + turned
     scale = 1.0 / math.sqrt(KEY)
     for b in range(mine // 384):
@@ -245,12 +268,13 @@
         for i in range(384 // rows):
             part = turned[i * rows : (i + 1) * rows, 64:]
             dq_ref[b * (384 // rows) + i] = side_by_side(part, 4).astype(BF)
+    for one in leaving:
+        one.wait()
 
 
 def weight_body(*refs):
     ring = 4
-    acts, cots, outs = refs[:ring], refs[ring : 2 * ring], refs[2 * ring : 3 * ring]
-    act_ref, cot_ref = refs[3 * ring :]
+    acts, cots, (out_ref, act_ref, cot_ref) = refs[:ring], refs[ring : 2 * ring], refs[2 * ring :]
     index = lax.axis_index("seq")
     stride = lax.axis_size("seq") // ring
     place, here = index // stride, index % stride
@@ -268,22 +292,15 @@
     )
     piece = share // 4
     parts = [
-        jnp.concatenate([t[g * piece : (g + 1) * piece] for t in terms], axis=0).astype(BF)
-        for g in range(4)
+        jnp.concatenate([t[g * piece : (g + 1) * piece] for t in terms], axis=0) for g in range(4)
     ]
+    order = []
     for r in range(4):
         part = parts[r]
         for g in range(1, 4):
             part = jnp.where(here == g, parts[g ^ r], part)
-        outs[r][...] = part
-
-
-def quarters(whole_ref, bit, outs):
-    size = whole_ref.shape[0] // 4
-    mine = lax.axis_index("dp") // bit % 4
-    for r, out_ref in enumerate(outs):
-        at = pl.ds(pl.multiple_of(jnp.bitwise_xor(mine, r) * size, size), size)
-        out_ref[...] = whole_ref[at, :].astype(out_ref.dtype)
+        order.append(part)
+    out_ref[...] = jnp.transpose(jnp.concatenate(order, axis=0)).astype(BF)
 
 
 def sum_of(refs):
@@ -293,14 +310,11 @@
     return both
 
 
-def first_sum_body(*refs):
-    refs[8][...] = jnp.transpose(sum_of(refs[:4]))
-    quarters(refs[8], 4, refs[4:8])
-
-
-def second_sum_body(*refs):
-    refs[8][...] = sum_of(refs[:4])
-    quarters(refs[8], 1, refs[4:8])
+def dp_sum_body(terms_ref, *outs):
+    both = sum_of([terms_ref.at[i] for i in range(terms_ref.shape[0])])
+    width = outs[0].shape[1]
+    for r, out_ref in enumerate(outs):
+        out_ref[...] = both[:, r * width : (r + 1) * width]
 
 
 def last_sum_body(*refs):
@@ -367,7 +381,7 @@
             shape(mine // block, 8, block, dtype=F32),
             shape(chips, 3 * quarter, WIDE),
         ],
-        [pltpu.VMEM((block, 2 * mine), F32)],
+        [pltpu.VMEM((block, 2 * mine), F32)] * 2,
         56,
         4 * pairs_done * WIDE,
         6 * MIB,
@@ -412,12 +426,11 @@
         2 * rows * channels,
         "middle",
     )(recv, out_proj, stream[0], cot, branch)
+    recv = exchange(send)
     moved = [round_ring(acts[ring - by], by * stride) for by in (1, 2, 3)]
-    send, *moved = lax.optimization_barrier((send, *moved))
-    recv = exchange(send)
-    parts = call(
+    terms = call(
         weight_body,
-        [shape(part, channels)] * 4,
+        [shape(channels, ring * part)],
         [
             pltpu.VMEM((ring * rows, channels // ring), BF),
             pltpu.VMEM((ring * rows, channels), BF),
@@ -428,51 +441,47 @@
         0,
         "weight",
     )(acts[0], *moved, cot, *cots)
-    def shared(parts, size, body, name):
-        return call(
-            body,
-            [shape(size, part, dtype=F32)] + [shape(size, part)] * 3,
-            [pltpu.VMEM((4 * size, part), F32)],
-            12,
-            0,
-            MIB,
-            0,
-            name,
-        )(*parts)
-
-    def dp_swap(value, bit):
-        return lax.ppermute(value, "dp", [(i, i ^ bit) for i in range(copies)])
-
-    given = [swap(parts[r], r) for r in (1, 2, 3)]
-    parts = shared([parts[0], *given], channels // 4, first_sum_body, "first_sum")
-    recv, *parts = lax.optimization_barrier((recv, *parts))
-    parts = [parts[0]] + [dp_swap(parts[r], 4 * r) for r in (1, 2, 3)]
+    recv, terms = lax.optimization_barrier((recv, terms))
+    terms = terms.reshape(copies, channels // copies, ring * part)
+    terms = lax.all_to_all(terms, "dp", 0, 0, tiled=True)
+    ins = (recv, attended, own, probs, keys_turned, query, oth)
     own_grad, oth_grad, dq = call(
         backward_body,
         [shape(chips, rows, WIDE), shape(chips, rows, WIDE), shape(chips, quarter, WIDE)],
         [
+            *[pltpu.VMEM(one.shape, one.dtype) for one in ins],
+            *[pltpu.VMEM((chips, rows, WIDE), BF)] * 2,
             pltpu.VMEM((mine, WIDE), BF),
             pltpu.VMEM((2, mine // 2, mine), BF),
             pltpu.VMEM((128, mine), F32),
-            pltpu.VMEM((2 * mine, mine), BF),
-            pltpu.SemaphoreType.DMA((4,)),
+            pltpu.SemaphoreType.DMA((14,)),
         ],
         56,
         8 * pairs_done * WIDE,
         16 * MIB,
         0,
         "backward",
-        far_in=(4,),
-    )(own, oth, query, keys_turned, probs, attended, recv)
-    *parts, oth_grad = lax.optimization_barrier((*parts, oth_grad))
+        far_in=range(7),
+        far_out=(0, 1),
+    )(*ins)
+    terms, oth_grad = lax.optimization_barrier((terms, oth_grad))
     swapped = swap(oth_grad)
-    parts = shared(parts, channels // copies, second_sum_body, "second_sum")
+    parts = call(
+        dp_sum_body,
+        [shape(channels // copies, part, dtype=F32)] * ring,
+        [],
+        12,
+        0,
+        MIB,
+        0,
+        "dp_sum",
+    )(terms)
     packed = call(add_body, [shape(chips, rows + quarter, WIDE)], [], 12, 0, 3 * MIB, 0, "add")(
         own_grad, swapped, dq
     )
+    parts = [parts[0]] + [swap(parts[r], r) for r in (1, 2, 3)]
     packed, *parts = lax.optimization_barrier((packed, *parts))
     recv = exchange(packed)
-    parts = [parts[0]] + [dp_swap(parts[r], r) for r in (1, 2, 3)]
     weight_grad = call(
         last_sum_body,
         [shape(3, channels // count, channels // copies, dtype=F32)],

time: 156 us -> 151 us (0.968)
  Pallas kernels: 61.6 us -> 53.3 us
  waiting for transfers between devices: 29.9 us -> 32.8 us
  starting transfers between devices: 38.1 us -> 40 us
    ppermute x5, waiting for transfers between devices: 14.5 us -> 0.01 us  [swap(): return lax.ppermute(value, 'seq', [(i, i ^ bit) for i in range(count)])]
    ppermute x6 -> x0, starting transfers between devices: 12.4 us -> none  [dp_swap(): return lax.ppermute(value, 'dp', [(i, i ^ bit) for i in range(copies)])]
    all_to_all x3, waiting for transfers between devices: 1.95 us -> 14 us  [exchange(): lax.all_to_all(value, 'seq', 0, 0, axis_index_groups=same_core, tiled=True)]
    all_to_all x0 -> x1, starting transfers between devices: none -> 10.6 us  [shards(): terms = lax.all_to_all(terms, 'dp', 0, 0, tiled=True)]
    ppermute x6 -> x0, waiting for transfers between devices: 8.41 us -> none  [dp_swap(): return lax.ppermute(value, 'dp', [(i, i ^ bit) for i in range(copies)])]
    pallas_call x12 -> x11, Pallas kernels: 61.6 us -> 53.3 us  [run(): pl.pallas_call(body, out_shape=outs, in_specs=[far if i in far_in else vm...]
    all_to_all x0 -> x1, waiting for transfers between devices: none -> 7.08 us  [shards(): terms = lax.all_to_all(terms, 'dp', 0, 0, tiled=True)]
    ppermute x6, waiting for transfers between devices: 5.09 us -> 11.7 us  [round_ring(): lax.ppermute(value, 'seq', [(i, (i - by) % count) for i in range(count)])]
  transfers between devices with their start and end apart: 20 -> 15, of which waited for: 8 -> 7; matrix products, arithmetic and copies ran while one was open for 0% -> 0% of each run, Pallas kernels for 33% -> 29%
where the time goes in v2:
time: 151 us
  Pallas kernels  53.3 us (35%)
  starting transfers between devices  40 us (26%)
  waiting for transfers between devices  32.8 us (22%)
  blocking collectives  19.4 us (13%)
  local copies, waits for them, and re-layouts  4.48 us (3%)
    pallas_call x11, Pallas kernels, run(): pl.pallas_call(body, out_shape=outs, in_specs=[far if i in far_in else vm...  53.3 us
    all_to_all x1, blocking collectives, exchange(): lax.all_to_all(value, 'seq', 0, 0, axis_index_groups=same_core, tiled=True)  19.4 us
    all_to_all x3, waiting for transfers between devices, exchange(): lax.all_to_all(value, 'seq', 0, 0, axis_index_groups=same_core, tiled=True)  14 us
    all_to_all x3, starting transfers between devices, exchange(): lax.all_to_all(value, 'seq', 0, 0, axis_index_groups=same_core, tiled=True)  13.2 us
    ppermute x6, waiting for transfers between devices, round_ring(): lax.ppermute(value, 'seq', [(i, (i - by) % count) for i in range(count)])  11.7 us
    all_to_all x1, starting transfers between devices, shards(): terms = lax.all_to_all(terms, 'dp', 0, 0, tiled=True)  10.6 us
    ppermute x5, starting transfers between devices, swap(): return lax.ppermute(value, 'seq', [(i, i ^ bit) for i in range(count)])  8.97 us
    ppermute x6, starting transfers between devices, round_ring(): lax.ppermute(value, 'seq', [(i, (i - by) % count) for i in range(count)])  7.23 us
  transfers between devices with their start and end apart: 15, of which 7 were waited for; matrix products, arithmetic and copies ran while one was open for 0% of the time, Pallas kernels for 29%

profile of v2, /device:TPU:1, one launch (start us, length us, event | category | flops | bytes accessed | tf_op | source)
XLA Modules:
  0.0 150.7 jit_solution(14264834177642398360)
XLA Ops:
  0.6 0.0 copy-start.2
  0.6 2.6 %pack.1 = bf16[8,240,256]{2,1,0:T(8,128)(2,1)} custom-call(bf16[192,512]{1,0:T(8,128)(2,1)} %bitcast.19, bf16[192,512]{1,0:T(8,128)(2,1)} %bitcast.20, bf16[192,1536]{1,0:T(8,128)(2,1)} %bitcast.17), custom_call_target="tpu_custom_call" | custom-call | bytes 2097152 | tf_op jit(solution)/shard_map/pack/pallas_call | solution.py:34
  3.2 19.4 %all_to_all.25.own_ref.refs_2_ = bf16[8,240,256]{2,1,0:T(8,128)(2,1)S(1)} all-to-all(bf16[8,240,256]{2,1,0:T(8,128)(2,1)} %pack.1), channel_id=1, replica_groups={{0,2,4,6,8,10,12,14},{1,3,5,7,9,11,13,15},{16,18,20,22,24,26,28,30},{17..., dimensions={0} | all-to-all | bytes 1966080 | tf_op jit(solution)/shard_map/all_to_all | solution.py:355
  22.6 2.1 %collective-permute-start = (bf16[8,240,256]{2,1,0:T(8,128)(2,1)S(1)}, bf16[8,240,256]{2,1,0:T(8,128)(2,1)S(1)}, u32[]{:S(2)}, u32[]{:S(2)}) collective-permute-start(bf16[8,240,256]{2,1,0:T(8,128)(2,1)S(1)} %all_to_all.25.own_ref.refs_2_), channel_id=1, source_target_pairs={{0,1},{1,0},{2,3},{3,2},{4,5},{5,4},{6,7},{7,6},{8,9},{9,8},{10,11... | collective-permute-start | bytes 2949128 | tf_op jit(solution)/shard_map/ppermute | solution.py:358
  24.8 0.2 collective-permute-start.3
  25.0 1.9 %collective-permute-start.2 = (bf16[192,768]{1,0:T(8,128)(2,1)S(1)}, bf16[192,768]{1,0:T(8,128)(2,1)S(1)}, u32[]{:S(2)}, u32[]{:S(2)}) collective-permute-start(bf16[192,768]{1,0:T(8,128)(2,1)S(1)} %bitcast.15), channel_id=1, source_target_pairs={{0,8},{1,9},{2,10},{3,11},{4,12},{5,13},{6,14},{7,15},{8,0},{9,1},... | collective-permute-start | bytes 884744 | tf_op jit(solution)/shard_map/ppermute | solution.py:361
  26.9 1.3 collective-permute-start.1
  28.2 0.0 collective-permute-done.oth_ref.refs_6_
  28.2 0.9 copy-done.12
  29.1 9.2 %forward.1 = (bf16[1536,256]{1,0:T(8,128)(2,1)}, bf16[1536,256]{1,0:T(8,128)(2,1)}, f32[3,8,512]{2,1,0:T(8,128)}, bf16[8,144,256]{2,1,0:T(8,128)(2,1)}) custom-call(bf16[8,240,256]{2,1,0:T(8,128)(2,1)} %copy-done.6, bf16[8,240,256]{2,1,0:T(8,128)(2,1)} %copy-done.12), custom_call_target="tpu_custom_call" | custom-call | flops 4831838208 | bytes 6291456 | tf_op jit(solution)/shard_map/forward/pallas_call | solution.py:34
  38.3 0.0 collective-permute-done.3.behind_ref.refs_7_
  38.3 2.0 %collective-permute-done.2.refs_6_ = bf16[192,768]{1,0:T(8,128)(2,1)S(1)} collective-permute-done((bf16[192,768]{1,0:T(8,128)(2,1)S(1)}, bf16[192,768]{1,0:T(8,128)(2,1)S(1)}, u32[]{:S(2)}, u32[]{:S(2)}) %collective-permute-start.2) | collective-permute-done | bytes 294944 | tf_op jit(solution)/shard_map/ppermute | solution.py:361
  40.4 0.8 collective-permute-done.1.ahead_ref.refs_5_
  41.2 4.4 %all-to-all-start.1 = ((bf16[8,144,256]{2,1,0:T(8,128)(2,1)}), bf16[8,144,256]{2,1,0:T(8,128)(2,1)S(1)}, u32[]{:S(2)}, u32[]{:S(2)}) async-start(bf16[8,144,256]{2,1,0:T(8,128)(2,1)} %get-tuple-element.48), calls=%async_computation.1 | async-start | bytes 1179648 | tf_op jit(solution)/shard_map/all_to_all | solution.py:355
  45.6 4.4 %branch.1.branch_ref = f32[192,768]{1,0:T(8,128)} custom-call(bf16[192,768]{1,0:T(8,128)(2,1)} %bitcast.11, bf16[192,768]{1,0:T(8,128)(2,1)} %copy-done.5, bf16[192,768]{1,0:T(8,128)(2,1)} %copy-done.4, bf16[3,768,768]{2,1,0:T(8,128)(2,1)} %conv_ref.1), custom_call_target="tpu_custom_call" | custom-call | flops 679477248 | bytes 5242880 | tf_op jit(solution)/shard_map/branch/pallas_call | solution.py:34
  50.1 7.1 %probs.1 = (bf16[3072,1536]{1,0:T(8,128)(2,1)}, bf16[128,3072]{1,0:T(8,128)(2,1)}) custom-call(bf16[8,240,256]{2,1,0:T(8,128)(2,1)} %copy-done.6, bf16[8,240,256]{2,1,0:T(8,128)(2,1)} %copy-done.12, bf16[1536,256]{1,0:T(8,128)(2,1)} %get-tuple-element.49.q_ref.refs_5_, f32[3,8,512]{2,1,0:T(8,128)} %get-tuple-element.50.lse_ref), custom_call_target="tpu_custom_call" | custom-call | flops 2415919104 | bytes 12582912 | tf_op jit(solution)/shard_map/probs/pallas_call | solution.py:34
  57.2 0.0 all-to-all-done.1.recv_ref
  57.2 0.0 copy-start.3
  57.3 0.8 copy-done.3
  58.1 5.2 %middle.1 = (bf16[192,768]{1,0:T(8,128)(2,1)}, bf16[8,144,256]{2,1,0:T(8,128)(2,1)}, bf16[192,192]{1,0:T(8,128)(2,1)}, bf16[192,192]{1,0:T(8,128)(2,1)}, bf16[19...) custom-call(bf16[8,144,256]{2,1,0:T(8,128)(2,1)} %copy-done.3, bf16[1536,768]{1,0:T(8,128)(2,1)} %proj_ref.1, ...), custom_call_target="tpu_custom_call" | custom-call | flops 905969664 | bytes 5242880 | tf_op jit(solution)/shard_map/middle/pallas_call | solution.py:34
  63.3 5.1 %all-to-all-start.2 = ((bf16[8,144,256]{2,1,0:T(8,128)(2,1)}), bf16[8,144,256]{2,1,0:T(8,128)(2,1)S(1)}, u32[]{:S(2)}, u32[]{:S(2)}) async-start(bf16[8,144,256]{2,1,0:T(8,128)(2,1)} %get-tuple-element.56), calls=%async_computation.2 | async-start | bytes 1179648 | tf_op jit(solution)/shard_map/all_to_all | solution.py:355
  68.4 2.7 %collective-permute-start.4 = (bf16[192,192]{1,0:T(8,128)(2,1)}, bf16[192,192]{1,0:T(8,128)(2,1)S(1)}, u32[]{:S(2)}, u32[]{:S(2)}) collective-permute-start(bf16[192,192]{1,0:T(8,128)(2,1)} %get-tuple-element.58), channel_id=1, source_target_pairs={{0,12},{1,13},{2,14},{3,15},{4,0},{5,1},{6,2},{7,3},{8,4},{9,5},{1... | collective-permute-start | bytes 221192 | tf_op jit(solution)/shard_map/ppermute | solution.py:361
  71.1 0.6 collective-permute-start.5
  71.6 0.6 collective-permute-start.6
  72.2 5.4 %collective-permute-done.4.refs_1_ = bf16[192,192]{1,0:T(8,128)(2,1)S(1)} collective-permute-done((bf16[192,192]{1,0:T(8,128)(2,1)}, bf16[192,192]{1,0:T(8,128)(2,1)S(1)}, u32[]{:S(2)}, u32[]{:S(2)}) %collective-permute-start.4) | collective-permute-done | bytes 73760 | tf_op jit(solution)/shard_map/ppermute | solution.py:361
  77.6 1.5 collective-permute-done.5.refs_2_
  79.1 2.0 %collective-permute-done.6.refs_3_ = bf16[192,192]{1,0:T(8,128)(2,1)S(1)} collective-permute-done((bf16[192,192]{1,0:T(8,128)(2,1)}, bf16[192,192]{1,0:T(8,128)(2,1)S(1)}, u32[]{:S(2)}, u32[]{:S(2)}) %collective-permute-start.6) | collective-permute-done | bytes 73760 | tf_op jit(solution)/shard_map/ppermute | solution.py:361
  81.1 0.6 copy-done.11
  81.7 3.7 %weight.1 = bf16[768,576]{1,0:T(8,128)(2,1)} custom-call(bf16[192,192]{1,0:T(8,128)(2,1)} %get-tuple-element.57.refs_0_, bf16[192,192]{1,0:T(8,128)(2,1)} %copy-done.9, bf16[192,192]{1,0:T(8,128)(2,1)} %copy-done.10, bf16[192,192]{1,0:T(8,128)(2,1)} %copy-done.11, bf16[192,768]{1,0:T(8,128)(2,1)} %bitcast.13, bf16[192,768]{1,0:T(8,128)(2,1)} %copy-done.5, ...), custom_call_target="tpu_custom_call" | custom-call | flops 679477248 | bytes 5242880 | tf_op jit(solution)/shard_map/weight/pallas_call | solution.py:34
  85.4 0.0 all-to-all-done.2.refs_0_
  85.4 10.6 %all-to-all-start.3 = ((bf16[16,48,576]{2,1,0:T(8,128)(2,1)}), bf16[16,48,576]{2,1,0:T(8,128)(2,1)S(1)}, u32[]{:S(2)}, u32[]{:S(2)}) async-start(bf16[16,48,576]{2,1,0:T(8,128)(2,1)} %bitcast.10), calls=%async_computation.3 | async-start | bytes 1966080 | tf_op jit(solution)/shard_map/all_to_all | solution.py:446
  96.1 17.5 %backward.1 = (bf16[8,192,256]{2,1,0:T(8,128)(2,1)}, bf16[8,192,256]{2,1,0:T(8,128)(2,1)}, bf16[8,48,256]{2,1,0:T(8,128)(2,1)}) custom-call(bf16[8,144,256]{2,1,0:T(8,128)(2,1)} %copy-done.7, bf16[1536,256]{1,0:T(8,128)(2,1)} %get-tuple-element.63.refs_1_, bf16[8,240,256]{2,1,0:T(8,128)(2,1)} %copy-done.6, bf16[3072,1536]{1,0:T(8,128)(2,1)} %get-tuple-element.64.refs_3_, ...), custom_call_target="tpu_custom_call" | custom-call | flops 9663676416 | bytes 16777216 | tf_op jit(solution)/shard_map/backward/pallas_call | solution.py:34
  113.6 7.1 %all-to-all-done.3.terms_ref = bf16[16,48,576]{2,1,0:T(8,128)(2,1)S(1)} async-done(((bf16[16,48,576]{2,1,0:T(8,128)(2,1)}), bf16[16,48,576]{2,1,0:T(8,128)(2,1)S(1)}, u32[]{:S(2)}, u32[]{:S(2)}) %all-to-all-start.3) | async-done | bytes 884768 | tf_op jit(solution)/shard_map/all_to_all | solution.py:446
  120.7 4.6 %collective-permute-start.7 = (bf16[8,192,256]{2,1,0:T(8,128)(2,1)}, bf16[8,192,256]{2,1,0:T(8,128)(2,1)S(1)}, u32[]{:S(2)}, u32[]{:S(2)}) collective-permute-start(bf16[8,192,256]{2,1,0:T(8,128)(2,1)} %get-tuple-element.69), channel_id=1, source_target_pairs={{0,1},{1,0},{2,3},{3,2},{4,5},{5,4},{6,7},{7,6},{8,9},{9,8},{10,11... | collective-permute-start | bytes 2359304 | tf_op jit(solution)/shard_map/ppermute | solution.py:358
  125.3 0.2 dp_sum.1
  125.5 0.1 collective-permute-start.8
  125.6 0.1 collective-permute-start.9
  125.7 2.0 %collective-permute-start.10 = (f32[48,144]{1,0:T(8,128)S(1)}, f32[48,144]{1,0:T(8,128)S(1)}, u32[]{:S(2)}, u32[]{:S(2)}) collective-permute-start(f32[48,144]{1,0:T(8,128)S(1)} %get-tuple-element.75), channel_id=1, source_target_pairs={{0,3},{1,2},{2,1},{3,0},{4,7},{5,6},{6,5},{7,4},{8,11},{9,10},{10,... | collective-permute-start | bytes 82952 | tf_op jit(solution)/shard_map/ppermute | solution.py:358
  127.7 0.0 collective-permute-done.7.recv_ref
  127.7 1.1 copy-done
  128.9 0.9 copy-done.1
  129.8 1.1 add.1
  130.9 0.0 collective-permute-done.8.refs_1_
  130.9 0.0 collective-permute-done.9.refs_2_
  131.0 3.6 %all-to-all-start.4 = ((bf16[8,240,256]{2,1,0:T(8,128)(2,1)}), bf16[8,240,256]{2,1,0:T(8,128)(2,1)S(1)}, u32[]{:S(2)}, u32[]{:S(2)}) async-start(bf16[8,240,256]{2,1,0:T(8,128)(2,1)} %add.1), calls=%async_computation.4 | async-start | bytes 1966080 | tf_op jit(solution)/shard_map/all_to_all | solution.py:355
  134.6 0.7 last_sum.1
  135.3 14.0 %all-to-all-done.4.recv_ref = bf16[8,240,256]{2,1,0:T(8,128)(2,1)S(1)} async-done(((bf16[8,240,256]{2,1,0:T(8,128)(2,1)}), bf16[8,240,256]{2,1,0:T(8,128)(2,1)S(1)}, u32[]{:S(2)}, u32[]{:S(2)}) %all-to-all-start.4) | async-done | bytes 983072 | tf_op jit(solution)/shard_map/all_to_all | solution.py:355
  149.2 1.5 finish.1
  (20 shorter events, 0.0 us)
Async XLA Ops:
  0.6 24.1 %copy-start.2 = (bf16[1,192,768]{2,1,0:T(8,128)(2,1)S(1)}, bf16[1,192,768]{2,1,0:T(8,128)(2,1)}, u32[]{:S(2)}) copy-start(bf16[1,192,768]{2,1,0:T(8,128)(2,1)} %param.12) | copy-start | bytes 884740
  22.6 5.5 %copy-start.6 = (bf16[8,240,256]{2,1,0:T(8,128)(2,1)}, bf16[8,240,256]{2,1,0:T(8,128)(2,1)S(1)}, u32[]{:S(2)}) copy-start(bf16[8,240,256]{2,1,0:T(8,128)(2,1)S(1)} %all_to_all.25.own_ref.refs_2_) | copy-start | bytes 2949124
  22.6 5.5 %collective-permute-start = (bf16[8,240,256]{2,1,0:T(8,128)(2,1)S(1)}, bf16[8,240,256]{2,1,0:T(8,128)(2,1)S(1)}, u32[]{:S(2)}, u32[]{:S(2)}) collective-permute-start(bf16[8,240,256]{2,1,0:T(8,128)(2,1)S(1)} %all_to_all.25.own_ref.refs_2_), channel_id=1, source_target_pairs={{0,1},{1,0},{2,3},{3,2},{4,5},{5,4},{6,7},{7,6},{8,9},{9,8},{10,11... | collective-permute-start | bytes 2949128 | tf_op jit(solution)/shard_map/ppermute | solution.py:358
  24.8 13.6 %collective-permute-start.3 = (bf16[192,768]{1,0:T(8,128)(2,1)S(1)}, bf16[192,768]{1,0:T(8,128)(2,1)S(1)}, u32[]{:S(2)}, u32[]{:S(2)}) collective-permute-start(bf16[192,768]{1,0:T(8,128)(2,1)S(1)} %bitcast.14), channel_id=1, source_target_pairs={{0,4},{1,5},{2,6},{3,7},{4,8},{5,9},{6,10},{7,11},{8,12},{9,13},{1... | collective-permute-start | bytes 884744 | tf_op jit(solution)/shard_map/ppermute | solution.py:361
  25.0 15.4 %collective-permute-start.2 = (bf16[192,768]{1,0:T(8,128)(2,1)S(1)}, bf16[192,768]{1,0:T(8,128)(2,1)S(1)}, u32[]{:S(2)}, u32[]{:S(2)}) collective-permute-start(bf16[192,768]{1,0:T(8,128)(2,1)S(1)} %bitcast.15), channel_id=1, source_target_pairs={{0,8},{1,9},{2,10},{3,11},{4,12},{5,13},{6,14},{7,15},{8,0},{9,1},... | collective-permute-start | bytes 884744 | tf_op jit(solution)/shard_map/ppermute | solution.py:361
  26.9 14.3 %collective-permute-start.1 = (bf16[192,768]{1,0:T(8,128)(2,1)S(1)}, bf16[192,768]{1,0:T(8,128)(2,1)S(1)}, u32[]{:S(2)}, u32[]{:S(2)}) collective-permute-start(bf16[192,768]{1,0:T(8,128)(2,1)S(1)} %bitcast.16), channel_id=1, source_target_pairs={{0,12},{1,13},{2,14},{3,15},{4,0},{5,1},{6,2},{7,3},{8,4},{9,5},{1... | collective-permute-start | bytes 884744 | tf_op jit(solution)/shard_map/ppermute | solution.py:361
  28.2 0.9 copy-start.12
  38.3 7.3 %copy-start.4 = (bf16[192,768]{1,0:T(8,128)(2,1)}, bf16[192,768]{1,0:T(8,128)(2,1)S(1)}, u32[]{:S(2)}) copy-start(bf16[192,768]{1,0:T(8,128)(2,1)S(1)} %collective-permute-done.3.behind_ref.refs_7_) | copy-start | bytes 884740
  40.4 16.9 %copy-start.8 = (bf16[192,768]{1,0:T(8,128)(2,1)}, bf16[192,768]{1,0:T(8,128)(2,1)S(1)}, u32[]{:S(2)}) copy-start(bf16[192,768]{1,0:T(8,128)(2,1)S(1)} %collective-permute-done.2.refs_6_) | copy-start | bytes 884740
  41.2 4.5 %copy-start.5 = (bf16[192,768]{1,0:T(8,128)(2,1)}, bf16[192,768]{1,0:T(8,128)(2,1)S(1)}, u32[]{:S(2)}) copy-start(bf16[192,768]{1,0:T(8,128)(2,1)S(1)} %collective-permute-done.1.ahead_ref.refs_5_) | copy-start | bytes 884740
  41.2 16.1 %all-to-all-start.1 = ((bf16[8,144,256]{2,1,0:T(8,128)(2,1)}), bf16[8,144,256]{2,1,0:T(8,128)(2,1)S(1)}, u32[]{:S(2)}, u32[]{:S(2)}) async-start(bf16[8,144,256]{2,1,0:T(8,128)(2,1)} %get-tuple-element.48), calls=%async_computation.1 | async-start | bytes 1179648 | tf_op jit(solution)/shard_map/all_to_all | solution.py:355
  57.2 0.8 copy-start.3
  63.3 22.1 %all-to-all-start.2 = ((bf16[8,144,256]{2,1,0:T(8,128)(2,1)}), bf16[8,144,256]{2,1,0:T(8,128)(2,1)S(1)}, u32[]{:S(2)}, u32[]{:S(2)}) async-start(bf16[8,144,256]{2,1,0:T(8,128)(2,1)} %get-tuple-element.56), calls=%async_computation.2 | async-start | bytes 1179648 | tf_op jit(solution)/shard_map/all_to_all | solution.py:355
  68.4 9.2 %collective-permute-start.4 = (bf16[192,192]{1,0:T(8,128)(2,1)}, bf16[192,192]{1,0:T(8,128)(2,1)S(1)}, u32[]{:S(2)}, u32[]{:S(2)}) collective-permute-start(bf16[192,192]{1,0:T(8,128)(2,1)} %get-tuple-element.58), channel_id=1, source_target_pairs={{0,12},{1,13},{2,14},{3,15},{4,0},{5,1},{6,2},{7,3},{8,4},{9,5},{1... | collective-permute-start | bytes 221192 | tf_op jit(solution)/shard_map/ppermute | solution.py:361
  71.1 8.1 %collective-permute-start.5 = (bf16[192,192]{1,0:T(8,128)(2,1)}, bf16[192,192]{1,0:T(8,128)(2,1)S(1)}, u32[]{:S(2)}, u32[]{:S(2)}) collective-permute-start(bf16[192,192]{1,0:T(8,128)(2,1)} %get-tuple-element.59), channel_id=1, source_target_pairs={{0,8},{1,9},{2,10},{3,11},{4,12},{5,13},{6,14},{7,15},{8,0},{9,1},... | collective-permute-start | bytes 221192 | tf_op jit(solution)/shard_map/ppermute | solution.py:361
  71.6 9.4 %collective-permute-start.6 = (bf16[192,192]{1,0:T(8,128)(2,1)}, bf16[192,192]{1,0:T(8,128)(2,1)S(1)}, u32[]{:S(2)}, u32[]{:S(2)}) collective-permute-start(bf16[192,192]{1,0:T(8,128)(2,1)} %get-tuple-element.60), channel_id=1, source_target_pairs={{0,4},{1,5},{2,6},{3,7},{4,8},{5,9},{6,10},{7,11},{8,12},{9,13},{1... | collective-permute-start | bytes 221192 | tf_op jit(solution)/shard_map/ppermute | solution.py:361
  77.6 3.5 %copy-start.9 = (bf16[192,192]{1,0:T(8,128)(2,1)}, bf16[192,192]{1,0:T(8,128)(2,1)S(1)}, u32[]{:S(2)}) copy-start(bf16[192,192]{1,0:T(8,128)(2,1)S(1)} %collective-permute-done.4.refs_1_) | copy-start | bytes 221188
  79.1 2.0 %copy-start.10 = (bf16[192,192]{1,0:T(8,128)(2,1)}, bf16[192,192]{1,0:T(8,128)(2,1)S(1)}, u32[]{:S(2)}) copy-start(bf16[192,192]{1,0:T(8,128)(2,1)S(1)} %collective-permute-done.5.refs_2_) | copy-start | bytes 221188
  81.1 0.6 copy-start.11
  85.4 10.7 %copy-start.7 = (bf16[8,144,256]{2,1,0:T(8,128)(2,1)}, bf16[8,144,256]{2,1,0:T(8,128)(2,1)S(1)}, u32[]{:S(2)}) copy-start(bf16[8,144,256]{2,1,0:T(8,128)(2,1)S(1)} %all-to-all-done.2.refs_0_) | copy-start | bytes 1769476
  85.4 35.3 %all-to-all-start.3 = ((bf16[16,48,576]{2,1,0:T(8,128)(2,1)}), bf16[16,48,576]{2,1,0:T(8,128)(2,1)S(1)}, u32[]{:S(2)}, u32[]{:S(2)}) async-start(bf16[16,48,576]{2,1,0:T(8,128)(2,1)} %bitcast.10), calls=%async_computation.3 | async-start | bytes 1966080 | tf_op jit(solution)/shard_map/all_to_all | solution.py:446
  120.7 7.1 %collective-permute-start.7 = (bf16[8,192,256]{2,1,0:T(8,128)(2,1)}, bf16[8,192,256]{2,1,0:T(8,128)(2,1)S(1)}, u32[]{:S(2)}, u32[]{:S(2)}) collective-permute-start(bf16[8,192,256]{2,1,0:T(8,128)(2,1)} %get-tuple-element.69), channel_id=1, source_target_pairs={{0,1},{1,0},{2,3},{3,2},{4,5},{5,4},{6,7},{7,6},{8,9},{9,8},{10,11... | collective-permute-start | bytes 2359304 | tf_op jit(solution)/shard_map/ppermute | solution.py:358
  125.5 5.4 %collective-permute-start.8 = (f32[48,144]{1,0:T(8,128)S(1)}, f32[48,144]{1,0:T(8,128)S(1)}, u32[]{:S(2)}, u32[]{:S(2)}) collective-permute-start(f32[48,144]{1,0:T(8,128)S(1)} %get-tuple-element.73), channel_id=1, source_target_pairs={{0,1},{1,0},{2,3},{3,2},{4,5},{5,4},{6,7},{7,6},{8,9},{9,8},{10,11... | collective-permute-start | bytes 82952 | tf_op jit(solution)/shard_map/ppermute | solution.py:358
  125.6 5.3 %collective-permute-start.9 = (f32[48,144]{1,0:T(8,128)S(1)}, f32[48,144]{1,0:T(8,128)S(1)}, u32[]{:S(2)}, u32[]{:S(2)}) collective-permute-start(f32[48,144]{1,0:T(8,128)S(1)} %get-tuple-element.74), channel_id=1, source_target_pairs={{0,2},{1,3},{2,0},{3,1},{4,6},{5,7},{6,4},{7,5},{8,10},{9,11},{10,... | collective-permute-start | bytes 82952 | tf_op jit(solution)/shard_map/ppermute | solution.py:358
  125.7 5.2 %collective-permute-start.10 = (f32[48,144]{1,0:T(8,128)S(1)}, f32[48,144]{1,0:T(8,128)S(1)}, u32[]{:S(2)}, u32[]{:S(2)}) collective-permute-start(f32[48,144]{1,0:T(8,128)S(1)} %get-tuple-element.75), channel_id=1, source_target_pairs={{0,3},{1,2},{2,1},{3,0},{4,7},{5,6},{6,5},{7,4},{8,11},{9,10},{10,... | collective-permute-start | bytes 82952 | tf_op jit(solution)/shard_map/ppermute | solution.py:358
  127.7 1.1 copy-start
  128.9 0.9 copy-start.1
  131.0 18.3 %all-to-all-start.4 = ((bf16[8,240,256]{2,1,0:T(8,128)(2,1)}), bf16[8,240,256]{2,1,0:T(8,128)(2,1)S(1)}, u32[]{:S(2)}, u32[]{:S(2)}) async-start(bf16[8,240,256]{2,1,0:T(8,128)(2,1)} %add.1), calls=%async_computation.4 | async-start | bytes 1966080 | tf_op jit(solution)/shard_map/all_to_all | solution.py:355

commit v3 on v2

--- a/solution.py
+++ b/solution.py
@@ -158,16 +158,28 @@
     return (wide * normal_cdf, normal_cdf + wide * density)
 
 
-def middle_body(recv_ref, proj_ref, stream_ref, cot_ref, branch_ref, grad_ref, send_ref, *rest):
-    *acts, att_ref = rest
+def middle_body(*refs):
+    fars, (grad_ref, send_ref, *acts) = refs[:5], refs[5:11]
+    recv_ref, proj_ref, stream_ref, cot_ref, branch_ref, att_ref, sems = refs[11:]
+    arriving = [
+        pltpu.make_async_copy(far, near, sems.at[i])
+        for i, (far, near) in enumerate(
+            zip(fars, (recv_ref, proj_ref, stream_ref, cot_ref, branch_ref))
+        )
+    ]
+    for one in arriving:
+        one.start()
     ring = len(acts)
     place = lax.axis_index("seq") // (lax.axis_size("seq") // ring)
     quarter = recv_ref.shape[1] // 3
+    arriving[0].wait()
     for h in range(HEADS):
         for j in range(3):
             piece = recv_ref[h, j * quarter : (j + 1) * quarter, :].astype(F32)
             at = h * VAL + j * 64
             att_ref[:, at : at + 64] = on_top(piece, 4).astype(BF)
+    for one in arriving[1:]:
+        one.wait()
     inside = stream_ref[...].astype(F32) + plain(att_ref[...], proj_ref[...])
     activated, slope = gelu_pieces(inside.astype(BF).astype(F32))
     grad = (cot_ref[...].astype(F32) + slope * branch_ref[...]).astype(BF)
@@ -189,10 +201,10 @@
 
 def backward_body(*refs):
     far_recv, far_att, far_own, far_prob, far_kt, far_q, far_oth = refs[:7]
-    far_own_out, far_oth_out, dq_ref = refs[7:10]
-    recv_ref, att_ref, own_ref, prob_ref, kt_ref, q_ref, oth_ref = refs[10:17]
-    own_out_ref, oth_out_ref, out_ref, grad_ref, turned_ref, sems = refs[17:]
-    chips, rows, _ = own_out_ref.shape
+    far_own_out, far_oth_out = refs[7:9]
+    recv_ref, att_ref, own_ref, prob_ref, kt_ref, q_ref, oth_ref = refs[9:16]
+    own_out_ref, oth_out_ref, out_ref, grad_ref, turned_ref, sems = refs[16:]
+    chips, rows, _ = oth_out_ref.shape
     mine = chips * rows
     quarter = rows // 4
     block = 512
@@ -218,10 +230,14 @@
     ]
     leaving = []
     for j, (side, first, step, _) in enumerate(tiles):
-        far, near = ((far_own_out, own_out_ref), (far_oth_out, oth_out_ref))[side]
-        at = slice(first, first + step)
-        leaving.append(pltpu.make_async_copy(near.at[at], far.at[at], sems.at[10 + j]))
-    for one in (recv, att, own, probs[0], query, kt, probs[1], oth, probs[2], probs[3]):
+        if side == 1:
+            at = slice(first, first + step)
+            leaving.append(
+                pltpu.make_async_copy(oth_out_ref.at[at], far_oth_out.at[at], sems.at[8 + j])
+            )
+    leaving.append(pltpu.make_async_copy(own_out_ref, far_own_out, sems.at[12]))
+    order = [2, 3, 0, 1]
+    for one in (recv, att, oth, probs[2], query, kt, probs[3], own, probs[0], probs[1]):
         one.start()
     recv.wait()
     for c in range(chips):
@@ -246,28 +262,31 @@
             grads = rows_by_rows(keys, out_ref[at, :]) - delta
             grad_ref[j % 2, :, at] = (prob_ref[heres[j], at].astype(F32) * grads).astype(BF)
 
-    own.wait()
-    score_grads(0)
+    oth.wait()
+    score_grads(order[0])
     query.wait()
     kt.wait()
-    for j, (side, first, step, _) in enumerate(tiles):
-        if j + 1 < len(tiles):
-            if j + 1 == len(tiles) // 2:
-                oth.wait()
-            score_grads(j + 1)
+    for i, j in enumerate(order):
+        side, first, step, _ = tiles[j]
+        if i + 1 < len(order):
+            if i + 1 == len(order) // 2:
+                own.wait()
+            score_grads(order[i + 1])
         slot = grad_ref[j % 2]
         summed = plain(prob_ref[heres[j], :], out_ref[...]) + plain(slot, q_ref[...])
         near = (own_out_ref, oth_out_ref)[side]
-        near[first : first + step] = summed.astype(BF).reshape(step, rows, WIDE)
-        leaving[j].start()
+        near[first : first + step, :rows, :] = summed.astype(BF).reshape(step, rows, WIDE)
+        if side == 1:
+            leaving[i].start()
         turned = plain(kt_ref[:, heres[j]], slot)
-        turned_ref[...] = turned if j == 0 else turned_ref[...] + turned
+        turned_ref[...] = turned if i == 0 else turned_ref[...] + turned
     scale = 1.0 / math.sqrt(KEY)
     for b in range(mine // 384):
         turned = jnp.transpose(turned_ref[:, b * 384 : (b + 1) * 384]) * scale
         for i in range(384 // rows):
             part = turned[i * rows : (i + 1) * rows, 64:]
-            dq_ref[b * (384 // rows) + i] = side_by_side(part, 4).astype(BF)
+            own_out_ref[b * (384 // rows) + i, rows:, :] = side_by_side(part, 4).astype(BF)
+    leaving[-1].start()
     for one in leaving:
         one.wait()
 
@@ -324,11 +343,12 @@
         refs[4][t] = both[t * rows : (t + 1) * rows]
 
 
-def add_body(own_ref, recv_ref, dq_ref, out_ref):
-    rows = own_ref.shape[1]
+def add_body(own_ref, recv_ref, out_ref):
+    rows = recv_ref.shape[1]
     for c in range(own_ref.shape[0]):
-        out_ref[c, :rows, :] = (own_ref[c].astype(F32) + recv_ref[c].astype(F32)).astype(BF)
-        out_ref[c, rows:, :] = dq_ref[c]
+        both = own_ref[c, :rows, :].astype(F32) + recv_ref[c].astype(F32)
+        out_ref[c, :rows, :] = both.astype(BF)
+        out_ref[c, rows:, :] = own_ref[c, rows:, :]
 
 
 def finish_body(recv_ref, q_ref, k_ref, v_ref):
@@ -412,6 +432,7 @@
         "branch",
     )(cot, cots[0], cots[2], conv_weight)
     recv, probs, branch = lax.optimization_barrier((recv, probs, branch))
+    ins = (recv, out_proj, stream[0], cot, branch)
     stream_grad, send, *acts = call(
         middle_body,
         [
@@ -419,13 +440,18 @@
             shape(chips, 3 * quarter, WIDE),
             *[shape(rows, channels // ring)] * ring,
         ],
-        [pltpu.VMEM((rows, HEADS * VAL), BF)],
+        [
+            *[pltpu.VMEM(one.shape, one.dtype) for one in ins],
+            pltpu.VMEM((rows, HEADS * VAL), BF),
+            pltpu.SemaphoreType.DMA((5,)),
+        ],
         56,
         4 * rows * channels * HEADS * VAL,
         5 * MIB,
         2 * rows * channels,
         "middle",
-    )(recv, out_proj, stream[0], cot, branch)
+        far_in=range(5),
+    )(*ins)
     recv = exchange(send)
     moved = [round_ring(acts[ring - by], by * stride) for by in (1, 2, 3)]
     terms = call(
@@ -445,16 +471,17 @@
     terms = terms.reshape(copies, channels // copies, ring * part)
     terms = lax.all_to_all(terms, "dp", 0, 0, tiled=True)
     ins = (recv, attended, own, probs, keys_turned, query, oth)
-    own_grad, oth_grad, dq = call(
+    own_grad, oth_grad = call(
         backward_body,
-        [shape(chips, rows, WIDE), shape(chips, rows, WIDE), shape(chips, quarter, WIDE)],
+        [shape(chips, rows + quarter, WIDE), shape(chips, rows, WIDE)],
         [
             *[pltpu.VMEM(one.shape, one.dtype) for one in ins],
-            *[pltpu.VMEM((chips, rows, WIDE), BF)] * 2,
+            pltpu.VMEM((chips, rows + quarter, WIDE), BF),
+            pltpu.VMEM((chips, rows, WIDE), BF),
             pltpu.VMEM((mine, WIDE), BF),
             pltpu.VMEM((2, mine // 2, mine), BF),
             pltpu.VMEM((128, mine), F32),
-            pltpu.SemaphoreType.DMA((14,)),
+            pltpu.SemaphoreType.DMA((13,)),
         ],
         56,
         8 * pairs_done * WIDE,
@@ -464,8 +491,12 @@
         far_in=range(7),
         far_out=(0, 1),
     )(*ins)
-    terms, oth_grad = lax.optimization_barrier((terms, oth_grad))
     swapped = swap(oth_grad)
+    packed = call(add_body, [shape(chips, rows + quarter, WIDE)], [], 12, 0, 3 * MIB, 0, "add")(
+        own_grad, swapped
+    )
+    packed, terms = lax.optimization_barrier((packed, terms))
+    recv = exchange(packed)
     parts = call(
         dp_sum_body,
         [shape(channels // copies, part, dtype=F32)] * ring,
@@ -476,12 +507,7 @@
         0,
         "dp_sum",
     )(terms)
-    packed = call(add_body, [shape(chips, rows + quarter, WIDE)], [], 12, 0, 3 * MIB, 0, "add")(
-        own_grad, swapped, dq
-    )
     parts = [parts[0]] + [swap(parts[r], r) for r in (1, 2, 3)]
-    packed, *parts = lax.optimization_barrier((packed, *parts))
-    recv = exchange(packed)
     weight_grad = call(
         last_sum_body,
         [shape(3, channels // count, channels // copies, dtype=F32)],

time: 151 us -> 143 us (0.947)
  waiting for transfers between devices: 32.8 us -> 23.7 us
  starting transfers between devices: 40 us -> 42.8 us
    all_to_all x3, waiting for transfers between devices: 14 us -> 0.01 us  [exchange(): lax.all_to_all(value, 'seq', 0, 0, axis_index_groups=same_core, tiled=True)]
    ppermute x5, waiting for transfers between devices: 0.01 us -> 11.9 us  [swap(): return lax.ppermute(value, 'seq', [(i, i ^ bit) for i in range(count)])]
    all_to_all x1, waiting for transfers between devices: 7.08 us -> 0.05 us  [shards(): terms = lax.all_to_all(terms, 'dp', 0, 0, tiled=True)]
    ppermute x5, starting transfers between devices: 8.97 us -> 11.6 us  [swap(): return lax.ppermute(value, 'seq', [(i, i ^ bit) for i in range(count)])]
    unnamed x26 -> x24, local copies, waits for them, and re-layouts: 4.48 us -> 3.63 us
  transfers between devices with their start and end apart: 15 -> 15, of which waited for: 7 -> 9; matrix products, arithmetic and copies ran while one was open for 0% -> 0% of each run, Pallas kernels for 29% -> 30%
where the time goes in v3:
time: 143 us
  Pallas kernels  52.5 us (37%)
  starting transfers between devices  42.8 us (30%)
  waiting for transfers between devices  23.7 us (17%)
  blocking collectives  19.4 us (14%)
  local copies, waits for them, and re-layouts  3.63 us (3%)
    pallas_call x11, Pallas kernels, run(): pl.pallas_call(body, out_shape=outs, in_specs=[far if i in far_in else vm...  52.5 us
    all_to_all x1, blocking collectives, exchange(): lax.all_to_all(value, 'seq', 0, 0, axis_index_groups=same_core, tiled=True)  19.4 us
    all_to_all x3, starting transfers between devices, exchange(): lax.all_to_all(value, 'seq', 0, 0, axis_index_groups=same_core, tiled=True)  13.3 us
    ppermute x5, waiting for transfers between devices, swap(): return lax.ppermute(value, 'seq', [(i, i ^ bit) for i in range(count)])  11.9 us
    ppermute x6, waiting for transfers between devices, round_ring(): lax.ppermute(value, 'seq', [(i, (i - by) % count) for i in range(count)])  11.7 us
    ppermute x5, starting transfers between devices, swap(): return lax.ppermute(value, 'seq', [(i, i ^ bit) for i in range(count)])  11.6 us
    all_to_all x1, starting transfers between devices, shards(): terms = lax.all_to_all(terms, 'dp', 0, 0, tiled=True)  10.7 us
    ppermute x6, starting transfers between devices, round_ring(): lax.ppermute(value, 'seq', [(i, (i - by) % count) for i in range(count)])  7.23 us
  transfers between devices with their start and end apart: 15, of which 9 were waited for; matrix products, arithmetic and copies ran while one was open for 0% of the time, Pallas kernels for 30%

profile of v3, /device:TPU:1, one launch (start us, length us, event | category | flops | bytes accessed | tf_op | source)
XLA Modules:
  0.0 142.8 jit_solution(1731047533035758194)
XLA Ops:
  0.6 0.0 copy-start.1
  0.6 2.6 %pack.1 = bf16[8,240,256]{2,1,0:T(8,128)(2,1)} custom-call(bf16[192,512]{1,0:T(8,128)(2,1)} %bitcast.19, bf16[192,512]{1,0:T(8,128)(2,1)} %bitcast.20, bf16[192,1536]{1,0:T(8,128)(2,1)} %bitcast.17), custom_call_target="tpu_custom_call" | custom-call | bytes 2097152 | tf_op jit(solution)/shard_map/pack/pallas_call | solution.py:34
  3.2 19.4 %all_to_all.25.own_ref.refs_2_ = bf16[8,240,256]{2,1,0:T(8,128)(2,1)S(1)} all-to-all(bf16[8,240,256]{2,1,0:T(8,128)(2,1)} %pack.1), channel_id=1, replica_groups={{0,2,4,6,8,10,12,14},{1,3,5,7,9,11,13,15},{16,18,20,22,24,26,28,30},{17..., dimensions={0} | all-to-all | bytes 1966080 | tf_op jit(solution)/shard_map/all_to_all | solution.py:375
  22.7 2.1 %collective-permute-start = (bf16[8,240,256]{2,1,0:T(8,128)(2,1)S(1)}, bf16[8,240,256]{2,1,0:T(8,128)(2,1)S(1)}, u32[]{:S(2)}, u32[]{:S(2)}) collective-permute-start(bf16[8,240,256]{2,1,0:T(8,128)(2,1)S(1)} %all_to_all.25.own_ref.refs_2_), channel_id=1, source_target_pairs={{0,1},{1,0},{2,3},{3,2},{4,5},{5,4},{6,7},{7,6},{8,9},{9,8},{10,11... | collective-permute-start | bytes 2949128 | tf_op jit(solution)/shard_map/ppermute | solution.py:378
  24.8 0.2 collective-permute-start.3
  25.0 1.9 %collective-permute-start.2 = (bf16[192,768]{1,0:T(8,128)(2,1)S(1)}, bf16[192,768]{1,0:T(8,128)(2,1)S(1)}, u32[]{:S(2)}, u32[]{:S(2)}) collective-permute-start(bf16[192,768]{1,0:T(8,128)(2,1)S(1)} %bitcast.15), channel_id=1, source_target_pairs={{0,8},{1,9},{2,10},{3,11},{4,12},{5,13},{6,14},{7,15},{8,0},{9,1},... | collective-permute-start | bytes 884744 | tf_op jit(solution)/shard_map/ppermute | solution.py:381
  26.9 1.3 collective-permute-start.1
  28.2 0.0 collective-permute-done.oth_ref.refs_6_
  28.2 1.0 copy-done.11
  29.1 9.2 %forward.1 = (bf16[1536,256]{1,0:T(8,128)(2,1)}, bf16[1536,256]{1,0:T(8,128)(2,1)}, f32[3,8,512]{2,1,0:T(8,128)}, bf16[8,144,256]{2,1,0:T(8,128)(2,1)}) custom-call(bf16[8,240,256]{2,1,0:T(8,128)(2,1)} %copy-done.5, bf16[8,240,256]{2,1,0:T(8,128)(2,1)} %copy-done.11), custom_call_target="tpu_custom_call" | custom-call | flops 4831838208 | bytes 6291456 | tf_op jit(solution)/shard_map/forward/pallas_call | solution.py:34
  38.3 0.0 collective-permute-done.3.behind_ref.refs_7_
  38.3 2.0 %collective-permute-done.2.refs_6_ = bf16[192,768]{1,0:T(8,128)(2,1)S(1)} collective-permute-done((bf16[192,768]{1,0:T(8,128)(2,1)S(1)}, bf16[192,768]{1,0:T(8,128)(2,1)S(1)}, u32[]{:S(2)}, u32[]{:S(2)}) %collective-permute-start.2) | collective-permute-done | bytes 294944 | tf_op jit(solution)/shard_map/ppermute | solution.py:381
  40.4 0.8 collective-permute-done.1.ahead_ref.refs_5_
  41.2 4.4 %all-to-all-start.1 = ((bf16[8,144,256]{2,1,0:T(8,128)(2,1)}), bf16[8,144,256]{2,1,0:T(8,128)(2,1)S(1)}, u32[]{:S(2)}, u32[]{:S(2)}) async-start(bf16[8,144,256]{2,1,0:T(8,128)(2,1)} %get-tuple-element.42), calls=%async_computation.1 | async-start | bytes 1179648 | tf_op jit(solution)/shard_map/all_to_all | solution.py:375
  45.7 4.4 %branch.1.refs_4_ = f32[192,768]{1,0:T(8,128)} custom-call(bf16[192,768]{1,0:T(8,128)(2,1)} %bitcast.11, bf16[192,768]{1,0:T(8,128)(2,1)} %copy-done.4, bf16[192,768]{1,0:T(8,128)(2,1)} %copy-done.3, bf16[3,768,768]{2,1,0:T(8,128)(2,1)} %conv_ref.1), custom_call_target="tpu_custom_call" | custom-call | flops 679477248 | bytes 5242880 | tf_op jit(solution)/shard_map/branch/pallas_call | solution.py:34
  50.1 7.1 %probs.1 = (bf16[3072,1536]{1,0:T(8,128)(2,1)}, bf16[128,3072]{1,0:T(8,128)(2,1)}) custom-call(bf16[8,240,256]{2,1,0:T(8,128)(2,1)} %copy-done.5, bf16[8,240,256]{2,1,0:T(8,128)(2,1)} %copy-done.11, bf16[1536,256]{1,0:T(8,128)(2,1)} %get-tuple-element.43.q_ref.refs_5_, f32[3,8,512]{2,1,0:T(8,128)} %get-tuple-element.44.lse_ref), custom_call_target="tpu_custom_call" | custom-call | flops 2415919104 | bytes 12582912 | tf_op jit(solution)/shard_map/probs/pallas_call | solution.py:34
  57.2 0.0 all-to-all-done.1.refs_0_
  57.2 0.0 copy-start.2
  57.3 0.8 copy-done.2
  58.1 4.9 %middle.1 = (bf16[192,768]{1,0:T(8,128)(2,1)}, bf16[8,144,256]{2,1,0:T(8,128)(2,1)}, bf16[192,192]{1,0:T(8,128)(2,1)}, bf16[192,192]{1,0:T(8,128)(2,1)}, bf16[19...) custom-call(bf16[8,144,256]{2,1,0:T(8,128)(2,1)} %copy-done.2, bf16[1536,768]{1,0:T(8,128)(2,1)} %refs_1_.1, ...), custom_call_target="tpu_custom_call" | custom-call | flops 905969664 | bytes 5242880 | tf_op jit(solution)/shard_map/middle/pallas_call | solution.py:34
  63.0 5.2 %all-to-all-start.2 = ((bf16[8,144,256]{2,1,0:T(8,128)(2,1)}), bf16[8,144,256]{2,1,0:T(8,128)(2,1)S(1)}, u32[]{:S(2)}, u32[]{:S(2)}) async-start(bf16[8,144,256]{2,1,0:T(8,128)(2,1)} %get-tuple-element.50), calls=%async_computation.2 | async-start | bytes 1179648 | tf_op jit(solution)/shard_map/all_to_all | solution.py:375
  68.1 2.7 %collective-permute-start.4 = (bf16[192,192]{1,0:T(8,128)(2,1)}, bf16[192,192]{1,0:T(8,128)(2,1)S(1)}, u32[]{:S(2)}, u32[]{:S(2)}) collective-permute-start(bf16[192,192]{1,0:T(8,128)(2,1)} %get-tuple-element.52), channel_id=1, source_target_pairs={{0,12},{1,13},{2,14},{3,15},{4,0},{5,1},{6,2},{7,3},{8,4},{9,5},{1... | collective-permute-start | bytes 221192 | tf_op jit(solution)/shard_map/ppermute | solution.py:381
  70.8 0.6 collective-permute-start.5
  71.4 0.6 collective-permute-start.6
  71.9 5.4 %collective-permute-done.4.refs_1_ = bf16[192,192]{1,0:T(8,128)(2,1)S(1)} collective-permute-done((bf16[192,192]{1,0:T(8,128)(2,1)}, bf16[192,192]{1,0:T(8,128)(2,1)S(1)}, u32[]{:S(2)}, u32[]{:S(2)}) %collective-permute-start.4) | collective-permute-done | bytes 73760 | tf_op jit(solution)/shard_map/ppermute | solution.py:381
  77.3 1.5 %collective-permute-done.5.refs_2_ = bf16[192,192]{1,0:T(8,128)(2,1)S(1)} collective-permute-done((bf16[192,192]{1,0:T(8,128)(2,1)}, bf16[192,192]{1,0:T(8,128)(2,1)S(1)}, u32[]{:S(2)}, u32[]{:S(2)}) %collective-permute-start.5) | collective-permute-done | bytes 73760 | tf_op jit(solution)/shard_map/ppermute | solution.py:381
  78.8 2.0 %collective-permute-done.6.refs_3_ = bf16[192,192]{1,0:T(8,128)(2,1)S(1)} collective-permute-done((bf16[192,192]{1,0:T(8,128)(2,1)}, bf16[192,192]{1,0:T(8,128)(2,1)S(1)}, u32[]{:S(2)}, u32[]{:S(2)}) %collective-permute-start.6) | collective-permute-done | bytes 73760 | tf_op jit(solution)/shard_map/ppermute | solution.py:381
  80.8 0.6 copy-done.10
  81.4 3.7 %weight.1 = bf16[768,576]{1,0:T(8,128)(2,1)} custom-call(bf16[192,192]{1,0:T(8,128)(2,1)} %get-tuple-element.51.refs_0_, bf16[192,192]{1,0:T(8,128)(2,1)} %copy-done.8, bf16[192,192]{1,0:T(8,128)(2,1)} %copy-done.9, bf16[192,192]{1,0:T(8,128)(2,1)} %copy-done.10, bf16[192,768]{1,0:T(8,128)(2,1)} %bitcast.13, bf16[192,768]{1,0:T(8,128)(2,1)} %copy-done.4, ...), custom_call_target="tpu_custom_call" | custom-call | flops 679477248 | bytes 5242880 | tf_op jit(solution)/shard_map/weight/pallas_call | solution.py:34
  85.1 0.0 all-to-all-done.2.refs_0_
  85.1 10.7 %all-to-all-start.3 = ((bf16[16,48,576]{2,1,0:T(8,128)(2,1)}), bf16[16,48,576]{2,1,0:T(8,128)(2,1)S(1)}, u32[]{:S(2)}, u32[]{:S(2)}) async-start(bf16[16,48,576]{2,1,0:T(8,128)(2,1)} %bitcast.10), calls=%async_computation.3 | async-start | bytes 1966080 | tf_op jit(solution)/shard_map/all_to_all | solution.py:472
  95.8 17.1 %backward.1 = (bf16[8,240,256]{2,1,0:T(8,128)(2,1)}, bf16[8,192,256]{2,1,0:T(8,128)(2,1)}) custom-call(bf16[8,144,256]{2,1,0:T(8,128)(2,1)} %copy-done.6, bf16[1536,256]{1,0:T(8,128)(2,1)} %get-tuple-element.57.refs_1_, bf16[8,240,256]{2,1,0:T(8,128)(2,1)} %copy-done.5, bf16[3072,1536]{1,0:T(8,128)(2,1)} %get-tuple-element.58.refs_3_, ...), custom_call_target="tpu_custom_call" | custom-call | flops 9663676416 | bytes 16777216 | tf_op jit(solution)/shard_map/backward/pallas_call | solution.py:34
  112.8 3.0 %collective-permute-start.7 = (bf16[8,192,256]{2,1,0:T(8,128)(2,1)}, bf16[8,192,256]{2,1,0:T(8,128)(2,1)S(1)}, u32[]{:S(2)}, u32[]{:S(2)}) collective-permute-start(bf16[8,192,256]{2,1,0:T(8,128)(2,1)} %get-tuple-element.61), channel_id=1, source_target_pairs={{0,1},{1,0},{2,3},{3,2},{4,5},{5,4},{6,7},{7,6},{8,9},{9,8},{10,11... | collective-permute-start | bytes 2359304 | tf_op jit(solution)/shard_map/ppermute | solution.py:378
  115.9 2.1 %collective-permute-done.7.recv_ref = bf16[8,192,256]{2,1,0:T(8,128)(2,1)S(1)} collective-permute-done((bf16[8,192,256]{2,1,0:T(8,128)(2,1)}, bf16[8,192,256]{2,1,0:T(8,128)(2,1)S(1)}, u32[]{:S(2)}, u32[]{:S(2)}) %collective-permute-start.7) | collective-permute-done | bytes 786464 | tf_op jit(solution)/shard_map/ppermute | solution.py:378
  118.0 1.2 copy-done
  119.2 1.1 add.1
  120.3 0.1 all-to-all-done.3.terms_ref
  120.4 3.7 %all-to-all-start.4 = ((bf16[8,240,256]{2,1,0:T(8,128)(2,1)}), bf16[8,240,256]{2,1,0:T(8,128)(2,1)S(1)}, u32[]{:S(2)}, u32[]{:S(2)}) async-start(bf16[8,240,256]{2,1,0:T(8,128)(2,1)} %add.1), calls=%async_computation.4 | async-start | bytes 1966080 | tf_op jit(solution)/shard_map/all_to_all | solution.py:375
  124.1 0.2 dp_sum.1
  124.3 4.6 %collective-permute-start.8 = (f32[48,144]{1,0:T(8,128)S(1)}, f32[48,144]{1,0:T(8,128)S(1)}, u32[]{:S(2)}, u32[]{:S(2)}) collective-permute-start(f32[48,144]{1,0:T(8,128)S(1)} %get-tuple-element.70), channel_id=1, source_target_pairs={{0,1},{1,0},{2,3},{3,2},{4,5},{5,4},{6,7},{7,6},{8,9},{9,8},{10,11... | collective-permute-start | bytes 82952 | tf_op jit(solution)/shard_map/ppermute | solution.py:378
  128.9 1.8 %collective-permute-start.9 = (f32[48,144]{1,0:T(8,128)S(1)}, f32[48,144]{1,0:T(8,128)S(1)}, u32[]{:S(2)}, u32[]{:S(2)}) collective-permute-start(f32[48,144]{1,0:T(8,128)S(1)} %get-tuple-element.71), channel_id=1, source_target_pairs={{0,2},{1,3},{2,0},{3,1},{4,6},{5,7},{6,4},{7,5},{8,10},{9,11},{10,... | collective-permute-start | bytes 82952 | tf_op jit(solution)/shard_map/ppermute | solution.py:378
  130.7 0.1 collective-permute-start.10
  130.8 0.0 collective-permute-done.8.refs_1_
  130.8 5.0 %collective-permute-done.9.refs_2_ = f32[48,144]{1,0:T(8,128)S(1)} collective-permute-done((f32[48,144]{1,0:T(8,128)S(1)}, f32[48,144]{1,0:T(8,128)S(1)}, u32[]{:S(2)}, u32[]{:S(2)}) %collective-permute-start.9) | collective-permute-done | bytes 27680 | tf_op jit(solution)/shard_map/ppermute | solution.py:378
  135.7 4.8 %collective-permute-done.10.refs_3_ = f32[48,144]{1,0:T(8,128)S(1)} collective-permute-done((f32[48,144]{1,0:T(8,128)S(1)}, f32[48,144]{1,0:T(8,128)S(1)}, u32[]{:S(2)}, u32[]{:S(2)}) %collective-permute-start.10) | collective-permute-done | bytes 27680 | tf_op jit(solution)/shard_map/ppermute | solution.py:378
  140.6 0.7 last_sum.1
  141.3 0.0 all-to-all-done.4.recv_ref
  141.3 1.5 %finish.1 = (bf16[192,512]{1,0:T(8,128)(2,1)}, bf16[192,512]{1,0:T(8,128)(2,1)}, bf16[192,1536]{1,0:T(8,128)(2,1)}) custom-call(bf16[8,240,256]{2,1,0:T(8,128)(2,1)S(1)} %all-to-all-done.4.recv_ref), custom_call_target="tpu_custom_call" | custom-call | bytes 2097152 | tf_op jit(solution)/shard_map/finish/pallas_call | solution.py:34
  (18 shorter events, 0.0 us)
Async XLA Ops:
  0.6 24.1 %copy-start.1 = (bf16[1,192,768]{2,1,0:T(8,128)(2,1)S(1)}, bf16[1,192,768]{2,1,0:T(8,128)(2,1)}, u32[]{:S(2)}) copy-start(bf16[1,192,768]{2,1,0:T(8,128)(2,1)} %param.12) | copy-start | bytes 884740
  22.7 5.5 %copy-start.5 = (bf16[8,240,256]{2,1,0:T(8,128)(2,1)}, bf16[8,240,256]{2,1,0:T(8,128)(2,1)S(1)}, u32[]{:S(2)}) copy-start(bf16[8,240,256]{2,1,0:T(8,128)(2,1)S(1)} %all_to_all.25.own_ref.refs_2_) | copy-start | bytes 2949124
  22.7 5.5 %collective-permute-start = (bf16[8,240,256]{2,1,0:T(8,128)(2,1)S(1)}, bf16[8,240,256]{2,1,0:T(8,128)(2,1)S(1)}, u32[]{:S(2)}, u32[]{:S(2)}) collective-permute-start(bf16[8,240,256]{2,1,0:T(8,128)(2,1)S(1)} %all_to_all.25.own_ref.refs_2_), channel_id=1, source_target_pairs={{0,1},{1,0},{2,3},{3,2},{4,5},{5,4},{6,7},{7,6},{8,9},{9,8},{10,11... | collective-permute-start | bytes 2949128 | tf_op jit(solution)/shard_map/ppermute | solution.py:378
  24.8 13.6 %collective-permute-start.3 = (bf16[192,768]{1,0:T(8,128)(2,1)S(1)}, bf16[192,768]{1,0:T(8,128)(2,1)S(1)}, u32[]{:S(2)}, u32[]{:S(2)}) collective-permute-start(bf16[192,768]{1,0:T(8,128)(2,1)S(1)} %bitcast.14), channel_id=1, source_target_pairs={{0,4},{1,5},{2,6},{3,7},{4,8},{5,9},{6,10},{7,11},{8,12},{9,13},{1... | collective-permute-start | bytes 884744 | tf_op jit(solution)/shard_map/ppermute | solution.py:381
  25.0 15.4 %collective-permute-start.2 = (bf16[192,768]{1,0:T(8,128)(2,1)S(1)}, bf16[192,768]{1,0:T(8,128)(2,1)S(1)}, u32[]{:S(2)}, u32[]{:S(2)}) collective-permute-start(bf16[192,768]{1,0:T(8,128)(2,1)S(1)} %bitcast.15), channel_id=1, source_target_pairs={{0,8},{1,9},{2,10},{3,11},{4,12},{5,13},{6,14},{7,15},{8,0},{9,1},... | collective-permute-start | bytes 884744 | tf_op jit(solution)/shard_map/ppermute | solution.py:381
  26.9 14.3 %collective-permute-start.1 = (bf16[192,768]{1,0:T(8,128)(2,1)S(1)}, bf16[192,768]{1,0:T(8,128)(2,1)S(1)}, u32[]{:S(2)}, u32[]{:S(2)}) collective-permute-start(bf16[192,768]{1,0:T(8,128)(2,1)S(1)} %bitcast.16), channel_id=1, source_target_pairs={{0,12},{1,13},{2,14},{3,15},{4,0},{5,1},{6,2},{7,3},{8,4},{9,5},{1... | collective-permute-start | bytes 884744 | tf_op jit(solution)/shard_map/ppermute | solution.py:381
  28.2 1.0 copy-start.11
  38.3 7.3 %copy-start.3 = (bf16[192,768]{1,0:T(8,128)(2,1)}, bf16[192,768]{1,0:T(8,128)(2,1)S(1)}, u32[]{:S(2)}) copy-start(bf16[192,768]{1,0:T(8,128)(2,1)S(1)} %collective-permute-done.3.behind_ref.refs_7_) | copy-start | bytes 884740
  40.4 16.9 %copy-start.7 = (bf16[192,768]{1,0:T(8,128)(2,1)}, bf16[192,768]{1,0:T(8,128)(2,1)S(1)}, u32[]{:S(2)}) copy-start(bf16[192,768]{1,0:T(8,128)(2,1)S(1)} %collective-permute-done.2.refs_6_) | copy-start | bytes 884740
  41.2 4.5 %copy-start.4 = (bf16[192,768]{1,0:T(8,128)(2,1)}, bf16[192,768]{1,0:T(8,128)(2,1)S(1)}, u32[]{:S(2)}) copy-start(bf16[192,768]{1,0:T(8,128)(2,1)S(1)} %collective-permute-done.1.ahead_ref.refs_5_) | copy-start | bytes 884740
  41.2 16.0 %all-to-all-start.1 = ((bf16[8,144,256]{2,1,0:T(8,128)(2,1)}), bf16[8,144,256]{2,1,0:T(8,128)(2,1)S(1)}, u32[]{:S(2)}, u32[]{:S(2)}) async-start(bf16[8,144,256]{2,1,0:T(8,128)(2,1)} %get-tuple-element.42), calls=%async_computation.1 | async-start | bytes 1179648 | tf_op jit(solution)/shard_map/all_to_all | solution.py:375
  57.2 0.8 copy-start.2
  63.0 22.1 %all-to-all-start.2 = ((bf16[8,144,256]{2,1,0:T(8,128)(2,1)}), bf16[8,144,256]{2,1,0:T(8,128)(2,1)S(1)}, u32[]{:S(2)}, u32[]{:S(2)}) async-start(bf16[8,144,256]{2,1,0:T(8,128)(2,1)} %get-tuple-element.50), calls=%async_computation.2 | async-start | bytes 1179648 | tf_op jit(solution)/shard_map/all_to_all | solution.py:375
  68.1 9.2 %collective-permute-start.4 = (bf16[192,192]{1,0:T(8,128)(2,1)}, bf16[192,192]{1,0:T(8,128)(2,1)S(1)}, u32[]{:S(2)}, u32[]{:S(2)}) collective-permute-start(bf16[192,192]{1,0:T(8,128)(2,1)} %get-tuple-element.52), channel_id=1, source_target_pairs={{0,12},{1,13},{2,14},{3,15},{4,0},{5,1},{6,2},{7,3},{8,4},{9,5},{1... | collective-permute-start | bytes 221192 | tf_op jit(solution)/shard_map/ppermute | solution.py:381
  70.8 8.1 %collective-permute-start.5 = (bf16[192,192]{1,0:T(8,128)(2,1)}, bf16[192,192]{1,0:T(8,128)(2,1)S(1)}, u32[]{:S(2)}, u32[]{:S(2)}) collective-permute-start(bf16[192,192]{1,0:T(8,128)(2,1)} %get-tuple-element.53), channel_id=1, source_target_pairs={{0,8},{1,9},{2,10},{3,11},{4,12},{5,13},{6,14},{7,15},{8,0},{9,1},... | collective-permute-start | bytes 221192 | tf_op jit(solution)/shard_map/ppermute | solution.py:381
  71.4 9.4 %collective-permute-start.6 = (bf16[192,192]{1,0:T(8,128)(2,1)}, bf16[192,192]{1,0:T(8,128)(2,1)S(1)}, u32[]{:S(2)}, u32[]{:S(2)}) collective-permute-start(bf16[192,192]{1,0:T(8,128)(2,1)} %get-tuple-element.54), channel_id=1, source_target_pairs={{0,4},{1,5},{2,6},{3,7},{4,8},{5,9},{6,10},{7,11},{8,12},{9,13},{1... | collective-permute-start | bytes 221192 | tf_op jit(solution)/shard_map/ppermute | solution.py:381
  77.3 3.5 %copy-start.8 = (bf16[192,192]{1,0:T(8,128)(2,1)}, bf16[192,192]{1,0:T(8,128)(2,1)S(1)}, u32[]{:S(2)}) copy-start(bf16[192,192]{1,0:T(8,128)(2,1)S(1)} %collective-permute-done.4.refs_1_) | copy-start | bytes 221188
  78.8 2.0 %copy-start.9 = (bf16[192,192]{1,0:T(8,128)(2,1)}, bf16[192,192]{1,0:T(8,128)(2,1)S(1)}, u32[]{:S(2)}) copy-start(bf16[192,192]{1,0:T(8,128)(2,1)S(1)} %collective-permute-done.5.refs_2_) | copy-start | bytes 221188
  80.8 0.6 copy-start.10
  85.1 10.7 %copy-start.6 = (bf16[8,144,256]{2,1,0:T(8,128)(2,1)}, bf16[8,144,256]{2,1,0:T(8,128)(2,1)S(1)}, u32[]{:S(2)}) copy-start(bf16[8,144,256]{2,1,0:T(8,128)(2,1)S(1)} %all-to-all-done.2.refs_0_) | copy-start | bytes 1769476
  85.1 35.3 %all-to-all-start.3 = ((bf16[16,48,576]{2,1,0:T(8,128)(2,1)}), bf16[16,48,576]{2,1,0:T(8,128)(2,1)S(1)}, u32[]{:S(2)}, u32[]{:S(2)}) async-start(bf16[16,48,576]{2,1,0:T(8,128)(2,1)} %bitcast.10), calls=%async_computation.3 | async-start | bytes 1966080 | tf_op jit(solution)/shard_map/all_to_all | solution.py:472
  112.8 5.2 %collective-permute-start.7 = (bf16[8,192,256]{2,1,0:T(8,128)(2,1)}, bf16[8,192,256]{2,1,0:T(8,128)(2,1)S(1)}, u32[]{:S(2)}, u32[]{:S(2)}) collective-permute-start(bf16[8,192,256]{2,1,0:T(8,128)(2,1)} %get-tuple-element.61), channel_id=1, source_target_pairs={{0,1},{1,0},{2,3},{3,2},{4,5},{5,4},{6,7},{7,6},{8,9},{9,8},{10,11... | collective-permute-start | bytes 2359304 | tf_op jit(solution)/shard_map/ppermute | solution.py:378
  118.0 1.2 copy-start
  120.4 20.9 %all-to-all-start.4 = ((bf16[8,240,256]{2,1,0:T(8,128)(2,1)}), bf16[8,240,256]{2,1,0:T(8,128)(2,1)S(1)}, u32[]{:S(2)}, u32[]{:S(2)}) async-start(bf16[8,240,256]{2,1,0:T(8,128)(2,1)} %add.1), calls=%async_computation.4 | async-start | bytes 1966080 | tf_op jit(solution)/shard_map/all_to_all | solution.py:375
  124.3 6.4 %collective-permute-start.8 = (f32[48,144]{1,0:T(8,128)S(1)}, f32[48,144]{1,0:T(8,128)S(1)}, u32[]{:S(2)}, u32[]{:S(2)}) collective-permute-start(f32[48,144]{1,0:T(8,128)S(1)} %get-tuple-element.70), channel_id=1, source_target_pairs={{0,1},{1,0},{2,3},{3,2},{4,5},{5,4},{6,7},{7,6},{8,9},{9,8},{10,11... | collective-permute-start | bytes 82952 | tf_op jit(solution)/shard_map/ppermute | solution.py:378
  128.9 6.8 %collective-permute-start.9 = (f32[48,144]{1,0:T(8,128)S(1)}, f32[48,144]{1,0:T(8,128)S(1)}, u32[]{:S(2)}, u32[]{:S(2)}) collective-permute-start(f32[48,144]{1,0:T(8,128)S(1)} %get-tuple-element.71), channel_id=1, source_target_pairs={{0,2},{1,3},{2,0},{3,1},{4,6},{5,7},{6,4},{7,5},{8,10},{9,11},{10,... | collective-permute-start | bytes 82952 | tf_op jit(solution)/shard_map/ppermute | solution.py:378
  130.7 9.9 %collective-permute-start.10 = (f32[48,144]{1,0:T(8,128)S(1)}, f32[48,144]{1,0:T(8,128)S(1)}, u32[]{:S(2)}, u32[]{:S(2)}) collective-permute-start(f32[48,144]{1,0:T(8,128)S(1)} %get-tuple-element.72), channel_id=1, source_target_pairs={{0,3},{1,2},{2,1},{3,0},{4,7},{5,6},{6,5},{7,4},{8,11},{9,10},{10,... | collective-permute-start | bytes 82952 | tf_op jit(solution)/shard_map/ppermute | solution.py:378

commit v4 on v3

--- a/solution.py
+++ b/solution.py
@@ -329,8 +329,16 @@
     return both
 
 
-def dp_sum_body(terms_ref, *outs):
-    both = sum_of([terms_ref.at[i] for i in range(terms_ref.shape[0])])
+def column_sum_body(terms_ref, keep_ref, give_ref, both_ref):
+    both_ref[...] = sum_of([terms_ref.at[i] for i in range(terms_ref.shape[0])])
+    rows = keep_ref.shape[0]
+    side = lax.axis_index("dp") % 2
+    keep_ref[...] = both_ref[pl.ds(pl.multiple_of(side * rows, rows), rows), :]
+    give_ref[...] = both_ref[pl.ds(pl.multiple_of((1 - side) * rows, rows), rows), :].astype(BF)
+
+
+def side_sum_body(keep_ref, came_ref, *outs):
+    both = sum_of((keep_ref, came_ref))
     width = outs[0].shape[1]
     for r, out_ref in enumerate(outs):
         out_ref[...] = both[:, r * width : (r + 1) * width]
@@ -392,7 +400,7 @@
     )
     own, cot = lax.optimization_barrier((exchange(packed), cotangent[0]))
     oth = swap(own)
-    cots = [round_ring(cot, by * stride) for by in (1, 2, 3)]
+    ahead, behind = round_ring(cot, stride), round_ring(cot, 3 * stride)
     query, attended, lse, send = call(
         forward_body,
         [
@@ -408,8 +416,9 @@
         pairs_done,
         "forward",
     )(own, oth)
-    send, *cots = lax.optimization_barrier((send, *cots))
+    send, ahead, behind = lax.optimization_barrier((send, ahead, behind))
     recv = exchange(send)
+    across = round_ring(ahead, stride)
     probs, keys_turned = call(
         probs_body,
         [shape(2 * mine, mine), shape(128, 2 * mine)],
@@ -430,8 +439,8 @@
         5 * MIB,
         0,
         "branch",
-    )(cot, cots[0], cots[2], conv_weight)
-    recv, probs, branch = lax.optimization_barrier((recv, probs, branch))
+    )(cot, ahead, behind, conv_weight)
+    recv, branch, across = lax.optimization_barrier((recv, branch, across))
     ins = (recv, out_proj, stream[0], cot, branch)
     stream_grad, send, *acts = call(
         middle_body,
@@ -466,10 +475,12 @@
         5 * MIB,
         0,
         "weight",
-    )(acts[0], *moved, cot, *cots)
-    recv, terms = lax.optimization_barrier((recv, terms))
-    terms = terms.reshape(copies, channels // copies, ring * part)
-    terms = lax.all_to_all(terms, "dp", 0, 0, tiled=True)
+    )(acts[0], *moved, cot, ahead, across, behind)
+    recv, terms, probs, keys_turned = lax.optimization_barrier((recv, terms, probs, keys_turned))
+    layers = copies // 2
+    terms = terms.reshape(layers, channels // layers, ring * part)
+    columns = [[2 * z + y for z in range(layers)] for y in range(2)]
+    terms = lax.all_to_all(terms, "dp", 0, 0, axis_index_groups=columns, tiled=True)
     ins = (recv, attended, own, probs, keys_turned, query, oth)
     own_grad, oth_grad = call(
         backward_body,
@@ -491,22 +502,28 @@
         far_in=range(7),
         far_out=(0, 1),
     )(*ins)
+    terms, oth_grad = lax.optimization_barrier((terms, oth_grad))
     swapped = swap(oth_grad)
+    share = channels // copies
+    keep, give = call(
+        column_sum_body,
+        [shape(share, ring * part, dtype=F32), shape(share, ring * part)],
+        [pltpu.VMEM((2 * share, ring * part), F32)],
+        12,
+        0,
+        MIB,
+        0,
+        "column_sum",
+    )(terms)
+    came = lax.ppermute(give, "dp", [(i, i ^ 1) for i in range(copies)])
     packed = call(add_body, [shape(chips, rows + quarter, WIDE)], [], 12, 0, 3 * MIB, 0, "add")(
         own_grad, swapped
     )
-    packed, terms = lax.optimization_barrier((packed, terms))
+    packed, came = lax.optimization_barrier((packed, came))
     recv = exchange(packed)
     parts = call(
-        dp_sum_body,
-        [shape(channels // copies, part, dtype=F32)] * ring,
-        [],
-        12,
-        0,
-        MIB,
-        0,
-        "dp_sum",
-    )(terms)
+        side_sum_body, [shape(share, part, dtype=F32)] * ring, [], 12, 0, MIB, 0, "side_sum"
+    )(keep, came)
     parts = [parts[0]] + [swap(parts[r], r) for r in (1, 2, 3)]
     weight_grad = call(
         last_sum_body,

time: 143 us -> 146 us (1.021)
  waiting for transfers between devices: 23.7 us -> 28.8 us
  starting transfers between devices: 42.8 us -> 40.6 us
    all_to_all x1, waiting for transfers between devices: 0.05 us -> 7.73 us  [shards(): lax.all_to_all(terms, 'dp', 0, 0, axis_index_groups=columns, tiled=True)]
    ppermute x6, waiting for transfers between devices: 11.7 us -> 8.57 us  [round_ring(): lax.ppermute(value, 'seq', [(i, (i - by) % count) for i in range(count)])]
    ppermute x5, starting transfers between devices: 11.6 us -> 8.61 us  [swap(): return lax.ppermute(value, 'seq', [(i, i ^ bit) for i in range(count)])]
    ppermute x0 -> x1, starting transfers between devices: none -> 2.95 us  [shards(): came = lax.ppermute(give, 'dp', [(i, i ^ 1) for i in range(copies)])]
    all_to_all x1, starting transfers between devices: 10.7 us -> 8.21 us  [shards(): lax.all_to_all(terms, 'dp', 0, 0, axis_index_groups=columns, tiled=True)]
    ppermute x6, starting transfers between devices: 7.23 us -> 9.12 us  [round_ring(): lax.ppermute(value, 'seq', [(i, (i - by) % count) for i in range(count)])]
    all_to_all x3, starting transfers between devices: 13.3 us -> 11.7 us  [exchange(): lax.all_to_all(value, 'seq', 0, 0, axis_index_groups=same_core, tiled=True)]
    pallas_call x11 -> x12, Pallas kernels: 52.5 us -> 52.6 us  [run(): pl.pallas_call(body, out_shape=outs, in_specs=[far if i in far_in else vm...]
  transfers between devices with their start and end apart: 15 -> 16, of which waited for: 9 -> 6; matrix products, arithmetic and copies ran while one was open for 0% -> 0% of each run, Pallas kernels for 30% -> 30%
where the time goes in v4:
time: 146 us
  Pallas kernels  52.6 us (36%)
  starting transfers between devices  40.6 us (28%)
  waiting for transfers between devices  28.8 us (20%)
  blocking collectives  19.4 us (13%)
  local copies, waits for them, and re-layouts  3.68 us (3%)
    pallas_call x12, Pallas kernels, run(): pl.pallas_call(body, out_shape=outs, in_specs=[far if i in far_in else vm...  52.6 us
    all_to_all x1, blocking collectives, exchange(): lax.all_to_all(value, 'seq', 0, 0, axis_index_groups=same_core, tiled=True)  19.4 us
    ppermute x5, waiting for transfers between devices, swap(): return lax.ppermute(value, 'seq', [(i, i ^ bit) for i in range(count)])  12.3 us
    all_to_all x3, starting transfers between devices, exchange(): lax.all_to_all(value, 'seq', 0, 0, axis_index_groups=same_core, tiled=True)  11.7 us
    ppermute x6, starting transfers between devices, round_ring(): lax.ppermute(value, 'seq', [(i, (i - by) % count) for i in range(count)])  9.12 us
    ppermute x5, starting transfers between devices, swap(): return lax.ppermute(value, 'seq', [(i, i ^ bit) for i in range(count)])  8.61 us
    ppermute x6, waiting for transfers between devices, round_ring(): lax.ppermute(value, 'seq', [(i, (i - by) % count) for i in range(count)])  8.57 us
    all_to_all x1, starting transfers between devices, shards(): lax.all_to_all(terms, 'dp', 0, 0, axis_index_groups=columns, tiled=True)  8.21 us
  transfers between devices with their start and end apart: 16, of which 6 were waited for; matrix products, arithmetic and copies ran while one was open for 0% of the time, Pallas kernels for 30%

profile of v4, /device:TPU:1, one launch (start us, length us, event | category | flops | bytes accessed | tf_op | source)
XLA Modules:
  0.0 145.9 jit_solution(11155574682704136179)
XLA Ops:
  0.6 0.0 copy-start.1
  0.6 2.6 %pack.1 = bf16[8,240,256]{2,1,0:T(8,128)(2,1)} custom-call(bf16[192,512]{1,0:T(8,128)(2,1)} %bitcast.18, bf16[192,512]{1,0:T(8,128)(2,1)} %bitcast.19, bf16[192,1536]{1,0:T(8,128)(2,1)} %bitcast.16), custom_call_target="tpu_custom_call" | custom-call | bytes 2097152 | tf_op jit(solution)/shard_map/pack/pallas_call | solution.py:34
  3.2 19.4 %all_to_all.25.own_ref.refs_2_ = bf16[8,240,256]{2,1,0:T(8,128)(2,1)S(1)} all-to-all(bf16[8,240,256]{2,1,0:T(8,128)(2,1)} %pack.1), channel_id=1, replica_groups={{0,2,4,6,8,10,12,14},{1,3,5,7,9,11,13,15},{16,18,20,22,24,26,28,30},{17..., dimensions={0} | all-to-all | bytes 1966080 | tf_op jit(solution)/shard_map/all_to_all | solution.py:383
  22.7 2.1 %collective-permute-start = (bf16[8,240,256]{2,1,0:T(8,128)(2,1)S(1)}, bf16[8,240,256]{2,1,0:T(8,128)(2,1)S(1)}, u32[]{:S(2)}, u32[]{:S(2)}) collective-permute-start(bf16[8,240,256]{2,1,0:T(8,128)(2,1)S(1)} %all_to_all.25.own_ref.refs_2_), channel_id=1, source_target_pairs={{0,1},{1,0},{2,3},{3,2},{4,5},{5,4},{6,7},{7,6},{8,9},{9,8},{10,11... | collective-permute-start | bytes 2949128 | tf_op jit(solution)/shard_map/ppermute | solution.py:386
  24.8 0.2 collective-permute-start.2
  25.0 2.5 %collective-permute-start.1 = (bf16[192,768]{1,0:T(8,128)(2,1)S(1)}, bf16[192,768]{1,0:T(8,128)(2,1)S(1)}, u32[]{:S(2)}, u32[]{:S(2)}) collective-permute-start(bf16[192,768]{1,0:T(8,128)(2,1)S(1)} %bitcast.15), channel_id=1, source_target_pairs={{0,12},{1,13},{2,14},{3,15},{4,0},{5,1},{6,2},{7,3},{8,4},{9,5},{1... | collective-permute-start | bytes 884744 | tf_op jit(solution)/shard_map/ppermute | solution.py:389
  27.5 0.0 collective-permute-done.oth_ref.refs_6_
  27.5 1.0 copy-done.11
  28.4 9.2 %forward.1 = (bf16[1536,256]{1,0:T(8,128)(2,1)}, bf16[1536,256]{1,0:T(8,128)(2,1)}, f32[3,8,512]{2,1,0:T(8,128)}, bf16[8,144,256]{2,1,0:T(8,128)(2,1)}) custom-call(bf16[8,240,256]{2,1,0:T(8,128)(2,1)} %copy-done.5, bf16[8,240,256]{2,1,0:T(8,128)(2,1)} %copy-done.11), custom_call_target="tpu_custom_call" | custom-call | flops 4831838208 | bytes 6291456 | tf_op jit(solution)/shard_map/forward/pallas_call | solution.py:34
  37.6 0.0 collective-permute-done.2.behind_ref.refs_7_
  37.6 0.0 collective-permute-done.1.ahead_ref.refs_5_
  37.7 3.6 %all-to-all-start.1 = ((bf16[8,144,256]{2,1,0:T(8,128)(2,1)}), bf16[8,144,256]{2,1,0:T(8,128)(2,1)S(1)}, u32[]{:S(2)}, u32[]{:S(2)}) async-start(bf16[8,144,256]{2,1,0:T(8,128)(2,1)} %get-tuple-element.47), calls=%async_computation.1 | async-start | bytes 1179648 | tf_op jit(solution)/shard_map/all_to_all | solution.py:383
  41.2 2.6 %collective-permute-start.3 = (bf16[192,768]{1,0:T(8,128)(2,1)S(1)}, bf16[192,768]{1,0:T(8,128)(2,1)S(1)}, u32[]{:S(2)}, u32[]{:S(2)}) collective-permute-start(bf16[192,768]{1,0:T(8,128)(2,1)S(1)} %collective-permute-done.1.ahead_ref.refs_5_), channel_id=1, source_target_pairs={{0,12},{1,13},{2,14},{3,15},{4,0},{5,1},{6,2},{7,3},{8,4},{9,5},{1... | collective-permute-start | bytes 884744 | tf_op jit(solution)/shard_map/ppermute | solution.py:389
  43.8 4.4 %branch.1.refs_4_ = f32[192,768]{1,0:T(8,128)} custom-call(bf16[192,768]{1,0:T(8,128)(2,1)} %bitcast.11, bf16[192,768]{1,0:T(8,128)(2,1)} %copy-done.4, bf16[192,768]{1,0:T(8,128)(2,1)} %copy-done.3, bf16[3,768,768]{2,1,0:T(8,128)(2,1)} %conv_ref.1), custom_call_target="tpu_custom_call" | custom-call | flops 679477248 | bytes 5242880 | tf_op jit(solution)/shard_map/branch/pallas_call | solution.py:34
  48.3 7.3 %collective-permute-done.3.refs_6_ = bf16[192,768]{1,0:T(8,128)(2,1)S(1)} collective-permute-done((bf16[192,768]{1,0:T(8,128)(2,1)S(1)}, bf16[192,768]{1,0:T(8,128)(2,1)S(1)}, u32[]{:S(2)}, u32[]{:S(2)}) %collective-permute-start.3) | collective-permute-done | bytes 294944 | tf_op jit(solution)/shard_map/ppermute | solution.py:389
  55.6 0.0 all-to-all-done.1.refs_0_
  55.6 0.9 copy-done.2
  56.5 4.9 %middle.1 = (bf16[192,768]{1,0:T(8,128)(2,1)}, bf16[8,144,256]{2,1,0:T(8,128)(2,1)}, bf16[192,192]{1,0:T(8,128)(2,1)}, bf16[192,192]{1,0:T(8,128)(2,1)}, bf16[19...) custom-call(bf16[8,144,256]{2,1,0:T(8,128)(2,1)} %copy-done.2, bf16[1536,768]{1,0:T(8,128)(2,1)} %refs_1_.1, ...), custom_call_target="tpu_custom_call" | custom-call | flops 905969664 | bytes 5242880 | tf_op jit(solution)/shard_map/middle/pallas_call | solution.py:34
  61.4 4.6 %all-to-all-start.2 = ((bf16[8,144,256]{2,1,0:T(8,128)(2,1)}), bf16[8,144,256]{2,1,0:T(8,128)(2,1)S(1)}, u32[]{:S(2)}, u32[]{:S(2)}) async-start(bf16[8,144,256]{2,1,0:T(8,128)(2,1)} %get-tuple-element.52), calls=%async_computation.2 | async-start | bytes 1179648 | tf_op jit(solution)/shard_map/all_to_all | solution.py:383
  65.9 2.7 %collective-permute-start.4 = (bf16[192,192]{1,0:T(8,128)(2,1)}, bf16[192,192]{1,0:T(8,128)(2,1)S(1)}, u32[]{:S(2)}, u32[]{:S(2)}) collective-permute-start(bf16[192,192]{1,0:T(8,128)(2,1)} %get-tuple-element.54), channel_id=1, source_target_pairs={{0,12},{1,13},{2,14},{3,15},{4,0},{5,1},{6,2},{7,3},{8,4},{9,5},{1... | collective-permute-start | bytes 221192 | tf_op jit(solution)/shard_map/ppermute | solution.py:389
  68.6 0.6 collective-permute-start.5
  69.2 0.6 collective-permute-start.6
  69.8 7.1 %probs.1 = (bf16[3072,1536]{1,0:T(8,128)(2,1)}, bf16[128,3072]{1,0:T(8,128)(2,1)}) custom-call(bf16[8,240,256]{2,1,0:T(8,128)(2,1)} %copy-done.5, bf16[8,240,256]{2,1,0:T(8,128)(2,1)} %copy-done.11, bf16[1536,256]{1,0:T(8,128)(2,1)} %get-tuple-element.58.q_ref.refs_5_, f32[3,8,512]{2,1,0:T(8,128)} %get-tuple-element.59.lse_ref), custom_call_target="tpu_custom_call" | custom-call | flops 2415919104 | bytes 12582912 | tf_op jit(solution)/shard_map/probs/pallas_call | solution.py:34
  76.9 0.0 collective-permute-done.4.refs_1_
  76.9 0.0 copy-start.8
  76.9 0.0 collective-permute-done.5.refs_2_
  77.0 1.2 collective-permute-done.6.refs_3_
  78.2 0.6 copy-done.10
  78.8 3.7 %weight.1 = bf16[768,576]{1,0:T(8,128)(2,1)} custom-call(bf16[192,192]{1,0:T(8,128)(2,1)} %get-tuple-element.53.refs_0_, bf16[192,192]{1,0:T(8,128)(2,1)} %copy-done.8, bf16[192,192]{1,0:T(8,128)(2,1)} %copy-done.9, bf16[192,192]{1,0:T(8,128)(2,1)} %copy-done.10, bf16[192,768]{1,0:T(8,128)(2,1)} %bitcast.13, bf16[192,768]{1,0:T(8,128)(2,1)} %copy-done.4, ...), custom_call_target="tpu_custom_call" | custom-call | flops 679477248 | bytes 5242880 | tf_op jit(solution)/shard_map/weight/pallas_call | solution.py:34
  82.5 8.2 %all-to-all-start.3 = ((bf16[8,96,576]{2,1,0:T(8,128)(2,1)}), bf16[8,96,576]{2,1,0:T(8,128)(2,1)S(1)}, u32[]{:S(2)}, u32[]{:S(2)}) async-start(bf16[8,96,576]{2,1,0:T(8,128)(2,1)} %bitcast.10), calls=%async_computation.3 | async-start | bytes 1966080 | tf_op jit(solution)/shard_map/all_to_all | solution.py:483
  90.7 17.1 %backward.1 = (bf16[8,240,256]{2,1,0:T(8,128)(2,1)}, bf16[8,192,256]{2,1,0:T(8,128)(2,1)}) custom-call(bf16[8,144,256]{2,1,0:T(8,128)(2,1)} %copy-done.6, bf16[1536,256]{1,0:T(8,128)(2,1)} %get-tuple-element.63.refs_1_, bf16[8,240,256]{2,1,0:T(8,128)(2,1)} %copy-done.5, bf16[3072,1536]{1,0:T(8,128)(2,1)} %get-tuple-element.64.refs_3_, ...), custom_call_target="tpu_custom_call" | custom-call | flops 9663676416 | bytes 16777216 | tf_op jit(solution)/shard_map/backward/pallas_call | solution.py:34
  107.8 7.7 %all-to-all-done.3.terms_ref = bf16[8,96,576]{2,1,0:T(8,128)(2,1)S(1)} async-done(((bf16[8,96,576]{2,1,0:T(8,128)(2,1)}), bf16[8,96,576]{2,1,0:T(8,128)(2,1)S(1)}, u32[]{:S(2)}, u32[]{:S(2)}) %all-to-all-start.3) | async-done | bytes 884768 | tf_op jit(solution)/shard_map/all_to_all | solution.py:483
  115.5 3.5 %collective-permute-start.7 = (bf16[8,192,256]{2,1,0:T(8,128)(2,1)}, bf16[8,192,256]{2,1,0:T(8,128)(2,1)S(1)}, u32[]{:S(2)}, u32[]{:S(2)}) collective-permute-start(bf16[8,192,256]{2,1,0:T(8,128)(2,1)} %get-tuple-element.69), channel_id=1, source_target_pairs={{0,1},{1,0},{2,3},{3,2},{4,5},{5,4},{6,7},{7,6},{8,9},{9,8},{10,11... | collective-permute-start | bytes 2359304 | tf_op jit(solution)/shard_map/ppermute | solution.py:386
  119.0 0.2 column_sum.1
  119.2 3.0 %collective-permute-start.8 = (bf16[48,576]{1,0:T(8,128)(2,1)S(1)}, bf16[48,576]{1,0:T(8,128)(2,1)S(1)}, u32[]{:S(2)}, u32[]{:S(2)}) collective-permute-start(bf16[48,576]{1,0:T(8,128)(2,1)S(1)} %get-tuple-element.71), channel_id=1, source_target_pairs={{0,16},{16,0},{32,48},{48,32},{64,80},{80,64},{96,112},{112,96},{1... | collective-permute-start | bytes 165896 | tf_op jit(solution)/shard_map/ppermute | solution.py:518
  122.2 1.2 copy-done
  123.4 1.2 add.1
  124.5 0.2 collective-permute-done.8.came_ref
  124.7 3.6 %all-to-all-start.4 = ((bf16[8,240,256]{2,1,0:T(8,128)(2,1)}), bf16[8,240,256]{2,1,0:T(8,128)(2,1)S(1)}, u32[]{:S(2)}, u32[]{:S(2)}) async-start(bf16[8,240,256]{2,1,0:T(8,128)(2,1)} %add.1), calls=%async_computation.4 | async-start | bytes 1966080 | tf_op jit(solution)/shard_map/all_to_all | solution.py:383
  128.3 0.1 side_sum.1
  128.4 1.2 collective-permute-start.9
  129.5 1.8 %collective-permute-start.10 = (f32[48,144]{1,0:T(8,128)S(1)}, f32[48,144]{1,0:T(8,128)S(1)}, u32[]{:S(2)}, u32[]{:S(2)}) collective-permute-start(f32[48,144]{1,0:T(8,128)S(1)} %get-tuple-element.81), channel_id=1, source_target_pairs={{0,2},{1,3},{2,0},{3,1},{4,6},{5,7},{6,4},{7,5},{8,10},{9,11},{10,... | collective-permute-start | bytes 82952 | tf_op jit(solution)/shard_map/ppermute | solution.py:386
  131.3 0.1 collective-permute-start.11
  131.4 5.4 %collective-permute-done.10.refs_2_ = f32[48,144]{1,0:T(8,128)S(1)} collective-permute-done((f32[48,144]{1,0:T(8,128)S(1)}, f32[48,144]{1,0:T(8,128)S(1)}, u32[]{:S(2)}, u32[]{:S(2)}) %collective-permute-start.10) | collective-permute-done | bytes 27680 | tf_op jit(solution)/shard_map/ppermute | solution.py:386
  136.8 6.9 %collective-permute-done.11.refs_3_ = f32[48,144]{1,0:T(8,128)S(1)} collective-permute-done((f32[48,144]{1,0:T(8,128)S(1)}, f32[48,144]{1,0:T(8,128)S(1)}, u32[]{:S(2)}, u32[]{:S(2)}) %collective-permute-start.11) | collective-permute-done | bytes 27680 | tf_op jit(solution)/shard_map/ppermute | solution.py:386
  143.7 0.7 last_sum.1
  144.4 0.0 all-to-all-done.4.recv_ref
  144.4 1.5 %finish.1 = (bf16[192,512]{1,0:T(8,128)(2,1)}, bf16[192,512]{1,0:T(8,128)(2,1)}, bf16[192,1536]{1,0:T(8,128)(2,1)}) custom-call(bf16[8,240,256]{2,1,0:T(8,128)(2,1)S(1)} %all-to-all-done.4.recv_ref), custom_call_target="tpu_custom_call" | custom-call | bytes 2097152 | tf_op jit(solution)/shard_map/finish/pallas_call | solution.py:34
  (21 shorter events, 0.0 us)
Async XLA Ops:
  0.6 24.2 %copy-start.1 = (bf16[1,192,768]{2,1,0:T(8,128)(2,1)S(1)}, bf16[1,192,768]{2,1,0:T(8,128)(2,1)}, u32[]{:S(2)}) copy-start(bf16[1,192,768]{2,1,0:T(8,128)(2,1)} %param.12) | copy-start | bytes 884740
  22.7 4.8 %copy-start.5 = (bf16[8,240,256]{2,1,0:T(8,128)(2,1)}, bf16[8,240,256]{2,1,0:T(8,128)(2,1)S(1)}, u32[]{:S(2)}) copy-start(bf16[8,240,256]{2,1,0:T(8,128)(2,1)S(1)} %all_to_all.25.own_ref.refs_2_) | copy-start | bytes 2949124
  22.7 4.8 %collective-permute-start = (bf16[8,240,256]{2,1,0:T(8,128)(2,1)S(1)}, bf16[8,240,256]{2,1,0:T(8,128)(2,1)S(1)}, u32[]{:S(2)}, u32[]{:S(2)}) collective-permute-start(bf16[8,240,256]{2,1,0:T(8,128)(2,1)S(1)} %all_to_all.25.own_ref.refs_2_), channel_id=1, source_target_pairs={{0,1},{1,0},{2,3},{3,2},{4,5},{5,4},{6,7},{7,6},{8,9},{9,8},{10,11... | collective-permute-start | bytes 2949128 | tf_op jit(solution)/shard_map/ppermute | solution.py:386
  24.8 12.9 %collective-permute-start.2 = (bf16[192,768]{1,0:T(8,128)(2,1)S(1)}, bf16[192,768]{1,0:T(8,128)(2,1)S(1)}, u32[]{:S(2)}, u32[]{:S(2)}) collective-permute-start(bf16[192,768]{1,0:T(8,128)(2,1)S(1)} %bitcast.14), channel_id=1, source_target_pairs={{0,4},{1,5},{2,6},{3,7},{4,8},{5,9},{6,10},{7,11},{8,12},{9,13},{1... | collective-permute-start | bytes 884744 | tf_op jit(solution)/shard_map/ppermute | solution.py:389
  25.0 12.7 %collective-permute-start.1 = (bf16[192,768]{1,0:T(8,128)(2,1)S(1)}, bf16[192,768]{1,0:T(8,128)(2,1)S(1)}, u32[]{:S(2)}, u32[]{:S(2)}) collective-permute-start(bf16[192,768]{1,0:T(8,128)(2,1)S(1)} %bitcast.15), channel_id=1, source_target_pairs={{0,12},{1,13},{2,14},{3,15},{4,0},{5,1},{6,2},{7,3},{8,4},{9,5},{1... | collective-permute-start | bytes 884744 | tf_op jit(solution)/shard_map/ppermute | solution.py:389
  27.5 1.0 copy-start.11
  37.6 6.2 %copy-start.3 = (bf16[192,768]{1,0:T(8,128)(2,1)}, bf16[192,768]{1,0:T(8,128)(2,1)S(1)}, u32[]{:S(2)}) copy-start(bf16[192,768]{1,0:T(8,128)(2,1)S(1)} %collective-permute-done.2.behind_ref.refs_7_) | copy-start | bytes 884740
  37.6 6.2 %copy-start.4 = (bf16[192,768]{1,0:T(8,128)(2,1)}, bf16[192,768]{1,0:T(8,128)(2,1)S(1)}, u32[]{:S(2)}) copy-start(bf16[192,768]{1,0:T(8,128)(2,1)S(1)} %collective-permute-done.1.ahead_ref.refs_5_) | copy-start | bytes 884740
  37.7 17.9 %all-to-all-start.1 = ((bf16[8,144,256]{2,1,0:T(8,128)(2,1)}), bf16[8,144,256]{2,1,0:T(8,128)(2,1)S(1)}, u32[]{:S(2)}, u32[]{:S(2)}) async-start(bf16[8,144,256]{2,1,0:T(8,128)(2,1)} %get-tuple-element.47), calls=%async_computation.1 | async-start | bytes 1179648 | tf_op jit(solution)/shard_map/all_to_all | solution.py:383
  41.2 14.4 %collective-permute-start.3 = (bf16[192,768]{1,0:T(8,128)(2,1)S(1)}, bf16[192,768]{1,0:T(8,128)(2,1)S(1)}, u32[]{:S(2)}, u32[]{:S(2)}) collective-permute-start(bf16[192,768]{1,0:T(8,128)(2,1)S(1)} %collective-permute-done.1.ahead_ref.refs_5_), channel_id=1, source_target_pairs={{0,12},{1,13},{2,14},{3,15},{4,0},{5,1},{6,2},{7,3},{8,4},{9,5},{1... | collective-permute-start | bytes 884744 | tf_op jit(solution)/shard_map/ppermute | solution.py:389
  55.6 22.6 %copy-start.7 = (bf16[192,768]{1,0:T(8,128)(2,1)}, bf16[192,768]{1,0:T(8,128)(2,1)S(1)}, u32[]{:S(2)}) copy-start(bf16[192,768]{1,0:T(8,128)(2,1)S(1)} %collective-permute-done.3.refs_6_) | copy-start | bytes 884740
  55.6 0.9 copy-start.2
  61.4 21.1 %all-to-all-start.2 = ((bf16[8,144,256]{2,1,0:T(8,128)(2,1)}), bf16[8,144,256]{2,1,0:T(8,128)(2,1)S(1)}, u32[]{:S(2)}, u32[]{:S(2)}) async-start(bf16[8,144,256]{2,1,0:T(8,128)(2,1)} %get-tuple-element.52), calls=%async_computation.2 | async-start | bytes 1179648 | tf_op jit(solution)/shard_map/all_to_all | solution.py:383
  65.9 11.0 %collective-permute-start.4 = (bf16[192,192]{1,0:T(8,128)(2,1)}, bf16[192,192]{1,0:T(8,128)(2,1)S(1)}, u32[]{:S(2)}, u32[]{:S(2)}) collective-permute-start(bf16[192,192]{1,0:T(8,128)(2,1)} %get-tuple-element.54), channel_id=1, source_target_pairs={{0,12},{1,13},{2,14},{3,15},{4,0},{5,1},{6,2},{7,3},{8,4},{9,5},{1... | collective-permute-start | bytes 221192 | tf_op jit(solution)/shard_map/ppermute | solution.py:389
  68.6 8.3 %collective-permute-start.5 = (bf16[192,192]{1,0:T(8,128)(2,1)}, bf16[192,192]{1,0:T(8,128)(2,1)S(1)}, u32[]{:S(2)}, u32[]{:S(2)}) collective-permute-start(bf16[192,192]{1,0:T(8,128)(2,1)} %get-tuple-element.55), channel_id=1, source_target_pairs={{0,8},{1,9},{2,10},{3,11},{4,12},{5,13},{6,14},{7,15},{8,0},{9,1},... | collective-permute-start | bytes 221192 | tf_op jit(solution)/shard_map/ppermute | solution.py:389
  69.2 9.0 %collective-permute-start.6 = (bf16[192,192]{1,0:T(8,128)(2,1)}, bf16[192,192]{1,0:T(8,128)(2,1)S(1)}, u32[]{:S(2)}, u32[]{:S(2)}) collective-permute-start(bf16[192,192]{1,0:T(8,128)(2,1)} %get-tuple-element.56), channel_id=1, source_target_pairs={{0,4},{1,5},{2,6},{3,7},{4,8},{5,9},{6,10},{7,11},{8,12},{9,13},{1... | collective-permute-start | bytes 221192 | tf_op jit(solution)/shard_map/ppermute | solution.py:389
  76.9 1.3 copy-start.8
  76.9 1.2 copy-start.9
  78.2 0.6 copy-start.10
  82.5 8.2 %copy-start.6 = (bf16[8,144,256]{2,1,0:T(8,128)(2,1)}, bf16[8,144,256]{2,1,0:T(8,128)(2,1)S(1)}, u32[]{:S(2)}) copy-start(bf16[8,144,256]{2,1,0:T(8,128)(2,1)S(1)} %all-to-all-done.2.refs_0_) | copy-start | bytes 1769476
  82.5 33.0 %all-to-all-start.3 = ((bf16[8,96,576]{2,1,0:T(8,128)(2,1)}), bf16[8,96,576]{2,1,0:T(8,128)(2,1)S(1)}, u32[]{:S(2)}, u32[]{:S(2)}) async-start(bf16[8,96,576]{2,1,0:T(8,128)(2,1)} %bitcast.10), calls=%async_computation.3 | async-start | bytes 1966080 | tf_op jit(solution)/shard_map/all_to_all | solution.py:483
  115.5 6.7 %collective-permute-start.7 = (bf16[8,192,256]{2,1,0:T(8,128)(2,1)}, bf16[8,192,256]{2,1,0:T(8,128)(2,1)S(1)}, u32[]{:S(2)}, u32[]{:S(2)}) collective-permute-start(bf16[8,192,256]{2,1,0:T(8,128)(2,1)} %get-tuple-element.69), channel_id=1, source_target_pairs={{0,1},{1,0},{2,3},{3,2},{4,5},{5,4},{6,7},{7,6},{8,9},{9,8},{10,11... | collective-permute-start | bytes 2359304 | tf_op jit(solution)/shard_map/ppermute | solution.py:386
  119.2 5.5 %collective-permute-start.8 = (bf16[48,576]{1,0:T(8,128)(2,1)S(1)}, bf16[48,576]{1,0:T(8,128)(2,1)S(1)}, u32[]{:S(2)}, u32[]{:S(2)}) collective-permute-start(bf16[48,576]{1,0:T(8,128)(2,1)S(1)} %get-tuple-element.71), channel_id=1, source_target_pairs={{0,16},{16,0},{32,48},{48,32},{64,80},{80,64},{96,112},{112,96},{1... | collective-permute-start | bytes 165896 | tf_op jit(solution)/shard_map/ppermute | solution.py:518
  122.2 1.2 copy-start
  124.7 19.7 %all-to-all-start.4 = ((bf16[8,240,256]{2,1,0:T(8,128)(2,1)}), bf16[8,240,256]{2,1,0:T(8,128)(2,1)S(1)}, u32[]{:S(2)}, u32[]{:S(2)}) async-start(bf16[8,240,256]{2,1,0:T(8,128)(2,1)} %add.1), calls=%async_computation.4 | async-start | bytes 1966080 | tf_op jit(solution)/shard_map/all_to_all | solution.py:383
  128.4 3.0 %collective-permute-start.9 = (f32[48,144]{1,0:T(8,128)S(1)}, f32[48,144]{1,0:T(8,128)S(1)}, u32[]{:S(2)}, u32[]{:S(2)}) collective-permute-start(f32[48,144]{1,0:T(8,128)S(1)} %get-tuple-element.80), channel_id=1, source_target_pairs={{0,1},{1,0},{2,3},{3,2},{4,5},{5,4},{6,7},{7,6},{8,9},{9,8},{10,11... | collective-permute-start | bytes 82952 | tf_op jit(solution)/shard_map/ppermute | solution.py:386
  129.5 7.2 %collective-permute-start.10 = (f32[48,144]{1,0:T(8,128)S(1)}, f32[48,144]{1,0:T(8,128)S(1)}, u32[]{:S(2)}, u32[]{:S(2)}) collective-permute-start(f32[48,144]{1,0:T(8,128)S(1)} %get-tuple-element.81), channel_id=1, source_target_pairs={{0,2},{1,3},{2,0},{3,1},{4,6},{5,7},{6,4},{7,5},{8,10},{9,11},{10,... | collective-permute-start | bytes 82952 | tf_op jit(solution)/shard_map/ppermute | solution.py:386
  131.3 12.4 %collective-permute-start.11 = (f32[48,144]{1,0:T(8,128)S(1)}, f32[48,144]{1,0:T(8,128)S(1)}, u32[]{:S(2)}, u32[]{:S(2)}) collective-permute-start(f32[48,144]{1,0:T(8,128)S(1)} %get-tuple-element.82), channel_id=1, source_target_pairs={{0,3},{1,2},{2,1},{3,0},{4,7},{5,6},{6,5},{7,4},{8,11},{9,10},{10,... | collective-permute-start | bytes 82952 | tf_op jit(solution)/shard_map/ppermute | solution.py:386

commit v5 on v3

--- a/solution.py
+++ b/solution.py
@@ -392,7 +392,7 @@
     )
     own, cot = lax.optimization_barrier((exchange(packed), cotangent[0]))
     oth = swap(own)
-    cots = [round_ring(cot, by * stride) for by in (1, 2, 3)]
+    ahead, behind = round_ring(cot, stride), round_ring(cot, 3 * stride)
     query, attended, lse, send = call(
         forward_body,
         [
@@ -408,8 +408,9 @@
         pairs_done,
         "forward",
     )(own, oth)
-    send, *cots = lax.optimization_barrier((send, *cots))
+    send, ahead, behind = lax.optimization_barrier((send, ahead, behind))
     recv = exchange(send)
+    across = round_ring(ahead, stride)
     probs, keys_turned = call(
         probs_body,
         [shape(2 * mine, mine), shape(128, 2 * mine)],
@@ -430,8 +431,8 @@
         5 * MIB,
         0,
         "branch",
-    )(cot, cots[0], cots[2], conv_weight)
-    recv, probs, branch = lax.optimization_barrier((recv, probs, branch))
+    )(cot, ahead, behind, conv_weight)
+    recv, branch = lax.optimization_barrier((recv, branch))
     ins = (recv, out_proj, stream[0], cot, branch)
     stream_grad, send, *acts = call(
         middle_body,
@@ -453,6 +454,7 @@
         far_in=range(5),
     )(*ins)
     recv = exchange(send)
+    across, *acts = lax.optimization_barrier((across, *acts))
     moved = [round_ring(acts[ring - by], by * stride) for by in (1, 2, 3)]
     terms = call(
         weight_body,
@@ -466,8 +468,8 @@
         5 * MIB,
         0,
         "weight",
-    )(acts[0], *moved, cot, *cots)
-    recv, terms = lax.optimization_barrier((recv, terms))
+    )(acts[0], *moved, cot, ahead, across, behind)
+    recv, terms, probs, keys_turned = lax.optimization_barrier((recv, terms, probs, keys_turned))
     terms = terms.reshape(copies, channels // copies, ring * part)
     terms = lax.all_to_all(terms, "dp", 0, 0, tiled=True)
     ins = (recv, attended, own, probs, keys_turned, query, oth)

time: 143 us -> 135 us (0.944)
  waiting for transfers between devices: 23.7 us -> 15.3 us
    ppermute x6, waiting for transfers between devices: 11.7 us -> 0.23 us  [round_ring(): lax.ppermute(value, 'seq', [(i, (i - by) % count) for i in range(count)])]
    all_to_all x3, waiting for transfers between devices: 0.01 us -> 2.69 us  [exchange(): lax.all_to_all(value, 'seq', 0, 0, axis_index_groups=same_core, tiled=True)]
    all_to_all x3, starting transfers between devices: 13.3 us -> 10.7 us  [exchange(): lax.all_to_all(value, 'seq', 0, 0, axis_index_groups=same_core, tiled=True)]
    ppermute x6, starting transfers between devices: 7.23 us -> 9.1 us  [round_ring(): lax.ppermute(value, 'seq', [(i, (i - by) % count) for i in range(count)])]
  transfers between devices with their start and end apart: 15 -> 15, of which waited for: 9 -> 5; matrix products, arithmetic and copies ran while one was open for 0% -> 0% of each run, Pallas kernels for 30% -> 36%
where the time goes in v5:
time: 135 us
  Pallas kernels  52.5 us (39%)
  starting transfers between devices  42.4 us (31%)
  blocking collectives  19.4 us (14%)
  waiting for transfers between devices  15.3 us (11%)
  local copies, waits for them, and re-layouts  4.09 us (3%)
    pallas_call x11, Pallas kernels, run(): pl.pallas_call(body, out_shape=outs, in_specs=[far if i in far_in else vm...  52.5 us
    all_to_all x1, blocking collectives, exchange(): lax.all_to_all(value, 'seq', 0, 0, axis_index_groups=same_core, tiled=True)  19.4 us
    ppermute x5, waiting for transfers between devices, swap(): return lax.ppermute(value, 'seq', [(i, i ^ bit) for i in range(count)])  12.4 us
    ppermute x5, starting transfers between devices, swap(): return lax.ppermute(value, 'seq', [(i, i ^ bit) for i in range(count)])  12 us
    all_to_all x3, starting transfers between devices, exchange(): lax.all_to_all(value, 'seq', 0, 0, axis_index_groups=same_core, tiled=True)  10.7 us
    all_to_all x1, starting transfers between devices, shards(): terms = lax.all_to_all(terms, 'dp', 0, 0, tiled=True)  10.6 us
    ppermute x6, starting transfers between devices, round_ring(): lax.ppermute(value, 'seq', [(i, (i - by) % count) for i in range(count)])  9.1 us
    unnamed x24, local copies, waits for them, and re-layouts  4.09 us
  transfers between devices with their start and end apart: 15, of which 5 were waited for; matrix products, arithmetic and copies ran while one was open for 0% of the time, Pallas kernels for 36%

profile of v5, /device:TPU:1, one launch (start us, length us, event | category | flops | bytes accessed | tf_op | source)
XLA Modules:
  0.0 134.5 jit_solution(9086937906805516337)
XLA Ops:
  0.6 0.0 copy-start.1
  0.6 2.6 %pack.1 = bf16[8,240,256]{2,1,0:T(8,128)(2,1)} custom-call(bf16[192,512]{1,0:T(8,128)(2,1)} %bitcast.18, bf16[192,512]{1,0:T(8,128)(2,1)} %bitcast.19, bf16[192,1536]{1,0:T(8,128)(2,1)} %bitcast.16), custom_call_target="tpu_custom_call" | custom-call | bytes 2097152 | tf_op jit(solution)/shard_map/pack/pallas_call | solution.py:34
  3.2 19.4 %all_to_all.25.own_ref.refs_2_ = bf16[8,240,256]{2,1,0:T(8,128)(2,1)S(1)} all-to-all(bf16[8,240,256]{2,1,0:T(8,128)(2,1)} %pack.1), channel_id=1, replica_groups={{0,2,4,6,8,10,12,14},{1,3,5,7,9,11,13,15},{16,18,20,22,24,26,28,30},{17..., dimensions={0} | all-to-all | bytes 1966080 | tf_op jit(solution)/shard_map/all_to_all | solution.py:375
  22.7 2.1 %collective-permute-start = (bf16[8,240,256]{2,1,0:T(8,128)(2,1)S(1)}, bf16[8,240,256]{2,1,0:T(8,128)(2,1)S(1)}, u32[]{:S(2)}, u32[]{:S(2)}) collective-permute-start(bf16[8,240,256]{2,1,0:T(8,128)(2,1)S(1)} %all_to_all.25.own_ref.refs_2_), channel_id=1, source_target_pairs={{0,1},{1,0},{2,3},{3,2},{4,5},{5,4},{6,7},{7,6},{8,9},{9,8},{10,11... | collective-permute-start | bytes 2949128 | tf_op jit(solution)/shard_map/ppermute | solution.py:378
  24.8 0.2 collective-permute-start.2
  25.0 2.5 %collective-permute-start.1 = (bf16[192,768]{1,0:T(8,128)(2,1)S(1)}, bf16[192,768]{1,0:T(8,128)(2,1)S(1)}, u32[]{:S(2)}, u32[]{:S(2)}) collective-permute-start(bf16[192,768]{1,0:T(8,128)(2,1)S(1)} %bitcast.15), channel_id=1, source_target_pairs={{0,12},{1,13},{2,14},{3,15},{4,0},{5,1},{6,2},{7,3},{8,4},{9,5},{1... | collective-permute-start | bytes 884744 | tf_op jit(solution)/shard_map/ppermute | solution.py:381
  27.5 0.0 collective-permute-done.oth_ref.refs_6_
  27.5 1.0 copy-done.11
  28.4 9.2 %forward.1 = (bf16[1536,256]{1,0:T(8,128)(2,1)}, bf16[1536,256]{1,0:T(8,128)(2,1)}, f32[3,8,512]{2,1,0:T(8,128)}, bf16[8,144,256]{2,1,0:T(8,128)(2,1)}) custom-call(bf16[8,240,256]{2,1,0:T(8,128)(2,1)} %copy-done.5, bf16[8,240,256]{2,1,0:T(8,128)(2,1)} %copy-done.11), custom_call_target="tpu_custom_call" | custom-call | flops 4831838208 | bytes 6291456 | tf_op jit(solution)/shard_map/forward/pallas_call | solution.py:34
  37.6 0.0 collective-permute-done.2.behind_ref.refs_7_
  37.6 0.0 collective-permute-done.1.ahead_ref.refs_5_
  37.7 3.6 %all-to-all-start.1 = ((bf16[8,144,256]{2,1,0:T(8,128)(2,1)}), bf16[8,144,256]{2,1,0:T(8,128)(2,1)S(1)}, u32[]{:S(2)}, u32[]{:S(2)}) async-start(bf16[8,144,256]{2,1,0:T(8,128)(2,1)} %get-tuple-element.47), calls=%async_computation.1 | async-start | bytes 1179648 | tf_op jit(solution)/shard_map/all_to_all | solution.py:375
  41.2 2.6 %collective-permute-start.3 = (bf16[192,768]{1,0:T(8,128)(2,1)S(1)}, bf16[192,768]{1,0:T(8,128)(2,1)S(1)}, u32[]{:S(2)}, u32[]{:S(2)}) collective-permute-start(bf16[192,768]{1,0:T(8,128)(2,1)S(1)} %collective-permute-done.1.ahead_ref.refs_5_), channel_id=1, source_target_pairs={{0,12},{1,13},{2,14},{3,15},{4,0},{5,1},{6,2},{7,3},{8,4},{9,5},{1... | collective-permute-start | bytes 884744 | tf_op jit(solution)/shard_map/ppermute | solution.py:381
  43.8 4.4 %branch.1.refs_4_ = f32[192,768]{1,0:T(8,128)} custom-call(bf16[192,768]{1,0:T(8,128)(2,1)} %bitcast.11, bf16[192,768]{1,0:T(8,128)(2,1)} %copy-done.4, bf16[192,768]{1,0:T(8,128)(2,1)} %copy-done.3, bf16[3,768,768]{2,1,0:T(8,128)(2,1)} %conv_ref.1), custom_call_target="tpu_custom_call" | custom-call | flops 679477248 | bytes 5242880 | tf_op jit(solution)/shard_map/branch/pallas_call | solution.py:34
  48.3 2.7 %all-to-all-done.1.refs_0_ = bf16[8,144,256]{2,1,0:T(8,128)(2,1)S(1)} async-done(((bf16[8,144,256]{2,1,0:T(8,128)(2,1)}), bf16[8,144,256]{2,1,0:T(8,128)(2,1)S(1)}, u32[]{:S(2)}, u32[]{:S(2)}) %all-to-all-start.1) | async-done | bytes 589856 | tf_op jit(solution)/shard_map/all_to_all | solution.py:375
  50.9 0.8 copy-done.2
  51.8 4.9 %middle.1 = (bf16[192,768]{1,0:T(8,128)(2,1)}, bf16[8,144,256]{2,1,0:T(8,128)(2,1)}, bf16[192,192]{1,0:T(8,128)(2,1)}, bf16[192,192]{1,0:T(8,128)(2,1)}, bf16[19...) custom-call(bf16[8,144,256]{2,1,0:T(8,128)(2,1)} %copy-done.2, bf16[1536,768]{1,0:T(8,128)(2,1)} %refs_1_.1, ...), custom_call_target="tpu_custom_call" | custom-call | flops 905969664 | bytes 5242880 | tf_op jit(solution)/shard_map/middle/pallas_call | solution.py:34
  56.7 3.5 %all-to-all-start.2 = ((bf16[8,144,256]{2,1,0:T(8,128)(2,1)}), bf16[8,144,256]{2,1,0:T(8,128)(2,1)S(1)}, u32[]{:S(2)}, u32[]{:S(2)}) async-start(bf16[8,144,256]{2,1,0:T(8,128)(2,1)} %get-tuple-element.52), calls=%async_computation.2 | async-start | bytes 1179648 | tf_op jit(solution)/shard_map/all_to_all | solution.py:375
  60.2 0.0 collective-permute-done.3.refs_6_
  60.2 0.0 copy-start.7
  60.2 2.7 %collective-permute-start.4 = (bf16[192,192]{1,0:T(8,128)(2,1)}, bf16[192,192]{1,0:T(8,128)(2,1)S(1)}, u32[]{:S(2)}, u32[]{:S(2)}) collective-permute-start(bf16[192,192]{1,0:T(8,128)(2,1)} %get-tuple-element.58), channel_id=1, source_target_pairs={{0,12},{1,13},{2,14},{3,15},{4,0},{5,1},{6,2},{7,3},{8,4},{9,5},{1... | collective-permute-start | bytes 221192 | tf_op jit(solution)/shard_map/ppermute | solution.py:381
  62.9 0.5 collective-permute-start.5
  63.5 0.6 collective-permute-start.6
  64.0 7.1 %probs.1 = (bf16[3072,1536]{1,0:T(8,128)(2,1)}, bf16[128,3072]{1,0:T(8,128)(2,1)}) custom-call(bf16[8,240,256]{2,1,0:T(8,128)(2,1)} %copy-done.5, bf16[8,240,256]{2,1,0:T(8,128)(2,1)} %copy-done.11, bf16[1536,256]{1,0:T(8,128)(2,1)} %get-tuple-element.62.q_ref.refs_5_, f32[3,8,512]{2,1,0:T(8,128)} %get-tuple-element.63.lse_ref), custom_call_target="tpu_custom_call" | custom-call | flops 2415919104 | bytes 12582912 | tf_op jit(solution)/shard_map/probs/pallas_call | solution.py:34
  71.2 0.0 collective-permute-done.4.refs_1_
  71.2 0.2 collective-permute-done.6.refs_3_
  71.5 0.4 copy-done.8
  71.9 0.1 copy-done.9
  71.9 0.6 copy-done.10
  72.6 3.7 %weight.1 = bf16[768,576]{1,0:T(8,128)(2,1)} custom-call(bf16[192,192]{1,0:T(8,128)(2,1)} %get-tuple-element.57.refs_0_, bf16[192,192]{1,0:T(8,128)(2,1)} %copy-done.8, bf16[192,192]{1,0:T(8,128)(2,1)} %copy-done.9, bf16[192,192]{1,0:T(8,128)(2,1)} %copy-done.10, bf16[192,768]{1,0:T(8,128)(2,1)} %bitcast.13, bf16[192,768]{1,0:T(8,128)(2,1)} %copy-done.4, ...), custom_call_target="tpu_custom_call" | custom-call | flops 679477248 | bytes 5242880 | tf_op jit(solution)/shard_map/weight/pallas_call | solution.py:34
  76.2 10.6 %all-to-all-start.3 = ((bf16[16,48,576]{2,1,0:T(8,128)(2,1)}), bf16[16,48,576]{2,1,0:T(8,128)(2,1)S(1)}, u32[]{:S(2)}, u32[]{:S(2)}) async-start(bf16[16,48,576]{2,1,0:T(8,128)(2,1)} %bitcast.10), calls=%async_computation.3 | async-start | bytes 1966080 | tf_op jit(solution)/shard_map/all_to_all | solution.py:474
  86.9 17.1 %backward.1 = (bf16[8,240,256]{2,1,0:T(8,128)(2,1)}, bf16[8,192,256]{2,1,0:T(8,128)(2,1)}) custom-call(bf16[8,144,256]{2,1,0:T(8,128)(2,1)} %copy-done.6, bf16[1536,256]{1,0:T(8,128)(2,1)} %get-tuple-element.67.refs_1_, bf16[8,240,256]{2,1,0:T(8,128)(2,1)} %copy-done.5, bf16[3072,1536]{1,0:T(8,128)(2,1)} %get-tuple-element.68.refs_3_, ...), custom_call_target="tpu_custom_call" | custom-call | flops 9663676416 | bytes 16777216 | tf_op jit(solution)/shard_map/backward/pallas_call | solution.py:34
  104.0 3.9 %collective-permute-start.7 = (bf16[8,192,256]{2,1,0:T(8,128)(2,1)}, bf16[8,192,256]{2,1,0:T(8,128)(2,1)S(1)}, u32[]{:S(2)}, u32[]{:S(2)}) collective-permute-start(bf16[8,192,256]{2,1,0:T(8,128)(2,1)} %get-tuple-element.71), channel_id=1, source_target_pairs={{0,1},{1,0},{2,3},{3,2},{4,5},{5,4},{6,7},{7,6},{8,9},{9,8},{10,11... | collective-permute-start | bytes 2359304 | tf_op jit(solution)/shard_map/ppermute | solution.py:378
  107.9 2.1 %collective-permute-done.7.recv_ref = bf16[8,192,256]{2,1,0:T(8,128)(2,1)S(1)} collective-permute-done((bf16[8,192,256]{2,1,0:T(8,128)(2,1)}, bf16[8,192,256]{2,1,0:T(8,128)(2,1)S(1)}, u32[]{:S(2)}, u32[]{:S(2)}) %collective-permute-start.7) | collective-permute-done | bytes 786464 | tf_op jit(solution)/shard_map/ppermute | solution.py:378
  110.0 1.2 copy-done
  111.2 1.1 add.1
  112.4 0.0 all-to-all-done.3.terms_ref
  112.4 3.6 %all-to-all-start.4 = ((bf16[8,240,256]{2,1,0:T(8,128)(2,1)}), bf16[8,240,256]{2,1,0:T(8,128)(2,1)S(1)}, u32[]{:S(2)}, u32[]{:S(2)}) async-start(bf16[8,240,256]{2,1,0:T(8,128)(2,1)} %add.1), calls=%async_computation.4 | async-start | bytes 1966080 | tf_op jit(solution)/shard_map/all_to_all | solution.py:375
  115.9 0.2 dp_sum.1
  116.1 4.1 %collective-permute-start.8 = (f32[48,144]{1,0:T(8,128)S(1)}, f32[48,144]{1,0:T(8,128)S(1)}, u32[]{:S(2)}, u32[]{:S(2)}) collective-permute-start(f32[48,144]{1,0:T(8,128)S(1)} %get-tuple-element.80), channel_id=1, source_target_pairs={{0,1},{1,0},{2,3},{3,2},{4,5},{5,4},{6,7},{7,6},{8,9},{9,8},{10,11... | collective-permute-start | bytes 82952 | tf_op jit(solution)/shard_map/ppermute | solution.py:378
  120.2 1.8 %collective-permute-start.9 = (f32[48,144]{1,0:T(8,128)S(1)}, f32[48,144]{1,0:T(8,128)S(1)}, u32[]{:S(2)}, u32[]{:S(2)}) collective-permute-start(f32[48,144]{1,0:T(8,128)S(1)} %get-tuple-element.81), channel_id=1, source_target_pairs={{0,2},{1,3},{2,0},{3,1},{4,6},{5,7},{6,4},{7,5},{8,10},{9,11},{10,... | collective-permute-start | bytes 82952 | tf_op jit(solution)/shard_map/ppermute | solution.py:378
  122.0 0.1 collective-permute-start.10
  122.1 0.0 collective-permute-done.8.refs_1_
  122.1 5.2 %collective-permute-done.9.refs_2_ = f32[48,144]{1,0:T(8,128)S(1)} collective-permute-done((f32[48,144]{1,0:T(8,128)S(1)}, f32[48,144]{1,0:T(8,128)S(1)}, u32[]{:S(2)}, u32[]{:S(2)}) %collective-permute-start.9) | collective-permute-done | bytes 27680 | tf_op jit(solution)/shard_map/ppermute | solution.py:378
  127.2 5.1 %collective-permute-done.10.refs_3_ = f32[48,144]{1,0:T(8,128)S(1)} collective-permute-done((f32[48,144]{1,0:T(8,128)S(1)}, f32[48,144]{1,0:T(8,128)S(1)}, u32[]{:S(2)}, u32[]{:S(2)}) %collective-permute-start.10) | collective-permute-done | bytes 27680 | tf_op jit(solution)/shard_map/ppermute | solution.py:378
  132.3 0.7 last_sum.1
  133.0 0.0 all-to-all-done.4.recv_ref
  133.0 1.5 %finish.1 = (bf16[192,512]{1,0:T(8,128)(2,1)}, bf16[192,512]{1,0:T(8,128)(2,1)}, bf16[192,1536]{1,0:T(8,128)(2,1)}) custom-call(bf16[8,240,256]{2,1,0:T(8,128)(2,1)S(1)} %all-to-all-done.4.recv_ref), custom_call_target="tpu_custom_call" | custom-call | bytes 2097152 | tf_op jit(solution)/shard_map/finish/pallas_call | solution.py:34
  (18 shorter events, 0.0 us)
Async XLA Ops:
  0.6 24.1 %copy-start.1 = (bf16[1,192,768]{2,1,0:T(8,128)(2,1)S(1)}, bf16[1,192,768]{2,1,0:T(8,128)(2,1)}, u32[]{:S(2)}) copy-start(bf16[1,192,768]{2,1,0:T(8,128)(2,1)} %param.12) | copy-start | bytes 884740
  22.7 4.8 %copy-start.5 = (bf16[8,240,256]{2,1,0:T(8,128)(2,1)}, bf16[8,240,256]{2,1,0:T(8,128)(2,1)S(1)}, u32[]{:S(2)}) copy-start(bf16[8,240,256]{2,1,0:T(8,128)(2,1)S(1)} %all_to_all.25.own_ref.refs_2_) | copy-start | bytes 2949124
  22.7 4.8 %collective-permute-start = (bf16[8,240,256]{2,1,0:T(8,128)(2,1)S(1)}, bf16[8,240,256]{2,1,0:T(8,128)(2,1)S(1)}, u32[]{:S(2)}, u32[]{:S(2)}) collective-permute-start(bf16[8,240,256]{2,1,0:T(8,128)(2,1)S(1)} %all_to_all.25.own_ref.refs_2_), channel_id=1, source_target_pairs={{0,1},{1,0},{2,3},{3,2},{4,5},{5,4},{6,7},{7,6},{8,9},{9,8},{10,11... | collective-permute-start | bytes 2949128 | tf_op jit(solution)/shard_map/ppermute | solution.py:378
  24.8 12.9 %collective-permute-start.2 = (bf16[192,768]{1,0:T(8,128)(2,1)S(1)}, bf16[192,768]{1,0:T(8,128)(2,1)S(1)}, u32[]{:S(2)}, u32[]{:S(2)}) collective-permute-start(bf16[192,768]{1,0:T(8,128)(2,1)S(1)} %bitcast.14), channel_id=1, source_target_pairs={{0,4},{1,5},{2,6},{3,7},{4,8},{5,9},{6,10},{7,11},{8,12},{9,13},{1... | collective-permute-start | bytes 884744 | tf_op jit(solution)/shard_map/ppermute | solution.py:381
  25.0 12.7 %collective-permute-start.1 = (bf16[192,768]{1,0:T(8,128)(2,1)S(1)}, bf16[192,768]{1,0:T(8,128)(2,1)S(1)}, u32[]{:S(2)}, u32[]{:S(2)}) collective-permute-start(bf16[192,768]{1,0:T(8,128)(2,1)S(1)} %bitcast.15), channel_id=1, source_target_pairs={{0,12},{1,13},{2,14},{3,15},{4,0},{5,1},{6,2},{7,3},{8,4},{9,5},{1... | collective-permute-start | bytes 884744 | tf_op jit(solution)/shard_map/ppermute | solution.py:381
  27.5 1.0 copy-start.11
  37.6 6.2 %copy-start.3 = (bf16[192,768]{1,0:T(8,128)(2,1)}, bf16[192,768]{1,0:T(8,128)(2,1)S(1)}, u32[]{:S(2)}) copy-start(bf16[192,768]{1,0:T(8,128)(2,1)S(1)} %collective-permute-done.2.behind_ref.refs_7_) | copy-start | bytes 884740
  37.6 6.2 %copy-start.4 = (bf16[192,768]{1,0:T(8,128)(2,1)}, bf16[192,768]{1,0:T(8,128)(2,1)S(1)}, u32[]{:S(2)}) copy-start(bf16[192,768]{1,0:T(8,128)(2,1)S(1)} %collective-permute-done.1.ahead_ref.refs_5_) | copy-start | bytes 884740
  37.7 13.3 %all-to-all-start.1 = ((bf16[8,144,256]{2,1,0:T(8,128)(2,1)}), bf16[8,144,256]{2,1,0:T(8,128)(2,1)S(1)}, u32[]{:S(2)}, u32[]{:S(2)}) async-start(bf16[8,144,256]{2,1,0:T(8,128)(2,1)} %get-tuple-element.47), calls=%async_computation.1 | async-start | bytes 1179648 | tf_op jit(solution)/shard_map/all_to_all | solution.py:375
  41.2 19.0 %collective-permute-start.3 = (bf16[192,768]{1,0:T(8,128)(2,1)S(1)}, bf16[192,768]{1,0:T(8,128)(2,1)S(1)}, u32[]{:S(2)}, u32[]{:S(2)}) collective-permute-start(bf16[192,768]{1,0:T(8,128)(2,1)S(1)} %collective-permute-done.1.ahead_ref.refs_5_), channel_id=1, source_target_pairs={{0,12},{1,13},{2,14},{3,15},{4,0},{5,1},{6,2},{7,3},{8,4},{9,5},{1... | collective-permute-start | bytes 884744 | tf_op jit(solution)/shard_map/ppermute | solution.py:381
  50.9 0.8 copy-start.2
  56.7 19.6 %all-to-all-start.2 = ((bf16[8,144,256]{2,1,0:T(8,128)(2,1)}), bf16[8,144,256]{2,1,0:T(8,128)(2,1)S(1)}, u32[]{:S(2)}, u32[]{:S(2)}) async-start(bf16[8,144,256]{2,1,0:T(8,128)(2,1)} %get-tuple-element.52), calls=%async_computation.2 | async-start | bytes 1179648 | tf_op jit(solution)/shard_map/all_to_all | solution.py:375
  60.2 11.0 %copy-start.7 = (bf16[192,768]{1,0:T(8,128)(2,1)}, bf16[192,768]{1,0:T(8,128)(2,1)S(1)}, u32[]{:S(2)}) copy-start(bf16[192,768]{1,0:T(8,128)(2,1)S(1)} %collective-permute-done.3.refs_6_) | copy-start | bytes 884740
  60.2 11.0 %collective-permute-start.4 = (bf16[192,192]{1,0:T(8,128)(2,1)}, bf16[192,192]{1,0:T(8,128)(2,1)S(1)}, u32[]{:S(2)}, u32[]{:S(2)}) collective-permute-start(bf16[192,192]{1,0:T(8,128)(2,1)} %get-tuple-element.58), channel_id=1, source_target_pairs={{0,12},{1,13},{2,14},{3,15},{4,0},{5,1},{6,2},{7,3},{8,4},{9,5},{1... | collective-permute-start | bytes 221192 | tf_op jit(solution)/shard_map/ppermute | solution.py:381
  62.9 8.3 %collective-permute-start.5 = (bf16[192,192]{1,0:T(8,128)(2,1)}, bf16[192,192]{1,0:T(8,128)(2,1)S(1)}, u32[]{:S(2)}, u32[]{:S(2)}) collective-permute-start(bf16[192,192]{1,0:T(8,128)(2,1)} %get-tuple-element.59), channel_id=1, source_target_pairs={{0,8},{1,9},{2,10},{3,11},{4,12},{5,13},{6,14},{7,15},{8,0},{9,1},... | collective-permute-start | bytes 221192 | tf_op jit(solution)/shard_map/ppermute | solution.py:381
  63.5 8.0 %collective-permute-start.6 = (bf16[192,192]{1,0:T(8,128)(2,1)}, bf16[192,192]{1,0:T(8,128)(2,1)S(1)}, u32[]{:S(2)}, u32[]{:S(2)}) collective-permute-start(bf16[192,192]{1,0:T(8,128)(2,1)} %get-tuple-element.60), channel_id=1, source_target_pairs={{0,4},{1,5},{2,6},{3,7},{4,8},{5,9},{6,10},{7,11},{8,12},{9,13},{1... | collective-permute-start | bytes 221192 | tf_op jit(solution)/shard_map/ppermute | solution.py:381
  71.2 0.7 copy-start.8
  71.2 0.7 copy-start.9
  71.9 0.6 copy-start.10
  76.2 10.6 %copy-start.6 = (bf16[8,144,256]{2,1,0:T(8,128)(2,1)}, bf16[8,144,256]{2,1,0:T(8,128)(2,1)S(1)}, u32[]{:S(2)}) copy-start(bf16[8,144,256]{2,1,0:T(8,128)(2,1)S(1)} %all-to-all-done.2.refs_0_) | copy-start | bytes 1769476
  76.2 36.1 %all-to-all-start.3 = ((bf16[16,48,576]{2,1,0:T(8,128)(2,1)}), bf16[16,48,576]{2,1,0:T(8,128)(2,1)S(1)}, u32[]{:S(2)}, u32[]{:S(2)}) async-start(bf16[16,48,576]{2,1,0:T(8,128)(2,1)} %bitcast.10), calls=%async_computation.3 | async-start | bytes 1966080 | tf_op jit(solution)/shard_map/all_to_all | solution.py:474
  104.0 6.1 %collective-permute-start.7 = (bf16[8,192,256]{2,1,0:T(8,128)(2,1)}, bf16[8,192,256]{2,1,0:T(8,128)(2,1)S(1)}, u32[]{:S(2)}, u32[]{:S(2)}) collective-permute-start(bf16[8,192,256]{2,1,0:T(8,128)(2,1)} %get-tuple-element.71), channel_id=1, source_target_pairs={{0,1},{1,0},{2,3},{3,2},{4,5},{5,4},{6,7},{7,6},{8,9},{9,8},{10,11... | collective-permute-start | bytes 2359304 | tf_op jit(solution)/shard_map/ppermute | solution.py:378
  110.0 1.2 copy-start
  112.4 20.7 %all-to-all-start.4 = ((bf16[8,240,256]{2,1,0:T(8,128)(2,1)}), bf16[8,240,256]{2,1,0:T(8,128)(2,1)S(1)}, u32[]{:S(2)}, u32[]{:S(2)}) async-start(bf16[8,240,256]{2,1,0:T(8,128)(2,1)} %add.1), calls=%async_computation.4 | async-start | bytes 1966080 | tf_op jit(solution)/shard_map/all_to_all | solution.py:375
  116.1 6.0 %collective-permute-start.8 = (f32[48,144]{1,0:T(8,128)S(1)}, f32[48,144]{1,0:T(8,128)S(1)}, u32[]{:S(2)}, u32[]{:S(2)}) collective-permute-start(f32[48,144]{1,0:T(8,128)S(1)} %get-tuple-element.80), channel_id=1, source_target_pairs={{0,1},{1,0},{2,3},{3,2},{4,5},{5,4},{6,7},{7,6},{8,9},{9,8},{10,11... | collective-permute-start | bytes 82952 | tf_op jit(solution)/shard_map/ppermute | solution.py:378
  120.2 7.0 %collective-permute-start.9 = (f32[48,144]{1,0:T(8,128)S(1)}, f32[48,144]{1,0:T(8,128)S(1)}, u32[]{:S(2)}, u32[]{:S(2)}) collective-permute-start(f32[48,144]{1,0:T(8,128)S(1)} %get-tuple-element.81), channel_id=1, source_target_pairs={{0,2},{1,3},{2,0},{3,1},{4,6},{5,7},{6,4},{7,5},{8,10},{9,11},{10,... | collective-permute-start | bytes 82952 | tf_op jit(solution)/shard_map/ppermute | solution.py:378
  122.0 10.3 %collective-permute-start.10 = (f32[48,144]{1,0:T(8,128)S(1)}, f32[48,144]{1,0:T(8,128)S(1)}, u32[]{:S(2)}, u32[]{:S(2)}) collective-permute-start(f32[48,144]{1,0:T(8,128)S(1)} %get-tuple-element.82), channel_id=1, source_target_pairs={{0,3},{1,2},{2,1},{3,0},{4,7},{5,6},{6,5},{7,4},{8,11},{9,10},{10,... | collective-permute-start | bytes 82952 | tf_op jit(solution)/shard_map/ppermute | solution.py:378

commit v6 on v5

--- a/solution.py
+++ b/solution.py
@@ -56,13 +56,22 @@
     return jnp.concatenate([block[:, i * width : (i + 1) * width] for i in range(parts)], axis=0)
 
 
-def pack_body(q_ref, k_ref, v_ref, out_ref):
+def pack_body(q_ref, k_ref, far_v, far_out, v_ref, out_ref, sems):
     rows = q_ref.shape[0]
+    value = pltpu.make_async_copy(far_v, v_ref, sems.at[HEADS])
+    value.start()
     for h in range(HEADS):
-        out_ref[h, :rows, :VAL] = v_ref[:, h * VAL : (h + 1) * VAL]
         out_ref[h, :rows, VAL:] = k_ref[:, h * KEY : (h + 1) * KEY]
         part = q_ref[:, h * KEY : (h + 1) * KEY].astype(F32) * (1.0 / math.sqrt(KEY))
         out_ref[h, rows:, :] = side_by_side(part, 4).astype(BF)
+    value.wait()
+    leaving = []
+    for h in range(HEADS):
+        out_ref[h, :rows, :VAL] = v_ref[:, h * VAL : (h + 1) * VAL]
+        leaving.append(pltpu.make_async_copy(out_ref.at[h], far_out.at[h], sems.at[h]))
+        leaving[-1].start()
+    for one in leaving:
+        one.wait()
 
 
 def key_tiles(own_ref, oth_ref, count=2):
@@ -80,8 +89,11 @@
     ]
 
 
-def forward_body(own_ref, oth_ref, q_ref, att_ref, lse_ref, send_ref, *score_refs):
+def forward_body(own_ref, far_oth, far_q, far_att, lse_ref, send_ref, *rest):
+    oth_ref, q_ref, att_ref, sems, *score_refs = rest
     block = score_refs[0].shape[0]
+    oth = pltpu.make_async_copy(far_oth, oth_ref, sems.at[0])
+    oth.start()
     chips = own_ref.shape[0]
     rows = own_ref.shape[1] * 4 // 5
     mine = chips * rows
@@ -90,6 +102,8 @@
         query = on_top(own_ref[c, rows:, :].astype(F32), 4)
         padded = jnp.concatenate([jnp.zeros((rows, VAL), F32), query], axis=1)
         q_ref[c * rows : (c + 1) * rows, :] = padded.astype(BF)
+    leaving = [pltpu.make_async_copy(q_ref, far_q, sems.at[1])]
+    leaving[0].start()
     tiles = key_tiles(own_ref, oth_ref)
     tile = 2 * mine // len(tiles)
 
@@ -101,6 +115,8 @@
 
     top = None
     for j in range(len(tiles)):
+        if j == len(tiles) // 2:
+            oth.wait()
         top = score(0, j, top)
     for b in range(blocks):
         following = None
@@ -113,7 +129,10 @@
             expo = jnp.exp2(score_refs[b % 2][:, j * tile : (j + 1) * tile] * LOG2E - top)
             total = total + jnp.sum(expo, axis=1, keepdims=True)
             summed = summed + plain(expo.astype(BF), part())
-        att_ref[b * block : (b + 1) * block, :] = (summed * (1.0 / total)).astype(BF)
+        at = slice(b * block, (b + 1) * block)
+        att_ref[at, :] = (summed * (1.0 / total)).astype(BF)
+        leaving.append(pltpu.make_async_copy(att_ref.at[at], far_att.at[at], sems.at[2 + b]))
+        leaving[-1].start()
         turned = jnp.transpose(jnp.broadcast_to(top + jnp.log2(total), (block, 128)))
         lse_ref[b] = turned[:8, :]
         top = following
@@ -122,6 +141,8 @@
         for j in range(3):
             piece = side_by_side(part[:, j * 64 : (j + 1) * 64], 4).astype(BF)
             send_ref[c, j * (rows // 4) : (j + 1) * (rows // 4), :] = piece
+    for one in leaving:
+        one.wait()
 
 
 def probs_body(own_ref, oth_ref, q_ref, lse_ref, far_prob_ref, kt_ref, prob_ref, sems):
@@ -343,14 +364,6 @@
         refs[4][t] = both[t * rows : (t + 1) * rows]
 
 
-def add_body(own_ref, recv_ref, out_ref):
-    rows = recv_ref.shape[1]
-    for c in range(own_ref.shape[0]):
-        both = own_ref[c, :rows, :].astype(F32) + recv_ref[c].astype(F32)
-        out_ref[c, :rows, :] = both.astype(BF)
-        out_ref[c, rows:, :] = own_ref[c, rows:, :]
-
-
 def finish_body(recv_ref, q_ref, k_ref, v_ref):
     rows = q_ref.shape[0]
     for h in range(HEADS):
@@ -387,9 +400,22 @@
     pairs_done = mine * 2 * mine
     part, quarter = 3 * channels // count, rows // 4
 
-    packed = call(pack_body, [shape(chips, rows + quarter, WIDE)], [], 60, 0, 2 * MIB, 0, "pack")(
-        queries[0], key_rows[0], values[0]
-    )
+    packed = call(
+        pack_body,
+        [shape(chips, rows + quarter, WIDE)],
+        [
+            pltpu.VMEM((rows, HEADS * VAL), BF),
+            pltpu.VMEM((chips, rows + quarter, WIDE), BF),
+            pltpu.SemaphoreType.DMA((HEADS + 1,)),
+        ],
+        60,
+        0,
+        2 * MIB,
+        0,
+        "pack",
+        far_in=(2,),
+        far_out=(0,),
+    )(queries[0], key_rows[0], values[0])
     own, cot = lax.optimization_barrier((exchange(packed), cotangent[0]))
     oth = swap(own)
     ahead, behind = round_ring(cot, stride), round_ring(cot, 3 * stride)
@@ -401,12 +427,20 @@
             shape(mine // block, 8, block, dtype=F32),
             shape(chips, 3 * quarter, WIDE),
         ],
-        [pltpu.VMEM((block, 2 * mine), F32)] * 2,
+        [
+            pltpu.VMEM((chips, rows + quarter, WIDE), BF),
+            pltpu.VMEM((mine, WIDE), BF),
+            pltpu.VMEM((mine, WIDE), BF),
+            pltpu.SemaphoreType.DMA((2 + mine // block,)),
+            *[pltpu.VMEM((block, 2 * mine), F32)] * 2,
+        ],
         56,
         4 * pairs_done * WIDE,
         6 * MIB,
         pairs_done,
         "forward",
+        far_in=(1,),
+        far_out=(0, 1),
     )(own, oth)
     send, ahead, behind = lax.optimization_barrier((send, ahead, behind))
     recv = exchange(send)
@@ -494,9 +528,8 @@
         far_out=(0, 1),
     )(*ins)
     swapped = swap(oth_grad)
-    packed = call(add_body, [shape(chips, rows + quarter, WIDE)], [], 12, 0, 3 * MIB, 0, "add")(
-        own_grad, swapped
-    )
+    swapped = jnp.pad(swapped.astype(F32), ((0, 0), (0, quarter), (0, 0)))
+    packed = (own_grad.astype(F32) + swapped).astype(BF)
     packed, terms = lax.optimization_barrier((packed, terms))
     recv = exchange(packed)
     parts = call(

time: 135 us -> 137 us (1.015)
  other arithmetic: 0 us -> 2.38 us
    convert_element_type x0 -> x1, other arithmetic: none -> 2.38 us  [shards(): packed = (own_grad.astype(F32) + swapped).astype(BF)]
    unnamed x24 -> x22, local copies, waits for them, and re-layouts: 4.09 us -> 2.9 us
    pallas_call x11 -> x10, Pallas kernels: 52.5 us -> 53 us  [run(): pl.pallas_call(body, out_shape=outs, in_specs=[far if i in far_in else vm...]
  transfers between devices with their start and end apart: 15 -> 15, of which waited for: 5 -> 5; matrix products, arithmetic and copies ran while one was open for 0% -> 2% of each run, Pallas kernels for 36% -> 35%
where the time goes in v6:
time: 137 us; the launch traced here: 136 us
  Pallas kernels  53 us (39%)
  starting transfers between devices  42.4 us (31%)
  blocking collectives  19.4 us (14%)
  waiting for transfers between devices  15.3 us (11%)
  local copies, waits for them, and re-layouts  2.9 us (2%)
  other arithmetic  2.38 us (2%)
    pallas_call x10, Pallas kernels, run(): pl.pallas_call(body, out_shape=outs, in_specs=[far if i in far_in else vm...  53 us
    all_to_all x1, blocking collectives, exchange(): lax.all_to_all(value, 'seq', 0, 0, axis_index_groups=same_core, tiled=True)  19.4 us
    ppermute x5, waiting for transfers between devices, swap(): return lax.ppermute(value, 'seq', [(i, i ^ bit) for i in range(count)])  12.4 us
    ppermute x5, starting transfers between devices, swap(): return lax.ppermute(value, 'seq', [(i, i ^ bit) for i in range(count)])  12 us
    all_to_all x3, starting transfers between devices, exchange(): lax.all_to_all(value, 'seq', 0, 0, axis_index_groups=same_core, tiled=True)  10.7 us
    all_to_all x1, starting transfers between devices, shards(): terms = lax.all_to_all(terms, 'dp', 0, 0, tiled=True)  10.6 us
    ppermute x6, starting transfers between devices, round_ring(): lax.ppermute(value, 'seq', [(i, (i - by) % count) for i in range(count)])  9.1 us
    unnamed x22, local copies, waits for them, and re-layouts  2.9 us
  transfers between devices with their start and end apart: 15, of which 5 were waited for; matrix products, arithmetic and copies ran while one was open for 2% of the time, Pallas kernels for 35%

profile of v6, /device:TPU:1, one launch (start us, length us, event | category | flops | bytes accessed | tf_op | source)
XLA Modules:
  0.0 136.3 jit_solution(8047384071326299000)
XLA Ops:
  0.6 0.0 copy-start
  0.6 3.3 %pack.1 = bf16[8,240,256]{2,1,0:T(8,128)(2,1)} custom-call(bf16[192,512]{1,0:T(8,128)(2,1)} %bitcast.18, bf16[192,512]{1,0:T(8,128)(2,1)} %bitcast.19, bf16[192,1536]{1,0:T(8,128)(2,1)} %bitcast.16), custom_call_target="tpu_custom_call" | custom-call | bytes 2097152 | tf_op jit(solution)/shard_map/pack/pallas_call | solution.py:34
  3.9 19.4 %all_to_all.25.own_ref.refs_2_ = bf16[8,240,256]{2,1,0:T(8,128)(2,1)S(1)} all-to-all(bf16[8,240,256]{2,1,0:T(8,128)(2,1)} %pack.1), channel_id=1, replica_groups={{0,2,4,6,8,10,12,14},{1,3,5,7,9,11,13,15},{16,18,20,22,24,26,28,30},{17..., dimensions={0} | all-to-all | bytes 1966080 | tf_op jit(solution)/shard_map/all_to_all | solution.py:388
  23.4 2.1 %collective-permute-start = (bf16[8,240,256]{2,1,0:T(8,128)(2,1)S(1)}, bf16[8,240,256]{2,1,0:T(8,128)(2,1)S(1)}, u32[]{:S(2)}, u32[]{:S(2)}) collective-permute-start(bf16[8,240,256]{2,1,0:T(8,128)(2,1)S(1)} %all_to_all.25.own_ref.refs_2_), channel_id=1, source_target_pairs={{0,1},{1,0},{2,3},{3,2},{4,5},{5,4},{6,7},{7,6},{8,9},{9,8},{10,11... | collective-permute-start | bytes 2949128 | tf_op jit(solution)/shard_map/ppermute | solution.py:391
  25.5 0.2 collective-permute-start.2
  25.7 2.5 %collective-permute-start.1 = (bf16[192,768]{1,0:T(8,128)(2,1)S(1)}, bf16[192,768]{1,0:T(8,128)(2,1)S(1)}, u32[]{:S(2)}, u32[]{:S(2)}) collective-permute-start(bf16[192,768]{1,0:T(8,128)(2,1)S(1)} %bitcast.15), channel_id=1, source_target_pairs={{0,12},{1,13},{2,14},{3,15},{4,0},{5,1},{6,2},{7,3},{8,4},{9,5},{1... | collective-permute-start | bytes 884744 | tf_op jit(solution)/shard_map/ppermute | solution.py:394
  28.2 0.0 collective-permute-done.far_oth.oth_ref.refs_6_
  28.2 1.0 copy-done.10
  29.1 10.2 %forward.1 = (bf16[1536,256]{1,0:T(8,128)(2,1)}, bf16[1536,256]{1,0:T(8,128)(2,1)}, f32[3,8,512]{2,1,0:T(8,128)}, bf16[8,144,256]{2,1,0:T(8,128)(2,1)}) custom-call(bf16[8,240,256]{2,1,0:T(8,128)(2,1)} %copy-done.4, bf16[8,240,256]{2,1,0:T(8,128)(2,1)} %copy-done.10), custom_call_target="tpu_custom_call" | custom-call | flops 4831838208 | bytes 6291456 | tf_op jit(solution)/shard_map/forward/pallas_call | solution.py:34
  39.3 0.0 collective-permute-done.2.behind_ref.refs_7_
  39.4 0.0 collective-permute-done.1.ahead_ref.refs_5_
  39.4 3.6 %all-to-all-start.1 = ((bf16[8,144,256]{2,1,0:T(8,128)(2,1)}), bf16[8,144,256]{2,1,0:T(8,128)(2,1)S(1)}, u32[]{:S(2)}, u32[]{:S(2)}) async-start(bf16[8,144,256]{2,1,0:T(8,128)(2,1)} %get-tuple-element.47), calls=%async_computation.1 | async-start | bytes 1179648 | tf_op jit(solution)/shard_map/all_to_all | solution.py:388
  42.9 2.6 %collective-permute-start.3 = (bf16[192,768]{1,0:T(8,128)(2,1)S(1)}, bf16[192,768]{1,0:T(8,128)(2,1)S(1)}, u32[]{:S(2)}, u32[]{:S(2)}) collective-permute-start(bf16[192,768]{1,0:T(8,128)(2,1)S(1)} %collective-permute-done.1.ahead_ref.refs_5_), channel_id=1, source_target_pairs={{0,12},{1,13},{2,14},{3,15},{4,0},{5,1},{6,2},{7,3},{8,4},{9,5},{1... | collective-permute-start | bytes 884744 | tf_op jit(solution)/shard_map/ppermute | solution.py:394
  45.6 4.4 %branch.1.refs_4_ = f32[192,768]{1,0:T(8,128)} custom-call(bf16[192,768]{1,0:T(8,128)(2,1)} %bitcast.11, bf16[192,768]{1,0:T(8,128)(2,1)} %copy-done.3, bf16[192,768]{1,0:T(8,128)(2,1)} %copy-done.2, bf16[3,768,768]{2,1,0:T(8,128)(2,1)} %conv_ref.1), custom_call_target="tpu_custom_call" | custom-call | flops 679477248 | bytes 5242880 | tf_op jit(solution)/shard_map/branch/pallas_call | solution.py:34
  50.0 2.7 %all-to-all-done.1.refs_0_ = bf16[8,144,256]{2,1,0:T(8,128)(2,1)S(1)} async-done(((bf16[8,144,256]{2,1,0:T(8,128)(2,1)}), bf16[8,144,256]{2,1,0:T(8,128)(2,1)S(1)}, u32[]{:S(2)}, u32[]{:S(2)}) %all-to-all-start.1) | async-done | bytes 589856 | tf_op jit(solution)/shard_map/all_to_all | solution.py:388
  52.7 0.8 copy-done.1
  53.5 4.9 %middle.1 = (bf16[192,768]{1,0:T(8,128)(2,1)}, bf16[8,144,256]{2,1,0:T(8,128)(2,1)}, bf16[192,192]{1,0:T(8,128)(2,1)}, bf16[192,192]{1,0:T(8,128)(2,1)}, bf16[19...) custom-call(bf16[8,144,256]{2,1,0:T(8,128)(2,1)} %copy-done.1, bf16[1536,768]{1,0:T(8,128)(2,1)} %refs_1_.1, ...), custom_call_target="tpu_custom_call" | custom-call | flops 905969664 | bytes 5242880 | tf_op jit(solution)/shard_map/middle/pallas_call | solution.py:34
  58.4 3.5 %all-to-all-start.2 = ((bf16[8,144,256]{2,1,0:T(8,128)(2,1)}), bf16[8,144,256]{2,1,0:T(8,128)(2,1)S(1)}, u32[]{:S(2)}, u32[]{:S(2)}) async-start(bf16[8,144,256]{2,1,0:T(8,128)(2,1)} %get-tuple-element.52), calls=%async_computation.2 | async-start | bytes 1179648 | tf_op jit(solution)/shard_map/all_to_all | solution.py:388
  62.0 0.0 collective-permute-done.3.refs_6_
  62.0 0.0 copy-start.6
  62.0 2.7 %collective-permute-start.4 = (bf16[192,192]{1,0:T(8,128)(2,1)}, bf16[192,192]{1,0:T(8,128)(2,1)S(1)}, u32[]{:S(2)}, u32[]{:S(2)}) collective-permute-start(bf16[192,192]{1,0:T(8,128)(2,1)} %get-tuple-element.58), channel_id=1, source_target_pairs={{0,12},{1,13},{2,14},{3,15},{4,0},{5,1},{6,2},{7,3},{8,4},{9,5},{1... | collective-permute-start | bytes 221192 | tf_op jit(solution)/shard_map/ppermute | solution.py:394
  64.6 0.5 collective-permute-start.5
  65.2 0.6 collective-permute-start.6
  65.8 7.1 %probs.1 = (bf16[3072,1536]{1,0:T(8,128)(2,1)}, bf16[128,3072]{1,0:T(8,128)(2,1)}) custom-call(bf16[8,240,256]{2,1,0:T(8,128)(2,1)} %copy-done.4, bf16[8,240,256]{2,1,0:T(8,128)(2,1)} %copy-done.10, bf16[1536,256]{1,0:T(8,128)(2,1)} %get-tuple-element.62.q_ref.refs_5_, f32[3,8,512]{2,1,0:T(8,128)} %get-tuple-element.63.lse_ref), custom_call_target="tpu_custom_call" | custom-call | flops 2415919104 | bytes 12582912 | tf_op jit(solution)/shard_map/probs/pallas_call | solution.py:34
  72.9 0.0 collective-permute-done.4.refs_1_
  73.0 0.0 collective-permute-done.5.refs_2_
  73.0 0.2 collective-permute-done.6.refs_3_
  73.2 0.4 copy-done.7
  73.6 0.0 copy-done.8
  73.6 0.6 copy-done.9
  74.3 3.7 %weight.1 = bf16[768,576]{1,0:T(8,128)(2,1)} custom-call(bf16[192,192]{1,0:T(8,128)(2,1)} %get-tuple-element.57.refs_0_, bf16[192,192]{1,0:T(8,128)(2,1)} %copy-done.7, bf16[192,192]{1,0:T(8,128)(2,1)} %copy-done.8, bf16[192,192]{1,0:T(8,128)(2,1)} %copy-done.9, bf16[192,768]{1,0:T(8,128)(2,1)} %bitcast.13, bf16[192,768]{1,0:T(8,128)(2,1)} %copy-done.3, ...), custom_call_target="tpu_custom_call" | custom-call | flops 679477248 | bytes 5242880 | tf_op jit(solution)/shard_map/weight/pallas_call | solution.py:34
  77.9 0.0 all-to-all-done.2.refs_0_
  77.9 10.6 %all-to-all-start.3 = ((bf16[16,48,576]{2,1,0:T(8,128)(2,1)}), bf16[16,48,576]{2,1,0:T(8,128)(2,1)S(1)}, u32[]{:S(2)}, u32[]{:S(2)}) async-start(bf16[16,48,576]{2,1,0:T(8,128)(2,1)} %bitcast.10), calls=%async_computation.3 | async-start | bytes 1966080 | tf_op jit(solution)/shard_map/all_to_all | solution.py:508
  88.6 17.1 %backward.1 = (bf16[8,240,256]{2,1,0:T(8,128)(2,1)}, bf16[8,192,256]{2,1,0:T(8,128)(2,1)}) custom-call(bf16[8,144,256]{2,1,0:T(8,128)(2,1)} %copy-done.5, bf16[1536,256]{1,0:T(8,128)(2,1)} %get-tuple-element.67.refs_1_, bf16[8,240,256]{2,1,0:T(8,128)(2,1)} %copy-done.4, bf16[3072,1536]{1,0:T(8,128)(2,1)} %get-tuple-element.68.refs_3_, ...), custom_call_target="tpu_custom_call" | custom-call | flops 9663676416 | bytes 16777216 | tf_op jit(solution)/shard_map/backward/pallas_call | solution.py:34
  105.7 4.0 %collective-permute-start.7 = (bf16[8,192,256]{2,1,0:T(8,128)(2,1)}, bf16[8,192,256]{2,1,0:T(8,128)(2,1)S(1)}, u32[]{:S(2)}, u32[]{:S(2)}) collective-permute-start(bf16[8,192,256]{2,1,0:T(8,128)(2,1)} %get-tuple-element.71), channel_id=1, source_target_pairs={{0,1},{1,0},{2,3},{3,2},{4,5},{5,4},{6,7},{7,6},{8,9},{9,8},{10,11... | collective-permute-start | bytes 2359304 | tf_op jit(solution)/shard_map/ppermute | solution.py:391
  109.6 2.1 %collective-permute-done.7 = bf16[8,192,256]{2,1,0:T(8,128)(2,1)S(1)} collective-permute-done((bf16[8,192,256]{2,1,0:T(8,128)(2,1)}, bf16[8,192,256]{2,1,0:T(8,128)(2,1)S(1)}, u32[]{:S(2)}, u32[]{:S(2)}) %collective-permute-start.7) | collective-permute-done | bytes 786464 | tf_op jit(solution)/shard_map/ppermute | solution.py:391
  111.7 2.4 %add_convert_fusion = bf16[8,240,256]{2,1,0:T(8,128)(2,1)} fusion(bf16[8,240,256]{2,1,0:T(8,128)(2,1)} %get-tuple-element.70, bf16[8,192,256]{2,1,0:T(8,128)(2,1)S(1)} %collective-permute-done.7), kind=kLoop, calls=%fused_computation | loop fusion | flops 1966080 | bytes 2752512 | tf_op jit(solution)/shard_map/convert_element_type | solution.py:532
  114.1 0.0 all-to-all-done.3.terms_ref
  114.1 3.6 %all-to-all-start.4 = ((bf16[8,240,256]{2,1,0:T(8,128)(2,1)}), bf16[8,240,256]{2,1,0:T(8,128)(2,1)S(1)}, u32[]{:S(2)}, u32[]{:S(2)}) async-start(bf16[8,240,256]{2,1,0:T(8,128)(2,1)} %add_convert_fusion), calls=%async_computation.4 | async-start | bytes 1966080 | tf_op jit(solution)/shard_map/all_to_all | solution.py:388
  117.7 0.2 dp_sum.1
  117.9 4.1 %collective-permute-start.8 = (f32[48,144]{1,0:T(8,128)S(1)}, f32[48,144]{1,0:T(8,128)S(1)}, u32[]{:S(2)}, u32[]{:S(2)}) collective-permute-start(f32[48,144]{1,0:T(8,128)S(1)} %get-tuple-element.80), channel_id=1, source_target_pairs={{0,1},{1,0},{2,3},{3,2},{4,5},{5,4},{6,7},{7,6},{8,9},{9,8},{10,11... | collective-permute-start | bytes 82952 | tf_op jit(solution)/shard_map/ppermute | solution.py:391
  122.0 1.8 %collective-permute-start.9 = (f32[48,144]{1,0:T(8,128)S(1)}, f32[48,144]{1,0:T(8,128)S(1)}, u32[]{:S(2)}, u32[]{:S(2)}) collective-permute-start(f32[48,144]{1,0:T(8,128)S(1)} %get-tuple-element.81), channel_id=1, source_target_pairs={{0,2},{1,3},{2,0},{3,1},{4,6},{5,7},{6,4},{7,5},{8,10},{9,11},{10,... | collective-permute-start | bytes 82952 | tf_op jit(solution)/shard_map/ppermute | solution.py:391
  123.7 0.1 collective-permute-start.10
  123.8 0.0 collective-permute-done.8.refs_1_
  123.8 5.2 %collective-permute-done.9.refs_2_ = f32[48,144]{1,0:T(8,128)S(1)} collective-permute-done((f32[48,144]{1,0:T(8,128)S(1)}, f32[48,144]{1,0:T(8,128)S(1)}, u32[]{:S(2)}, u32[]{:S(2)}) %collective-permute-start.9) | collective-permute-done | bytes 27680 | tf_op jit(solution)/shard_map/ppermute | solution.py:391
  129.0 5.1 %collective-permute-done.10.refs_3_ = f32[48,144]{1,0:T(8,128)S(1)} collective-permute-done((f32[48,144]{1,0:T(8,128)S(1)}, f32[48,144]{1,0:T(8,128)S(1)}, u32[]{:S(2)}, u32[]{:S(2)}) %collective-permute-start.10) | collective-permute-done | bytes 27680 | tf_op jit(solution)/shard_map/ppermute | solution.py:391
  134.1 0.7 last_sum.1
  134.8 1.5 %finish.1 = (bf16[192,512]{1,0:T(8,128)(2,1)}, bf16[192,512]{1,0:T(8,128)(2,1)}, bf16[192,1536]{1,0:T(8,128)(2,1)}) custom-call(bf16[8,240,256]{2,1,0:T(8,128)(2,1)S(1)} %all-to-all-done.4.recv_ref), custom_call_target="tpu_custom_call" | custom-call | bytes 2097152 | tf_op jit(solution)/shard_map/finish/pallas_call | solution.py:34
  (16 shorter events, 0.0 us)
Async XLA Ops:
  0.6 24.9 %copy-start = (bf16[1,192,768]{2,1,0:T(8,128)(2,1)S(1)}, bf16[1,192,768]{2,1,0:T(8,128)(2,1)}, u32[]{:S(2)}) copy-start(bf16[1,192,768]{2,1,0:T(8,128)(2,1)} %param.12) | copy-start | bytes 884740
  23.4 4.8 %copy-start.4 = (bf16[8,240,256]{2,1,0:T(8,128)(2,1)}, bf16[8,240,256]{2,1,0:T(8,128)(2,1)S(1)}, u32[]{:S(2)}) copy-start(bf16[8,240,256]{2,1,0:T(8,128)(2,1)S(1)} %all_to_all.25.own_ref.refs_2_) | copy-start | bytes 2949124
  23.4 4.8 %collective-permute-start = (bf16[8,240,256]{2,1,0:T(8,128)(2,1)S(1)}, bf16[8,240,256]{2,1,0:T(8,128)(2,1)S(1)}, u32[]{:S(2)}, u32[]{:S(2)}) collective-permute-start(bf16[8,240,256]{2,1,0:T(8,128)(2,1)S(1)} %all_to_all.25.own_ref.refs_2_), channel_id=1, source_target_pairs={{0,1},{1,0},{2,3},{3,2},{4,5},{5,4},{6,7},{7,6},{8,9},{9,8},{10,11... | collective-permute-start | bytes 2949128 | tf_op jit(solution)/shard_map/ppermute | solution.py:391
  25.5 13.9 %collective-permute-start.2 = (bf16[192,768]{1,0:T(8,128)(2,1)S(1)}, bf16[192,768]{1,0:T(8,128)(2,1)S(1)}, u32[]{:S(2)}, u32[]{:S(2)}) collective-permute-start(bf16[192,768]{1,0:T(8,128)(2,1)S(1)} %bitcast.14), channel_id=1, source_target_pairs={{0,4},{1,5},{2,6},{3,7},{4,8},{5,9},{6,10},{7,11},{8,12},{9,13},{1... | collective-permute-start | bytes 884744 | tf_op jit(solution)/shard_map/ppermute | solution.py:394
  25.7 13.7 %collective-permute-start.1 = (bf16[192,768]{1,0:T(8,128)(2,1)S(1)}, bf16[192,768]{1,0:T(8,128)(2,1)S(1)}, u32[]{:S(2)}, u32[]{:S(2)}) collective-permute-start(bf16[192,768]{1,0:T(8,128)(2,1)S(1)} %bitcast.15), channel_id=1, source_target_pairs={{0,12},{1,13},{2,14},{3,15},{4,0},{5,1},{6,2},{7,3},{8,4},{9,5},{1... | collective-permute-start | bytes 884744 | tf_op jit(solution)/shard_map/ppermute | solution.py:394
  28.2 1.0 copy-start.10
  39.4 6.2 %copy-start.2 = (bf16[192,768]{1,0:T(8,128)(2,1)}, bf16[192,768]{1,0:T(8,128)(2,1)S(1)}, u32[]{:S(2)}) copy-start(bf16[192,768]{1,0:T(8,128)(2,1)S(1)} %collective-permute-done.2.behind_ref.refs_7_) | copy-start | bytes 884740
  39.4 6.2 %copy-start.3 = (bf16[192,768]{1,0:T(8,128)(2,1)}, bf16[192,768]{1,0:T(8,128)(2,1)S(1)}, u32[]{:S(2)}) copy-start(bf16[192,768]{1,0:T(8,128)(2,1)S(1)} %collective-permute-done.1.ahead_ref.refs_5_) | copy-start | bytes 884740
  39.4 13.3 %all-to-all-start.1 = ((bf16[8,144,256]{2,1,0:T(8,128)(2,1)}), bf16[8,144,256]{2,1,0:T(8,128)(2,1)S(1)}, u32[]{:S(2)}, u32[]{:S(2)}) async-start(bf16[8,144,256]{2,1,0:T(8,128)(2,1)} %get-tuple-element.47), calls=%async_computation.1 | async-start | bytes 1179648 | tf_op jit(solution)/shard_map/all_to_all | solution.py:388
  42.9 19.0 %collective-permute-start.3 = (bf16[192,768]{1,0:T(8,128)(2,1)S(1)}, bf16[192,768]{1,0:T(8,128)(2,1)S(1)}, u32[]{:S(2)}, u32[]{:S(2)}) collective-permute-start(bf16[192,768]{1,0:T(8,128)(2,1)S(1)} %collective-permute-done.1.ahead_ref.refs_5_), channel_id=1, source_target_pairs={{0,12},{1,13},{2,14},{3,15},{4,0},{5,1},{6,2},{7,3},{8,4},{9,5},{1... | collective-permute-start | bytes 884744 | tf_op jit(solution)/shard_map/ppermute | solution.py:394
  52.7 0.8 copy-start.1
  58.4 19.5 %all-to-all-start.2 = ((bf16[8,144,256]{2,1,0:T(8,128)(2,1)}), bf16[8,144,256]{2,1,0:T(8,128)(2,1)S(1)}, u32[]{:S(2)}, u32[]{:S(2)}) async-start(bf16[8,144,256]{2,1,0:T(8,128)(2,1)} %get-tuple-element.52), calls=%async_computation.2 | async-start | bytes 1179648 | tf_op jit(solution)/shard_map/all_to_all | solution.py:388
  62.0 11.0 %copy-start.6 = (bf16[192,768]{1,0:T(8,128)(2,1)}, bf16[192,768]{1,0:T(8,128)(2,1)S(1)}, u32[]{:S(2)}) copy-start(bf16[192,768]{1,0:T(8,128)(2,1)S(1)} %collective-permute-done.3.refs_6_) | copy-start | bytes 884740
  62.0 11.0 %collective-permute-start.4 = (bf16[192,192]{1,0:T(8,128)(2,1)}, bf16[192,192]{1,0:T(8,128)(2,1)S(1)}, u32[]{:S(2)}, u32[]{:S(2)}) collective-permute-start(bf16[192,192]{1,0:T(8,128)(2,1)} %get-tuple-element.58), channel_id=1, source_target_pairs={{0,12},{1,13},{2,14},{3,15},{4,0},{5,1},{6,2},{7,3},{8,4},{9,5},{1... | collective-permute-start | bytes 221192 | tf_op jit(solution)/shard_map/ppermute | solution.py:394
  64.6 8.3 %collective-permute-start.5 = (bf16[192,192]{1,0:T(8,128)(2,1)}, bf16[192,192]{1,0:T(8,128)(2,1)S(1)}, u32[]{:S(2)}, u32[]{:S(2)}) collective-permute-start(bf16[192,192]{1,0:T(8,128)(2,1)} %get-tuple-element.59), channel_id=1, source_target_pairs={{0,8},{1,9},{2,10},{3,11},{4,12},{5,13},{6,14},{7,15},{8,0},{9,1},... | collective-permute-start | bytes 221192 | tf_op jit(solution)/shard_map/ppermute | solution.py:394
  65.2 8.0 %collective-permute-start.6 = (bf16[192,192]{1,0:T(8,128)(2,1)}, bf16[192,192]{1,0:T(8,128)(2,1)S(1)}, u32[]{:S(2)}, u32[]{:S(2)}) collective-permute-start(bf16[192,192]{1,0:T(8,128)(2,1)} %get-tuple-element.60), channel_id=1, source_target_pairs={{0,4},{1,5},{2,6},{3,7},{4,8},{5,9},{6,10},{7,11},{8,12},{9,13},{1... | collective-permute-start | bytes 221192 | tf_op jit(solution)/shard_map/ppermute | solution.py:394
  72.9 0.6 copy-start.7
  73.0 0.7 copy-start.8
  73.6 0.6 copy-start.9
  77.9 10.7 %copy-start.5 = (bf16[8,144,256]{2,1,0:T(8,128)(2,1)}, bf16[8,144,256]{2,1,0:T(8,128)(2,1)S(1)}, u32[]{:S(2)}) copy-start(bf16[8,144,256]{2,1,0:T(8,128)(2,1)S(1)} %all-to-all-done.2.refs_0_) | copy-start | bytes 1769476
  77.9 36.2 %all-to-all-start.3 = ((bf16[16,48,576]{2,1,0:T(8,128)(2,1)}), bf16[16,48,576]{2,1,0:T(8,128)(2,1)S(1)}, u32[]{:S(2)}, u32[]{:S(2)}) async-start(bf16[16,48,576]{2,1,0:T(8,128)(2,1)} %bitcast.10), calls=%async_computation.3 | async-start | bytes 1966080 | tf_op jit(solution)/shard_map/all_to_all | solution.py:508
  105.7 6.1 %collective-permute-start.7 = (bf16[8,192,256]{2,1,0:T(8,128)(2,1)}, bf16[8,192,256]{2,1,0:T(8,128)(2,1)S(1)}, u32[]{:S(2)}, u32[]{:S(2)}) collective-permute-start(bf16[8,192,256]{2,1,0:T(8,128)(2,1)} %get-tuple-element.71), channel_id=1, source_target_pairs={{0,1},{1,0},{2,3},{3,2},{4,5},{5,4},{6,7},{7,6},{8,9},{9,8},{10,11... | collective-permute-start | bytes 2359304 | tf_op jit(solution)/shard_map/ppermute | solution.py:391
  114.1 20.7 %all-to-all-start.4 = ((bf16[8,240,256]{2,1,0:T(8,128)(2,1)}), bf16[8,240,256]{2,1,0:T(8,128)(2,1)S(1)}, u32[]{:S(2)}, u32[]{:S(2)}) async-start(bf16[8,240,256]{2,1,0:T(8,128)(2,1)} %add_convert_fusion), calls=%async_computation.4 | async-start | bytes 1966080 | tf_op jit(solution)/shard_map/all_to_all | solution.py:388
  117.9 5.9 %collective-permute-start.8 = (f32[48,144]{1,0:T(8,128)S(1)}, f32[48,144]{1,0:T(8,128)S(1)}, u32[]{:S(2)}, u32[]{:S(2)}) collective-permute-start(f32[48,144]{1,0:T(8,128)S(1)} %get-tuple-element.80), channel_id=1, source_target_pairs={{0,1},{1,0},{2,3},{3,2},{4,5},{5,4},{6,7},{7,6},{8,9},{9,8},{10,11... | collective-permute-start | bytes 82952 | tf_op jit(solution)/shard_map/ppermute | solution.py:391
  122.0 7.0 %collective-permute-start.9 = (f32[48,144]{1,0:T(8,128)S(1)}, f32[48,144]{1,0:T(8,128)S(1)}, u32[]{:S(2)}, u32[]{:S(2)}) collective-permute-start(f32[48,144]{1,0:T(8,128)S(1)} %get-tuple-element.81), channel_id=1, source_target_pairs={{0,2},{1,3},{2,0},{3,1},{4,6},{5,7},{6,4},{7,5},{8,10},{9,11},{10,... | collective-permute-start | bytes 82952 | tf_op jit(solution)/shard_map/ppermute | solution.py:391
  123.7 10.3 %collective-permute-start.10 = (f32[48,144]{1,0:T(8,128)S(1)}, f32[48,144]{1,0:T(8,128)S(1)}, u32[]{:S(2)}, u32[]{:S(2)}) collective-permute-start(f32[48,144]{1,0:T(8,128)S(1)} %get-tuple-element.82), channel_id=1, source_target_pairs={{0,3},{1,2},{2,1},{3,0},{4,7},{5,6},{6,5},{7,4},{8,11},{9,10},{10,... | collective-permute-start | bytes 82952 | tf_op jit(solution)/shard_map/ppermute | solution.py:391

commit v7 on v5

--- a/solution.py
+++ b/solution.py
@@ -402,7 +402,7 @@
             shape(chips, 3 * quarter, WIDE),
         ],
         [pltpu.VMEM((block, 2 * mine), F32)] * 2,
-        56,
+        36,
         4 * pairs_done * WIDE,
         6 * MIB,
         pairs_done,

time: 135 us -> 134 us (level)
  Pallas kernels: 52.5 us -> 50.8 us
    pallas_call x11, Pallas kernels: 52.5 us -> 50.8 us  [run(): pl.pallas_call(body, out_shape=outs, in_specs=[far if i in far_in else vm...]
    unnamed x24 -> x30, local copies, waits for them, and re-layouts: 4.09 us -> 4.23 us
  transfers between devices with their start and end apart: 15 -> 15, of which waited for: 5 -> 4; matrix products, arithmetic and copies ran while one was open for 0% -> 0% of each run, Pallas kernels for 36% -> 35%
where the time goes in v7:
time: 134 us; the launch traced here: 133 us
  Pallas kernels  50.8 us (38%)
  starting transfers between devices  42.6 us (32%)
  blocking collectives  19.4 us (14%)
  waiting for transfers between devices  15.2 us (11%)
  local copies, waits for them, and re-layouts  4.23 us (3%)
    pallas_call x11, Pallas kernels, run(): pl.pallas_call(body, out_shape=outs, in_specs=[far if i in far_in else vm...  50.8 us
    all_to_all x1, blocking collectives, exchange(): lax.all_to_all(value, 'seq', 0, 0, axis_index_groups=same_core, tiled=True)  19.4 us
    ppermute x5, waiting for transfers between devices, swap(): return lax.ppermute(value, 'seq', [(i, i ^ bit) for i in range(count)])  12.6 us
    ppermute x5, starting transfers between devices, swap(): return lax.ppermute(value, 'seq', [(i, i ^ bit) for i in range(count)])  12.1 us
    all_to_all x3, starting transfers between devices, exchange(): lax.all_to_all(value, 'seq', 0, 0, axis_index_groups=same_core, tiled=True)  10.8 us
    all_to_all x1, starting transfers between devices, shards(): terms = lax.all_to_all(terms, 'dp', 0, 0, tiled=True)  10.6 us
    ppermute x6, starting transfers between devices, round_ring(): lax.ppermute(value, 'seq', [(i, (i - by) % count) for i in range(count)])  9.1 us
    unnamed x30, local copies, waits for them, and re-layouts  4.23 us
  transfers between devices with their start and end apart: 15, of which 4 were waited for; matrix products, arithmetic and copies ran while one was open for 0% of the time, Pallas kernels for 35%

profile of v7, /device:TPU:1, one launch (start us, length us, event | category | flops | bytes accessed | tf_op | source)
XLA Modules:
  0.0 133.1 jit_solution(17948244710800259561)
XLA Ops:
  0.6 0.0 copy-start.6
  0.6 2.6 %pack.1 = bf16[8,240,256]{2,1,0:T(8,128)(2,1)} custom-call(bf16[192,512]{1,0:T(8,128)(2,1)} %bitcast.18, bf16[192,512]{1,0:T(8,128)(2,1)} %bitcast.19, bf16[192,1536]{1,0:T(8,128)(2,1)} %bitcast.16), custom_call_target="tpu_custom_call" | custom-call | bytes 2097152 | tf_op jit(solution)/shard_map/pack/pallas_call | solution.py:34
  3.2 19.4 %all_to_all.25.own_ref.refs_2_ = bf16[8,240,256]{2,1,0:T(8,128)(2,1)S(1)} all-to-all(bf16[8,240,256]{2,1,0:T(8,128)(2,1)} %pack.1), channel_id=1, replica_groups={{0,2,4,6,8,10,12,14},{1,3,5,7,9,11,13,15},{16,18,20,22,24,26,28,30},{17..., dimensions={0} | all-to-all | bytes 1966080 | tf_op jit(solution)/shard_map/all_to_all | solution.py:375
  22.7 2.1 %collective-permute-start = (bf16[8,240,256]{2,1,0:T(8,128)(2,1)S(1)}, bf16[8,240,256]{2,1,0:T(8,128)(2,1)S(1)}, u32[]{:S(2)}, u32[]{:S(2)}) collective-permute-start(bf16[8,240,256]{2,1,0:T(8,128)(2,1)S(1)} %all_to_all.25.own_ref.refs_2_), channel_id=1, source_target_pairs={{0,1},{1,0},{2,3},{3,2},{4,5},{5,4},{6,7},{7,6},{8,9},{9,8},{10,11... | collective-permute-start | bytes 2949128 | tf_op jit(solution)/shard_map/ppermute | solution.py:378
  24.8 0.2 collective-permute-start.2
  25.0 2.5 %collective-permute-start.1 = (bf16[192,768]{1,0:T(8,128)(2,1)S(1)}, bf16[192,768]{1,0:T(8,128)(2,1)S(1)}, u32[]{:S(2)}, u32[]{:S(2)}) collective-permute-start(bf16[192,768]{1,0:T(8,128)(2,1)S(1)} %bitcast.15), channel_id=1, source_target_pairs={{0,12},{1,13},{2,14},{3,15},{4,0},{5,1},{6,2},{7,3},{8,4},{9,5},{1... | collective-permute-start | bytes 884744 | tf_op jit(solution)/shard_map/ppermute | solution.py:381
  27.5 0.0 collective-permute-done.oth_ref.refs_6_
  27.5 7.6 %forward.1 = (bf16[1536,256]{1,0:T(8,128)(2,1)S(1)}, bf16[1536,256]{1,0:T(8,128)(2,1)S(1)}, f32[3,8,512]{2,1,0:T(8,128)S(1)}, bf16[8,144,256]{2,1,0:T(8,128)(2,1)}) custom-call(bf16[8,240,256]{2,1,0:T(8,128)(2,1)S(1)} %all_to_all.25.own_ref.refs_2_, bf16[8,240,256]{2,1,0:T(8,128)(2,1)S(1)} %collective-permute-done.oth_ref.refs_6_), custom_call_target="tpu_custom_call" | custom-call | flops 4831838208 | bytes 6291456 | tf_op jit(solution)/shard_map/forward/pallas_call | solution.py:34
  35.0 0.9 copy-done.4
  35.9 0.0 collective-permute-done.2.behind_ref.refs_7_
  36.0 0.0 collective-permute-done.1.ahead_ref.refs_5_
  36.0 3.6 %all-to-all-start.1 = ((bf16[8,144,256]{2,1,0:T(8,128)(2,1)}), bf16[8,144,256]{2,1,0:T(8,128)(2,1)S(1)}, u32[]{:S(2)}, u32[]{:S(2)}) async-start(bf16[8,144,256]{2,1,0:T(8,128)(2,1)} %get-tuple-element.47), calls=%async_computation.1 | async-start | bytes 1179648 | tf_op jit(solution)/shard_map/all_to_all | solution.py:375
  39.5 2.6 %collective-permute-start.3 = (bf16[192,768]{1,0:T(8,128)(2,1)S(1)}, bf16[192,768]{1,0:T(8,128)(2,1)S(1)}, u32[]{:S(2)}, u32[]{:S(2)}) collective-permute-start(bf16[192,768]{1,0:T(8,128)(2,1)S(1)} %collective-permute-done.1.ahead_ref.refs_5_), channel_id=1, source_target_pairs={{0,12},{1,13},{2,14},{3,15},{4,0},{5,1},{6,2},{7,3},{8,4},{9,5},{1... | collective-permute-start | bytes 884744 | tf_op jit(solution)/shard_map/ppermute | solution.py:381
  42.1 4.4 %branch.1.refs_4_ = f32[192,768]{1,0:T(8,128)} custom-call(bf16[192,768]{1,0:T(8,128)(2,1)} %bitcast.11, bf16[192,768]{1,0:T(8,128)(2,1)} %copy-done.9, bf16[192,768]{1,0:T(8,128)(2,1)} %copy-done.8, bf16[3,768,768]{2,1,0:T(8,128)(2,1)} %conv_ref.1), custom_call_target="tpu_custom_call" | custom-call | flops 679477248 | bytes 5242880 | tf_op jit(solution)/shard_map/branch/pallas_call | solution.py:34
  46.6 2.6 %all-to-all-done.1.refs_0_ = bf16[8,144,256]{2,1,0:T(8,128)(2,1)S(1)} async-done(((bf16[8,144,256]{2,1,0:T(8,128)(2,1)}), bf16[8,144,256]{2,1,0:T(8,128)(2,1)S(1)}, u32[]{:S(2)}, u32[]{:S(2)}) %all-to-all-start.1) | async-done | bytes 589856 | tf_op jit(solution)/shard_map/all_to_all | solution.py:375
  49.2 0.8 copy-done.7
  50.0 4.9 %middle.1 = (bf16[192,768]{1,0:T(8,128)(2,1)}, bf16[8,144,256]{2,1,0:T(8,128)(2,1)}, bf16[192,192]{1,0:T(8,128)(2,1)}, bf16[192,192]{1,0:T(8,128)(2,1)}, bf16[19...) custom-call(bf16[8,144,256]{2,1,0:T(8,128)(2,1)} %copy-done.7, bf16[1536,768]{1,0:T(8,128)(2,1)} %refs_1_.1, ...), custom_call_target="tpu_custom_call" | custom-call | flops 905969664 | bytes 5242880 | tf_op jit(solution)/shard_map/middle/pallas_call | solution.py:34
  54.9 3.5 %all-to-all-start.2 = ((bf16[8,144,256]{2,1,0:T(8,128)(2,1)}), bf16[8,144,256]{2,1,0:T(8,128)(2,1)S(1)}, u32[]{:S(2)}, u32[]{:S(2)}) async-start(bf16[8,144,256]{2,1,0:T(8,128)(2,1)} %get-tuple-element.52), calls=%async_computation.2 | async-start | bytes 1179648 | tf_op jit(solution)/shard_map/all_to_all | solution.py:375
  58.5 0.0 collective-permute-done.3.refs_6_
  58.5 0.0 copy-start.11
  58.5 2.7 %collective-permute-start.4 = (bf16[192,192]{1,0:T(8,128)(2,1)}, bf16[192,192]{1,0:T(8,128)(2,1)S(1)}, u32[]{:S(2)}, u32[]{:S(2)}) collective-permute-start(bf16[192,192]{1,0:T(8,128)(2,1)} %get-tuple-element.58), channel_id=1, source_target_pairs={{0,12},{1,13},{2,14},{3,15},{4,0},{5,1},{6,2},{7,3},{8,4},{9,5},{1... | collective-permute-start | bytes 221192 | tf_op jit(solution)/shard_map/ppermute | solution.py:381
  61.2 0.5 collective-permute-start.5
  61.7 0.6 collective-permute-start.6
  62.3 7.1 %probs.1 = (bf16[3072,1536]{1,0:T(8,128)(2,1)}, bf16[128,3072]{1,0:T(8,128)(2,1)}) custom-call(bf16[8,240,256]{2,1,0:T(8,128)(2,1)} %copy-done, bf16[8,240,256]{2,1,0:T(8,128)(2,1)} %copy-done.2, bf16[1536,256]{1,0:T(8,128)(2,1)} %copy-done.3, f32[3,8,512]{2,1,0:T(8,128)} %copy-done.5), custom_call_target="tpu_custom_call" | custom-call | flops 2415919104 | bytes 12582912 | tf_op jit(solution)/shard_map/probs/pallas_call | solution.py:34
  69.5 0.0 collective-permute-done.4.refs_1_
  69.5 0.0 collective-permute-done.6.refs_3_
  69.5 0.6 copy-done.12
  70.1 0.0 copy-done.13
  70.1 0.6 copy-done.14
  70.8 3.6 %weight.1 = bf16[768,576]{1,0:T(8,128)(2,1)} custom-call(bf16[192,192]{1,0:T(8,128)(2,1)} %get-tuple-element.57.refs_0_, bf16[192,192]{1,0:T(8,128)(2,1)} %copy-done.12, bf16[192,192]{1,0:T(8,128)(2,1)} %copy-done.13, bf16[192,192]{1,0:T(8,128)(2,1)} %copy-done.14, bf16[192,768]{1,0:T(8,128)(2,1)} %bitcast.13, bf16[192,768]{1,0:T(8,128)(2,1)} %copy-done.9, ...), custom_call_target="tpu_custom_call" | custom-call | flops 679477248 | bytes 5242880 | tf_op jit(solution)/shard_map/weight/pallas_call | solution.py:34
  74.4 0.0 all-to-all-done.2.refs_0_
  74.4 10.6 %all-to-all-start.3 = ((bf16[16,48,576]{2,1,0:T(8,128)(2,1)}), bf16[16,48,576]{2,1,0:T(8,128)(2,1)S(1)}, u32[]{:S(2)}, u32[]{:S(2)}) async-start(bf16[16,48,576]{2,1,0:T(8,128)(2,1)} %bitcast.10), calls=%async_computation.3 | async-start | bytes 1966080 | tf_op jit(solution)/shard_map/all_to_all | solution.py:474
  85.1 17.1 %backward.1 = (bf16[8,240,256]{2,1,0:T(8,128)(2,1)}, bf16[8,192,256]{2,1,0:T(8,128)(2,1)}) custom-call(bf16[8,144,256]{2,1,0:T(8,128)(2,1)} %copy-done.10, bf16[1536,256]{1,0:T(8,128)(2,1)} %copy-done.4, bf16[8,240,256]{2,1,0:T(8,128)(2,1)} %copy-done, bf16[3072,1536]{1,0:T(8,128)(2,1)} %get-tuple-element.68.refs_3_, ...), custom_call_target="tpu_custom_call" | custom-call | flops 9663676416 | bytes 16777216 | tf_op jit(solution)/shard_map/backward/pallas_call | solution.py:34
  102.2 4.1 %collective-permute-start.7 = (bf16[8,192,256]{2,1,0:T(8,128)(2,1)}, bf16[8,192,256]{2,1,0:T(8,128)(2,1)S(1)}, u32[]{:S(2)}, u32[]{:S(2)}) collective-permute-start(bf16[8,192,256]{2,1,0:T(8,128)(2,1)} %get-tuple-element.71), channel_id=1, source_target_pairs={{0,1},{1,0},{2,3},{3,2},{4,5},{5,4},{6,7},{7,6},{8,9},{9,8},{10,11... | collective-permute-start | bytes 2359304 | tf_op jit(solution)/shard_map/ppermute | solution.py:378
  106.3 2.1 %collective-permute-done.7.recv_ref = bf16[8,192,256]{2,1,0:T(8,128)(2,1)S(1)} collective-permute-done((bf16[8,192,256]{2,1,0:T(8,128)(2,1)}, bf16[8,192,256]{2,1,0:T(8,128)(2,1)S(1)}, u32[]{:S(2)}, u32[]{:S(2)}) %collective-permute-start.7) | collective-permute-done | bytes 786464 | tf_op jit(solution)/shard_map/ppermute | solution.py:378
  108.4 1.2 copy-done.1
  109.6 1.1 add.1
  110.8 3.7 %all-to-all-start.4 = ((bf16[8,240,256]{2,1,0:T(8,128)(2,1)}), bf16[8,240,256]{2,1,0:T(8,128)(2,1)S(1)}, u32[]{:S(2)}, u32[]{:S(2)}) async-start(bf16[8,240,256]{2,1,0:T(8,128)(2,1)} %add.1), calls=%async_computation.4 | async-start | bytes 1966080 | tf_op jit(solution)/shard_map/all_to_all | solution.py:375
  114.4 0.2 dp_sum.1
  114.6 4.0 %collective-permute-start.8 = (f32[48,144]{1,0:T(8,128)S(1)}, f32[48,144]{1,0:T(8,128)S(1)}, u32[]{:S(2)}, u32[]{:S(2)}) collective-permute-start(f32[48,144]{1,0:T(8,128)S(1)} %get-tuple-element.80), channel_id=1, source_target_pairs={{0,1},{1,0},{2,3},{3,2},{4,5},{5,4},{6,7},{7,6},{8,9},{9,8},{10,11... | collective-permute-start | bytes 82952 | tf_op jit(solution)/shard_map/ppermute | solution.py:378
  118.6 1.8 %collective-permute-start.9 = (f32[48,144]{1,0:T(8,128)S(1)}, f32[48,144]{1,0:T(8,128)S(1)}, u32[]{:S(2)}, u32[]{:S(2)}) collective-permute-start(f32[48,144]{1,0:T(8,128)S(1)} %get-tuple-element.81), channel_id=1, source_target_pairs={{0,2},{1,3},{2,0},{3,1},{4,6},{5,7},{6,4},{7,5},{8,10},{9,11},{10,... | collective-permute-start | bytes 82952 | tf_op jit(solution)/shard_map/ppermute | solution.py:378
  120.4 0.1 collective-permute-start.10
  120.4 0.0 collective-permute-done.8.refs_1_
  120.4 5.3 %collective-permute-done.9.refs_2_ = f32[48,144]{1,0:T(8,128)S(1)} collective-permute-done((f32[48,144]{1,0:T(8,128)S(1)}, f32[48,144]{1,0:T(8,128)S(1)}, u32[]{:S(2)}, u32[]{:S(2)}) %collective-permute-start.9) | collective-permute-done | bytes 27680 | tf_op jit(solution)/shard_map/ppermute | solution.py:378
  125.8 5.1 %collective-permute-done.10.refs_3_ = f32[48,144]{1,0:T(8,128)S(1)} collective-permute-done((f32[48,144]{1,0:T(8,128)S(1)}, f32[48,144]{1,0:T(8,128)S(1)}, u32[]{:S(2)}, u32[]{:S(2)}) %collective-permute-start.10) | collective-permute-done | bytes 27680 | tf_op jit(solution)/shard_map/ppermute | solution.py:378
  130.9 0.7 last_sum.1
  131.6 0.0 all-to-all-done.4.recv_ref
  131.6 1.5 %finish.1 = (bf16[192,512]{1,0:T(8,128)(2,1)}, bf16[192,512]{1,0:T(8,128)(2,1)}, bf16[192,1536]{1,0:T(8,128)(2,1)}) custom-call(bf16[8,240,256]{2,1,0:T(8,128)(2,1)S(1)} %all-to-all-done.4.recv_ref), custom_call_target="tpu_custom_call" | custom-call | bytes 2097152 | tf_op jit(solution)/shard_map/finish/pallas_call | solution.py:34
  (24 shorter events, 0.0 us)
Async XLA Ops:
  0.6 24.1 %copy-start.6 = (bf16[1,192,768]{2,1,0:T(8,128)(2,1)S(1)}, bf16[1,192,768]{2,1,0:T(8,128)(2,1)}, u32[]{:S(2)}) copy-start(bf16[1,192,768]{2,1,0:T(8,128)(2,1)} %param.12) | copy-start | bytes 884740
  22.7 12.4 %copy-start = (bf16[8,240,256]{2,1,0:T(8,128)(2,1)}, bf16[8,240,256]{2,1,0:T(8,128)(2,1)S(1)}, u32[]{:S(2)}) copy-start(bf16[8,240,256]{2,1,0:T(8,128)(2,1)S(1)} %all_to_all.25.own_ref.refs_2_) | copy-start | bytes 2949124
  22.7 4.8 %collective-permute-start = (bf16[8,240,256]{2,1,0:T(8,128)(2,1)S(1)}, bf16[8,240,256]{2,1,0:T(8,128)(2,1)S(1)}, u32[]{:S(2)}, u32[]{:S(2)}) collective-permute-start(bf16[8,240,256]{2,1,0:T(8,128)(2,1)S(1)} %all_to_all.25.own_ref.refs_2_), channel_id=1, source_target_pairs={{0,1},{1,0},{2,3},{3,2},{4,5},{5,4},{6,7},{7,6},{8,9},{9,8},{10,11... | collective-permute-start | bytes 2949128 | tf_op jit(solution)/shard_map/ppermute | solution.py:378
  24.8 11.2 %collective-permute-start.2 = (bf16[192,768]{1,0:T(8,128)(2,1)S(1)}, bf16[192,768]{1,0:T(8,128)(2,1)S(1)}, u32[]{:S(2)}, u32[]{:S(2)}) collective-permute-start(bf16[192,768]{1,0:T(8,128)(2,1)S(1)} %bitcast.14), channel_id=1, source_target_pairs={{0,4},{1,5},{2,6},{3,7},{4,8},{5,9},{6,10},{7,11},{8,12},{9,13},{1... | collective-permute-start | bytes 884744 | tf_op jit(solution)/shard_map/ppermute | solution.py:381
  25.0 11.0 %collective-permute-start.1 = (bf16[192,768]{1,0:T(8,128)(2,1)S(1)}, bf16[192,768]{1,0:T(8,128)(2,1)S(1)}, u32[]{:S(2)}, u32[]{:S(2)}) collective-permute-start(bf16[192,768]{1,0:T(8,128)(2,1)S(1)} %bitcast.15), channel_id=1, source_target_pairs={{0,12},{1,13},{2,14},{3,15},{4,0},{5,1},{6,2},{7,3},{8,4},{9,5},{1... | collective-permute-start | bytes 884744 | tf_op jit(solution)/shard_map/ppermute | solution.py:381
  27.5 7.6 %copy-start.2 = (bf16[8,240,256]{2,1,0:T(8,128)(2,1)}, bf16[8,240,256]{2,1,0:T(8,128)(2,1)S(1)}, u32[]{:S(2)}) copy-start(bf16[8,240,256]{2,1,0:T(8,128)(2,1)S(1)} %collective-permute-done.oth_ref.refs_6_) | copy-start | bytes 2949124
  35.0 0.9 copy-start.4
  35.9 19.0 %copy-start.3 = (bf16[1536,256]{1,0:T(8,128)(2,1)}, bf16[1536,256]{1,0:T(8,128)(2,1)S(1)}, u32[]{:S(2)}) copy-start(bf16[1536,256]{1,0:T(8,128)(2,1)S(1)} %get-tuple-element.62.q_ref.refs_5_) | copy-start | bytes 2359300
  35.9 19.0 %copy-start.5 = (f32[3,8,512]{2,1,0:T(8,128)}, f32[3,8,512]{2,1,0:T(8,128)S(1)}, u32[]{:S(2)}) copy-start(f32[3,8,512]{2,1,0:T(8,128)S(1)} %get-tuple-element.63.lse_ref) | copy-start | bytes 147460
  35.9 6.2 %copy-start.8 = (bf16[192,768]{1,0:T(8,128)(2,1)}, bf16[192,768]{1,0:T(8,128)(2,1)S(1)}, u32[]{:S(2)}) copy-start(bf16[192,768]{1,0:T(8,128)(2,1)S(1)} %collective-permute-done.2.behind_ref.refs_7_) | copy-start | bytes 884740
  36.0 6.2 %copy-start.9 = (bf16[192,768]{1,0:T(8,128)(2,1)}, bf16[192,768]{1,0:T(8,128)(2,1)S(1)}, u32[]{:S(2)}) copy-start(bf16[192,768]{1,0:T(8,128)(2,1)S(1)} %collective-permute-done.1.ahead_ref.refs_5_) | copy-start | bytes 884740
  36.0 13.2 %all-to-all-start.1 = ((bf16[8,144,256]{2,1,0:T(8,128)(2,1)}), bf16[8,144,256]{2,1,0:T(8,128)(2,1)S(1)}, u32[]{:S(2)}, u32[]{:S(2)}) async-start(bf16[8,144,256]{2,1,0:T(8,128)(2,1)} %get-tuple-element.47), calls=%async_computation.1 | async-start | bytes 1179648 | tf_op jit(solution)/shard_map/all_to_all | solution.py:375
  39.5 19.0 %collective-permute-start.3 = (bf16[192,768]{1,0:T(8,128)(2,1)S(1)}, bf16[192,768]{1,0:T(8,128)(2,1)S(1)}, u32[]{:S(2)}, u32[]{:S(2)}) collective-permute-start(bf16[192,768]{1,0:T(8,128)(2,1)S(1)} %collective-permute-done.1.ahead_ref.refs_5_), channel_id=1, source_target_pairs={{0,12},{1,13},{2,14},{3,15},{4,0},{5,1},{6,2},{7,3},{8,4},{9,5},{1... | collective-permute-start | bytes 884744 | tf_op jit(solution)/shard_map/ppermute | solution.py:381
  49.2 0.8 copy-start.7
  54.9 19.5 %all-to-all-start.2 = ((bf16[8,144,256]{2,1,0:T(8,128)(2,1)}), bf16[8,144,256]{2,1,0:T(8,128)(2,1)S(1)}, u32[]{:S(2)}, u32[]{:S(2)}) async-start(bf16[8,144,256]{2,1,0:T(8,128)(2,1)} %get-tuple-element.52), calls=%async_computation.2 | async-start | bytes 1179648 | tf_op jit(solution)/shard_map/all_to_all | solution.py:375
  58.5 10.9 %copy-start.11 = (bf16[192,768]{1,0:T(8,128)(2,1)}, bf16[192,768]{1,0:T(8,128)(2,1)S(1)}, u32[]{:S(2)}) copy-start(bf16[192,768]{1,0:T(8,128)(2,1)S(1)} %collective-permute-done.3.refs_6_) | copy-start | bytes 884740
  58.5 10.9 %collective-permute-start.4 = (bf16[192,192]{1,0:T(8,128)(2,1)}, bf16[192,192]{1,0:T(8,128)(2,1)S(1)}, u32[]{:S(2)}, u32[]{:S(2)}) collective-permute-start(bf16[192,192]{1,0:T(8,128)(2,1)} %get-tuple-element.58), channel_id=1, source_target_pairs={{0,12},{1,13},{2,14},{3,15},{4,0},{5,1},{6,2},{7,3},{8,4},{9,5},{1... | collective-permute-start | bytes 221192 | tf_op jit(solution)/shard_map/ppermute | solution.py:381
  61.2 8.3 %collective-permute-start.5 = (bf16[192,192]{1,0:T(8,128)(2,1)}, bf16[192,192]{1,0:T(8,128)(2,1)S(1)}, u32[]{:S(2)}, u32[]{:S(2)}) collective-permute-start(bf16[192,192]{1,0:T(8,128)(2,1)} %get-tuple-element.59), channel_id=1, source_target_pairs={{0,8},{1,9},{2,10},{3,11},{4,12},{5,13},{6,14},{7,15},{8,0},{9,1},... | collective-permute-start | bytes 221192 | tf_op jit(solution)/shard_map/ppermute | solution.py:381
  61.7 7.8 %collective-permute-start.6 = (bf16[192,192]{1,0:T(8,128)(2,1)}, bf16[192,192]{1,0:T(8,128)(2,1)S(1)}, u32[]{:S(2)}, u32[]{:S(2)}) collective-permute-start(bf16[192,192]{1,0:T(8,128)(2,1)} %get-tuple-element.60), channel_id=1, source_target_pairs={{0,4},{1,5},{2,6},{3,7},{4,8},{5,9},{6,10},{7,11},{8,12},{9,13},{1... | collective-permute-start | bytes 221192 | tf_op jit(solution)/shard_map/ppermute | solution.py:381
  69.5 0.6 copy-start.12
  69.5 0.7 copy-start.13
  70.1 0.6 copy-start.14
  74.4 10.6 %copy-start.10 = (bf16[8,144,256]{2,1,0:T(8,128)(2,1)}, bf16[8,144,256]{2,1,0:T(8,128)(2,1)S(1)}, u32[]{:S(2)}) copy-start(bf16[8,144,256]{2,1,0:T(8,128)(2,1)S(1)} %all-to-all-done.2.refs_0_) | copy-start | bytes 1769476
  74.4 36.3 %all-to-all-start.3 = ((bf16[16,48,576]{2,1,0:T(8,128)(2,1)}), bf16[16,48,576]{2,1,0:T(8,128)(2,1)S(1)}, u32[]{:S(2)}, u32[]{:S(2)}) async-start(bf16[16,48,576]{2,1,0:T(8,128)(2,1)} %bitcast.10), calls=%async_computation.3 | async-start | bytes 1966080 | tf_op jit(solution)/shard_map/all_to_all | solution.py:474
  102.2 6.3 %collective-permute-start.7 = (bf16[8,192,256]{2,1,0:T(8,128)(2,1)}, bf16[8,192,256]{2,1,0:T(8,128)(2,1)S(1)}, u32[]{:S(2)}, u32[]{:S(2)}) collective-permute-start(bf16[8,192,256]{2,1,0:T(8,128)(2,1)} %get-tuple-element.71), channel_id=1, source_target_pairs={{0,1},{1,0},{2,3},{3,2},{4,5},{5,4},{6,7},{7,6},{8,9},{9,8},{10,11... | collective-permute-start | bytes 2359304 | tf_op jit(solution)/shard_map/ppermute | solution.py:378
  108.4 1.2 copy-start.1
  110.8 20.9 %all-to-all-start.4 = ((bf16[8,240,256]{2,1,0:T(8,128)(2,1)}), bf16[8,240,256]{2,1,0:T(8,128)(2,1)S(1)}, u32[]{:S(2)}, u32[]{:S(2)}) async-start(bf16[8,240,256]{2,1,0:T(8,128)(2,1)} %add.1), calls=%async_computation.4 | async-start | bytes 1966080 | tf_op jit(solution)/shard_map/all_to_all | solution.py:375
  114.6 5.8 %collective-permute-start.8 = (f32[48,144]{1,0:T(8,128)S(1)}, f32[48,144]{1,0:T(8,128)S(1)}, u32[]{:S(2)}, u32[]{:S(2)}) collective-permute-start(f32[48,144]{1,0:T(8,128)S(1)} %get-tuple-element.80), channel_id=1, source_target_pairs={{0,1},{1,0},{2,3},{3,2},{4,5},{5,4},{6,7},{7,6},{8,9},{9,8},{10,11... | collective-permute-start | bytes 82952 | tf_op jit(solution)/shard_map/ppermute | solution.py:378
  118.6 7.2 %collective-permute-start.9 = (f32[48,144]{1,0:T(8,128)S(1)}, f32[48,144]{1,0:T(8,128)S(1)}, u32[]{:S(2)}, u32[]{:S(2)}) collective-permute-start(f32[48,144]{1,0:T(8,128)S(1)} %get-tuple-element.81), channel_id=1, source_target_pairs={{0,2},{1,3},{2,0},{3,1},{4,6},{5,7},{6,4},{7,5},{8,10},{9,11},{10,... | collective-permute-start | bytes 82952 | tf_op jit(solution)/shard_map/ppermute | solution.py:378
  120.4 10.5 %collective-permute-start.10 = (f32[48,144]{1,0:T(8,128)S(1)}, f32[48,144]{1,0:T(8,128)S(1)}, u32[]{:S(2)}, u32[]{:S(2)}) collective-permute-start(f32[48,144]{1,0:T(8,128)S(1)} %get-tuple-element.82), channel_id=1, source_target_pairs={{0,3},{1,2},{2,1},{3,0},{4,7},{5,6},{6,5},{7,4},{8,11},{9,10},{10,... | collective-permute-start | bytes 82952 | tf_op jit(solution)/shard_map/ppermute | solution.py:378
